TPU v7x, 32 devices: a whole 2x2x4 slice. The times are simulated.
32 devices in a mesh: blk: 16 (over z, y, core), uly: 2 (over x).
Axes of the slice: x: 2, y: 2, z: 4, core: 2. Of those that a mesh axis runs over, the one named last changes fastest.
Arguments:
- query_rows: bfloat16 [4096, 8192], P(('blk', 'uly')), may hold values from -6 to 6
- key_rows: bfloat16 [4096, 1024], P(('blk', 'uly')), may hold values from -6 to 6
- value_rows: bfloat16 [4096, 1024], P(('blk', 'uly')), may hold values from -6 to 6
- out_grad: bfloat16 [4096, 8192], P(('blk', 'uly')), may hold values from -6 to 6
- segment_ids: int32 [4096], P(('blk', 'uly')), may hold values from 0 to 15, never falling along the last dimension, each value on 1 to 1024 neighbouring positions
Outputs:
- attn_out: bfloat16 [4096, 8192], P(('blk', 'uly'))
- query_grad: bfloat16 [4096, 8192], P(('blk', 'uly'))
- key_grad: bfloat16 [4096, 1024], P(('blk', 'uly'))
- value_grad: bfloat16 [4096, 1024], P(('blk', 'uly'))
Inputs may be any that keep to these rules, and one draw needn't show every extreme that they name: `segment_ids`: segment numbers never fall along the sequence and start at 0; each segment holds 1 to 1024 positions, and one holds exactly that many.
All inputs are finite; a program needn't handle non-finite values.
Results may differ from a plain program's by a relative error of at most 0.0096.
Values may be sent and summed in bfloat16 or wider, within the bound.
No kernel may reach another device: no remote copies, remote signals or barrier semaphores. Data moves between devices by JAX's collectives and lax.ppermute only.
A program may use at most 128 MiB of HBM per device.

v0:
```python
import functools
import math

import jax
import jax.numpy as jnp
import numpy as np
from jax import lax
from jax.experimental import pallas as pl
from jax.experimental.pallas import tpu as pltpu
from jax.sharding import Mesh
from jax.sharding import PartitionSpec as P

HEAD_DIM = 128
BLOCK = 256
LIMIT = 1024
NEG = -1e30
FAR = 1 << 30
ALL = ("z", "y", "c", "x")
CORES = 2
F32 = jnp.float32
BF16 = jnp.bfloat16


def dot(a, b, dims):
    return lax.dot_general(a, b, (dims, ((), ())), preferred_element_type=F32)


def attention_kernel(n_sub, chunk, group, parts, *refs):
    need, kinfo, rinfo = refs[:3]
    q_refs, g_refs = refs[3:5], refs[5:7]
    at = 7
    kv_refs = []
    for _ in parts:
        kv_refs.append(refs[at : at + n_sub])
        at += n_sub
    o_refs, dq_refs = refs[at : at + 2], refs[at + 2 : at + 4]
    at += 4
    dkv_refs = []
    for _ in parts:
        dkv_refs.append(refs[at : at + n_sub])
        at += n_sub
    kv, dkv, bias, s_buf, dp_buf, m_buf, l_buf, d_buf, acc, q_all, g_all = refs[at:]
    n_blocks = sum(parts)
    rows = group * chunk
    scale = 1.0 / math.sqrt(HEAD_DIM)
    log_scale = scale * math.log2(math.e)
    d = HEAD_DIM

    base = 0
    for s, n in enumerate(parts):
        for b in range(n):
            for k in range(n_sub):
                kv[base + b, pl.ds(k * chunk, chunk), :] = kv_refs[s][k][b]
        base += n
    dkv[...] = jnp.zeros_like(dkv)

    @pl.when(pl.program_id(0) == 0)
    def _():
        for r in range(CORES):
            rpos = rinfo[r, 0]
            rseg = rinfo[r, 1]
            for b in range(n_blocks):
                kpos = kinfo[b, 0:1, :]
                kseg = kinfo[b, 1:2, :]
                seen = (kpos <= rpos) & ((kseg == rseg) | (kseg == 0))
                bias[r, b] = jnp.where(seen, 0.0, NEG)

    for r in range(CORES):
        for h in range(group):
            q_all[pl.ds(h * chunk, chunk), :] = q_refs[r][:, h * d : (h + 1) * d]
            g_all[pl.ds(h * chunk, chunk), :] = g_refs[r][:, h * d : (h + 1) * d]
        m_buf[...] = jnp.full_like(m_buf, NEG)

        def each(fn):
            def turn(b, carry):
                @pl.when(need[r * n_blocks + b] > 0)
                def _():
                    fn(b)

                return carry

            lax.fori_loop(0, n_blocks, turn, 0)

        def score_pass(b):
            s = dot(q_all[...], kv[b, :, :d], ((1,), (1,))) * log_scale
            s = (s.reshape(group, chunk, BLOCK) + bias[r, b][None]).reshape(rows, BLOCK)
            s_buf[b] = s
            m_buf[...] = jnp.maximum(m_buf[...], jnp.maximum(s[:, :d], s[:, d:]))

        each(score_pass)
        m_buf[...] = jnp.broadcast_to(jnp.max(m_buf[...], axis=1, keepdims=True), m_buf.shape)
        l_buf[...] = jnp.zeros_like(l_buf)
        d_buf[...] = jnp.zeros_like(d_buf)
        acc[...] = jnp.zeros_like(acc)

        def weight_pass(b):
            m = m_buf[...]
            p = jnp.exp2(s_buf[b] - jnp.concatenate([m, m], axis=1))
            dp = dot(g_all[...], kv[b, :, d:], ((1,), (1,)))
            s_buf[b] = p
            dp_buf[b] = dp
            l_buf[...] += p[:, :d] + p[:, d:]
            pd = p * dp
            d_buf[...] += pd[:, :d] + pd[:, d:]
            acc[...] += dot(p.astype(BF16), kv[b, :, d:], ((1,), (0,)))

        each(weight_pass)
        inv = 1.0 / jnp.sum(l_buf[...], axis=1, keepdims=True)
        delta = jnp.sum(d_buf[...], axis=1, keepdims=True) * inv
        l_buf[...] = jnp.broadcast_to(inv, l_buf.shape)
        d_buf[...] = jnp.broadcast_to(delta, d_buf.shape)
        out = (acc[...] * inv).astype(BF16)
        for h in range(group):
            o_refs[r][:, h * d : (h + 1) * d] = out[h * chunk : (h + 1) * chunk]
        acc[...] = jnp.zeros_like(acc)

        def slope_pass(b):
            inv = l_buf[...]
            delta = d_buf[...]
            w = s_buf[b] * jnp.concatenate([inv, inv], axis=1)
            ds = (w * (dp_buf[b] - jnp.concatenate([delta, delta], axis=1))).astype(BF16)
            acc[...] += dot(ds, kv[b, :, :d], ((1,), (0,)))
            dkv[b, :, :d] += dot(ds, q_all[...], ((0,), (0,)))
            dkv[b, :, d:] += dot(w.astype(BF16), g_all[...], ((0,), (0,)))

        each(slope_pass)
        out = (acc[...] * scale).astype(BF16)
        for h in range(group):
            dq_refs[r][:, h * d : (h + 1) * d] = out[h * chunk : (h + 1) * chunk]

    base = 0
    for s, n in enumerate(parts):
        for b in range(n):
            for k in range(n_sub):
                rows_k = pl.ds(k * chunk, chunk)
                dkv_refs[s][k][b, :, :d] = (dkv[base + b, rows_k, :d] * scale).astype(BF16)
                dkv_refs[s][k][b, :, d:] = dkv[base + b, rows_k, d:].astype(BF16)
        base += n


def attention(need, kinfo, rinfo, q_pair, g_pair, kv_sets, group):
    chunk = q_pair[0].shape[0]
    n_sub = len(kv_sets[0])
    heads = q_pair[0].shape[1] // (group * HEAD_DIM)
    parts = tuple(s[0].shape[0] for s in kv_sets)
    n_blocks = sum(parts)
    rows = group * chunk
    width = group * HEAD_DIM
    pair = 2 * HEAD_DIM
    whole = lambda shape: pl.BlockSpec(shape, lambda h: (0,) * len(shape))
    row_spec = pl.BlockSpec((chunk, width), lambda h: (0, h))
    kv_specs = [
        pl.BlockSpec((n, chunk, pair), lambda h: (0, 0, h)) for n in parts for _ in range(n_sub)
    ]
    row_out = jax.ShapeDtypeStruct(q_pair[0].shape, BF16)
    pairs = rows * n_blocks * BLOCK * CORES * heads
    outs = pl.pallas_call(
        functools.partial(attention_kernel, n_sub, chunk, group, parts),
        grid=(heads,),
        in_specs=[pl.BlockSpec(memory_space=pltpu.SMEM), whole(kinfo.shape), whole(rinfo.shape)]
        + [row_spec] * 4
        + kv_specs,
        out_specs=[row_spec] * 4 + kv_specs,
        out_shape=[row_out] * 4
        + [jax.ShapeDtypeStruct(a.shape, BF16) for s in kv_sets for a in s],
        scratch_shapes=[
            pltpu.VMEM((n_blocks, BLOCK, pair), BF16),
            pltpu.VMEM((n_blocks, BLOCK, pair), F32),
            pltpu.VMEM((CORES, n_blocks, chunk, BLOCK), F32),
            pltpu.VMEM((n_blocks, rows, BLOCK), F32),
            pltpu.VMEM((n_blocks, rows, BLOCK), F32),
            pltpu.VMEM((rows, HEAD_DIM), F32),
            pltpu.VMEM((rows, HEAD_DIM), F32),
            pltpu.VMEM((rows, HEAD_DIM), F32),
            pltpu.VMEM((rows, HEAD_DIM), F32),
            pltpu.VMEM((rows, HEAD_DIM), BF16),
            pltpu.VMEM((rows, HEAD_DIM), BF16),
        ],
        compiler_params=pltpu.CompilerParams(vmem_limit_bytes=56 << 20),
        cost_estimate=pl.CostEstimate(
            flops=4 * pairs * HEAD_DIM, bytes_accessed=16 << 20, transcendentals=pairs
        ),
        name="attention",
    )(need, kinfo, rinfo, *q_pair, *g_pair, *[a for s in kv_sets for a in s])
    o_pair, dq_pair = outs[:2], outs[2:4]
    grads = [
        outs[4 + i * n_sub : 4 + (i + 1) * n_sub] for i in range(len(parts))
    ]
    return o_pair, dq_pair, grads


def per_device(query_rows, key_rows, value_rows, out_grad, segment_ids):
    chunk = query_rows.shape[0]
    planes, n_sub = lax.axis_size("z"), lax.axis_size("x")
    halves = 2 * planes
    z, y, c, x = (lax.axis_index(a) for a in ALL)
    half = 2 * z + y
    devices = planes * 2 * CORES * n_sub
    kv_heads = key_rows.shape[1] // HEAD_DIM
    group = query_rows.shape[1] // key_rows.shape[1]
    my_heads = kv_heads // CORES
    pair = 2 * HEAD_DIM

    def swap_cores(a):
        return lax.ppermute(a, "c", [(0, 1), (1, 0)])

    def rotate(a, by):
        return lax.ppermute(a, "x", [(i, (i + by) % n_sub) for i in range(n_sub)])

    def shift(a, by):
        moves = [(i, i + by) for i in range(halves) if 0 <= i + by < halves]
        return lax.ppermute(a, ("z", "y"), moves)

    def spread(a):
        return [a] + [rotate(a, k) for k in range(1, n_sub)]

    def gather_back(arrays):
        total = arrays[0].astype(F32)
        for k in range(1, n_sub):
            total = total + rotate(arrays[k], -k).astype(F32)
        return total

    ids = lax.all_to_all(
        jnp.broadcast_to(segment_ids[None], (devices, chunk)), ALL, split_axis=0, concat_axis=0, tiled=True
    )

    kv = jnp.concatenate(
        [key_rows.reshape(chunk, kv_heads, HEAD_DIM), value_rows.reshape(chunk, kv_heads, HEAD_DIM)], axis=2
    ).reshape(chunk, CORES, my_heads * pair)
    take = lambda a, i: lax.dynamic_index_in_dim(a, i, 1, keepdims=False)
    kv_mine = jnp.stack([take(kv, c), swap_cores(take(kv, 1 - c))])
    q_cols = query_rows.reshape(chunk, CORES, -1)
    g_cols = out_grad.reshape(chunk, CORES, -1)
    q_pair = (take(q_cols, c), swap_cores(take(q_cols, 1 - c)))
    g_pair = (take(g_cols, c), swap_cores(take(g_cols, 1 - c)))

    own_set = spread(kv_mine)
    set_1 = spread(shift(kv_mine, 1))
    set_2 = spread(shift(kv_mine, 2))

    n0 = jnp.sum((ids == 0).astype(jnp.int32))
    row_chunk = [(2 * half + (c ^ r)) * n_sub + x for r in range(CORES)]
    row_pos = jnp.stack([i * chunk + jnp.arange(chunk, dtype=jnp.int32) for i in row_chunk])
    row_seg = jnp.stack([lax.dynamic_index_in_dim(ids, i, 0, keepdims=False) for i in row_chunk])
    rinfo = jnp.stack([row_pos, row_seg], axis=1)[..., None]
    starts = jnp.sum((ids[None] < row_seg[:, :1, None]).astype(jnp.int32), axis=(1, 2))
    sub = (x - jnp.arange(n_sub, dtype=jnp.int32)) % n_sub

    def branch(prompt_blocks):
        def run(_):
            wide = prompt_blocks > 1
            prompt = kv_mine if wide else lax.dynamic_index_in_dim(kv_mine, c, 0)
            step = planes // 2
            while step:
                got = lax.ppermute(prompt, "z", [(i, i + step) for i in range(0, planes, 2 * step)])
                prompt = jnp.where(z % (2 * step) == step, got, prompt)
                step //= 2
            if wide:
                other = lax.ppermute(prompt, "y", [(0, 1), (1, 0)])
                prompt = jnp.concatenate(
                    [jnp.where(y == 0, prompt, other), jnp.where(y == 0, other, prompt)]
                )
                prompt_index = jnp.stack([c, 1 - c, 2 + c, 3 - c])
            else:
                prompt = jnp.where(y == 0, prompt, lax.ppermute(prompt, "y", [(0, 1)]))
                prompt_index = jnp.zeros((1,), jnp.int32)
            prompt_set = spread(prompt)

            band = jnp.stack([2 * (half - s) + (c ^ k) for s in range(3) for k in range(CORES)])
            block = jnp.concatenate([band, prompt_index])
            usable = jnp.concatenate([band >= prompt_blocks, jnp.full(prompt_index.shape, True)])
            key_chunk = jnp.clip(block, 0)[:, None] * n_sub + sub[None]
            key_seg = jnp.take(ids, key_chunk.reshape(-1), axis=0).reshape(-1, BLOCK)
            key_pos = (
                key_chunk[..., None] * chunk + jnp.arange(chunk, dtype=jnp.int32)
            ).reshape(-1, BLOCK)
            key_pos = jnp.where(usable[:, None], key_pos, FAR)
            kinfo = jnp.stack([key_pos, key_seg], axis=1)
            first = block * BLOCK
            need = (
                usable[None]
                & (first[None] <= row_pos[:, -1:])
                & ((first[None] < n0) | (first[None] + BLOCK > starts[:, None]))
            )
            need = need.astype(jnp.int32).reshape(-1)

            o_pair, dq_pair, grads = attention(
                need, kinfo, rinfo, q_pair, g_pair, [own_set, set_1, set_2, prompt_set], group
            )

            total = gather_back(grads[0])
            total = total + shift(gather_back(grads[1]).astype(BF16), -1).astype(F32)
            total = total + shift(gather_back(grads[2]).astype(BF16), -2).astype(F32)
            back = gather_back(grads[3]).astype(BF16)
            if wide:
                keep = jnp.where(y == 0, back[:2], back[2:])
                send = jnp.where(y == 0, back[2:], back[:2])
                got = lax.ppermute(send, "y", [(0, 1), (1, 0)])
                back = keep.astype(F32) + got.astype(F32)
            else:
                back = back.astype(F32) + lax.ppermute(back, "y", [(1, 0)]).astype(F32)
            step = 1
            while step < planes:
                got = lax.ppermute(
                    back.astype(BF16), "z", [(i + step, i) for i in range(0, planes, 2 * step)]
                )
                back = back + got.astype(F32)
                step *= 2
            here = (z == 0) if wide else (z == 0) & (y == 0)
            back = jnp.where(here, back, 0.0)
            if wide:
                total = total + back
            else:
                place = (jnp.arange(CORES) == c)[:, None, None]
                total = total + jnp.where(place, back, 0.0)
            total = total.astype(BF16)
            return o_pair[0], o_pair[1], dq_pair[0], dq_pair[1], total

        return run

    o_mine, o_other, dq_mine, dq_other, grads = lax.cond(
        n0 <= BLOCK, branch(1), branch(LIMIT // BLOCK), 0
    )

    def join(mine, other):
        got = swap_cores(other)
        low = jnp.where(c == 0, mine, got)
        high = jnp.where(c == 0, got, mine)
        return jnp.concatenate([low, high], axis=1)

    kv_grad = join(grads[0], grads[1]).reshape(chunk, kv_heads, 2, HEAD_DIM)
    key_grad = kv_grad[:, :, 0].reshape(chunk, -1)
    value_grad = kv_grad[:, :, 1].reshape(chunk, -1)
    return join(o_mine, o_other), join(dq_mine, dq_other), key_grad, value_grad


def solution(mesh):
    blk, uly = mesh.shape["blk"], mesh.shape["uly"]
    parts = Mesh(np.asarray(mesh.devices).reshape(blk // 4, 2, CORES, uly), ALL)
    rows = P(ALL, None)
    return jax.shard_map(
        per_device,
        mesh=parts,
        in_specs=(rows, rows, rows, rows, P(ALL)),
        out_specs=(rows, rows, rows, rows),
        check_vma=False,
    )
```

profile of v0, /device:TPU:0, one launch (start us, length us, event | category | flops | bytes accessed | tf_op | source)
XLA Modules:
  0.0 242.8 jit_solution(1647046017472752935)
XLA Ops:
  3.8 3.3 %reshape.881 = bf16[128,2,4096]{2,1,0:T(2,128)(2,1)S(1)} reshape(bf16[128,8192]{1,0:T(8,128)(2,1)} %param.7) | data formatting | bytes 4194304 | tf_op jit(solution)/shard_map/reshape | solution.py:232
  7.1 4.5 %reshape.882 = bf16[128,2,4096]{2,1,0:T(2,128)(2,1)} reshape(bf16[128,8192]{1,0:T(8,128)(2,1)} %param.10) | data formatting | bytes 4194304 | tf_op jit(solution)/shard_map/reshape | solution.py:233
  11.6 4.5 %collective-permute-start.30 = (bf16[2,128,1024]{2,1,0:T(8,128)(2,1)S(1)}, bf16[2,128,1024]{2,1,0:T(8,128)(2,1)S(1)}, u32[]{:S(2)}, u32[]{:S(2)}) collective-permute-start(bf16[2,128,1024]{2,1,0:T(8,128)(2,1)S(1)} %pad_maximum_fusion.4), channel_id=1, source_target_pairs={{0,4},{4,8},{8,12},{12,16},{16,20},{20,24},{24,28},{1,5},{5,9},{9,... | collective-permute-start | bytes 1572872 | tf_op jit(solution)/shard_map/ppermute | solution.py:212
  16.1 4.2 %collective-permute-start.32 = (bf16[2,128,1024]{2,1,0:T(8,128)(2,1)S(1)}, bf16[2,128,1024]{2,1,0:T(8,128)(2,1)}, u32[]{:S(2)}, u32[]{:S(2)}) collective-permute-start(bf16[2,128,1024]{2,1,0:T(8,128)(2,1)S(1)} %pad_maximum_fusion.4), channel_id=1, source_target_pairs={{0,8},{4,12},{8,16},{12,20},{16,24},{20,28},{1,9},{5,13},{9,17},{1... | collective-permute-start | bytes 1572872 | tf_op jit(solution)/shard_map/ppermute | solution.py:212
  20.4 11.9 %constant_dynamic-slice_fusion.1 = (bf16[128,1,4096]{2,1,0:T(2,128)(2,1)S(1)}, bf16[128,1,4096]{2,1,0:T(2,128)(2,1)}, bf16[128,1,4096]{2,1,0:T(2,128)(2,1)}, bf16[128,1,4096]{2,1,0:T(2,128)(2,1)S(1)}) fusion(bf16[128,2,4096]{2,1,0:T(2,128)(2,1)} %reshape.882, s32[]{:T(128)S(6)} %select_n.235, s32[]{:T(128)S(6)} %select_n.234, ...), kind=kLoop, calls=%fused_computation.95 | loop fusion | bytes 8388616 | tf_op jit(solution)/shard_map/jit(dynamic_index_in_dim)/dynamic_slice | solution.py:230
  32.2 2.1 copy.123
  34.4 2.1 copy.121
  37.6 3.1 %all-to-all-start = ((s32[32,1,128]{2,1,0:T(1,128)}), s32[32,1,128]{2,1,0:T(1,128)S(1)}, u32[]{:S(2)}, u32[]{:S(2)}) async-start(s32[32,1,128]{2,1,0:T(1,128)} %broadcast_in_dim.110), calls=%async_computation | async-start | bytes 32768 | tf_op jit(solution)/shard_map/all_to_all | solution.py:223
  40.8 3.7 %copy.122 = bf16[128,1,4096]{2,0,1:T(8,128)(2,1)} copy(bf16[128,1,4096]{2,1,0:T(2,128)(2,1)} %get-tuple-element.429) | data formatting | bytes 2097152
  44.5 2.1 copy.124
  49.7 1.5 collective-permute-start.31
  52.1 12.0 %collective-permute-done.29 = bf16[2,128,1024]{2,1,0:T(8,128)(2,1)} collective-permute-done((bf16[2,128,1024]{2,1,0:T(8,128)(2,1)S(1)}, bf16[2,128,1024]{2,1,0:T(8,128)(2,1)}, u32[]{:S(2)}, u32[]{:S(2)}) %collective-permute-start.29) | collective-permute-done | bytes 524320 | tf_op jit(solution)/shard_map/ppermute | solution.py:208
  64.1 11.2 %collective-permute-done.31 = bf16[2,128,1024]{2,1,0:T(8,128)(2,1)} collective-permute-done((bf16[2,128,1024]{2,1,0:T(8,128)(2,1)S(1)}, bf16[2,128,1024]{2,1,0:T(8,128)(2,1)}, u32[]{:S(2)}, u32[]{:S(2)}) %collective-permute-start.31) | collective-permute-done | bytes 524320 | tf_op jit(solution)/shard_map/ppermute | solution.py:208
  75.3 10.0 %collective-permute-done.33 = bf16[2,128,1024]{2,1,0:T(8,128)(2,1)} collective-permute-done((bf16[2,128,1024]{2,1,0:T(8,128)(2,1)}, bf16[2,128,1024]{2,1,0:T(8,128)(2,1)}, u32[]{:S(2)}, u32[]{:S(2)}) %collective-permute-start.33) | collective-permute-done | bytes 524320 | tf_op jit(solution)/shard_map/ppermute | solution.py:208
  85.3 143.9 %conditional.2 = (bf16[128,4096]{1,0:T(8,128)(2,1)}, bf16[128,4096]{1,0:T(8,128)(2,1)}, bf16[128,4096]{1,0:T(8,128)(2,1)}, bf16[128,4096]{1,0:T(8,128)(2,1)}, bf16[2,128,1024]{2,1,0:T(8,128)(2,1)S(1)}) conditional(s32[]{:T(128)} %convert_element_type.143, (s32[]{:T(128)}, s32[]{:T(128)}, s32[2,128]{1,0:T(2,128)S(1)}, s32[]{:T(128)}, s32[2]{0:T(128)S(1)}, ...), branch_computations={%region_2.3_spmd, %region_3.4_spmd} | conditional | flops 10750801920 | bytes 96103560
  86.2 3.9 %collective-permute-start = (bf16[1,128,1024]{2,1,0:T(8,128)(2,1)S(1)}, bf16[1,128,1024]{2,1,0:T(8,128)(2,1)S(1)}, u32[]{:S(2)}, u32[]{:S(2)}) collective-permute-start(bf16[1,128,1024]{2,1,0:T(8,128)(2,1)S(1)} %constant_dynamic-slice_fusion), channel_id=1, source_target_pairs={{0,16},{1,17},{2,18},{3,19},{4,20},{5,21},{6,22},{7,23}} | collective-permute-start | bytes 786440 | tf_op jit(solution)/shard_map/cond/branch_1_fun/ppermute | solution.py:255
  91.3 3.8 %collective-permute-done = bf16[1,128,1024]{2,1,0:T(8,128)(2,1)S(1)} collective-permute-done((bf16[1,128,1024]{2,1,0:T(8,128)(2,1)S(1)}, bf16[1,128,1024]{2,1,0:T(8,128)(2,1)S(1)}, u32[]{:S(2)}, u32[]{:S(2)}) %collective-permute-start) | collective-permute-done | bytes 262176 | tf_op jit(solution)/shard_map/cond/branch_1_fun/ppermute | solution.py:255
  96.5 4.2 %collective-permute-done.1 = bf16[1,128,1024]{2,1,0:T(8,128)(2,1)S(1)} collective-permute-done((bf16[1,128,1024]{2,1,0:T(8,128)(2,1)S(1)}, bf16[1,128,1024]{2,1,0:T(8,128)(2,1)S(1)}, u32[]{:S(2)}, u32[]{:S(2)}) %collective-permute-start.1) | collective-permute-done | bytes 262176 | tf_op jit(solution)/shard_map/cond/branch_1_fun/ppermute | solution.py:255
  100.8 3.4 %collective-permute-start.2 = (bf16[1,128,1024]{2,1,0:T(8,128)(2,1)S(1)}, bf16[1,128,1024]{2,1,0:T(8,128)(2,1)S(1)}, u32[]{:S(2)}, u32[]{:S(2)}) collective-permute-start(bf16[1,128,1024]{2,1,0:T(8,128)(2,1)S(1)} %broadcast_select_fusion.9), channel_id=1, source_target_pairs={{0,4},{1,5},{2,6},{3,7},{8,12},{9,13},{10,14},{11,15},{16,20},{17,... | collective-permute-start | bytes 786440 | tf_op jit(solution)/shard_map/cond/branch_1_fun/ppermute | solution.py:265
  106.5 1.6 collective-permute-done.2
  108.1 1.5 collective-permute-start.3
  110.4 4.1 %collective-permute-done.3.refs_14_ = bf16[1,128,1024]{2,1,0:T(8,128)(2,1)S(1)} collective-permute-done((bf16[1,128,1024]{2,1,0:T(8,128)(2,1)S(1)}, bf16[1,128,1024]{2,1,0:T(8,128)(2,1)S(1)}, u32[]{:S(2)}, u32[]{:S(2)}) %collective-permute-start.3) | collective-permute-done | bytes 262176 | tf_op jit(solution)/shard_map/cond/branch_1_fun/ppermute | solution.py:208
  115.3 29.6 %attention.3 = (bf16[128,4096]{1,0:T(8,128)(2,1)}, bf16[128,4096]{1,0:T(8,128)(2,1)}, bf16[128,4096]{1,0:T(8,128)(2,1)}, bf16[128,4096]{1,0:T(8,128)(2,1)}, bf16...) custom-call(s32[14]{0:T(128)} %reshape.885.refs_0_, ...), custom_call_target="tpu_custom_call" | custom-call | flops 7516192768 | bytes 16777216 | tf_op jit(solution)/shard_map/cond/branch_1_fun/attention/pallas_call | solution.py:157
  144.9 1.5 collective-permute-start.9
  146.9 7.4 %collective-permute-done.9 = bf16[1,128,1024]{2,1,0:T(8,128)(2,1)S(1)} collective-permute-done((bf16[1,128,1024]{2,1,0:T(8,128)(2,1)}, bf16[1,128,1024]{2,1,0:T(8,128)(2,1)S(1)}, u32[]{:S(2)}, u32[]{:S(2)}) %collective-permute-start.9) | collective-permute-done | bytes 262176 | tf_op jit(solution)/shard_map/cond/branch_1_fun/ppermute | solution.py:208
  156.8 1.5 collective-permute-start.7
  158.8 28.8 %collective-permute-done.10 = bf16[1,128,1024]{2,1,0:T(8,128)(2,1)S(1)} collective-permute-done((bf16[1,128,1024]{2,1,0:T(8,128)(2,1)S(1)}, bf16[1,128,1024]{2,1,0:T(8,128)(2,1)S(1)}, u32[]{:S(2)}, u32[]{:S(2)}) %collective-permute-start.10) | collective-permute-done | bytes 262176 | tf_op jit(solution)/shard_map/cond/branch_1_fun/ppermute | solution.py:301
  191.7 19.9 %collective-permute-done.11 = bf16[1,128,1024]{2,1,0:T(8,128)(2,1)S(1)} collective-permute-done((bf16[1,128,1024]{2,1,0:T(8,128)(2,1)S(1)}, bf16[1,128,1024]{2,1,0:T(8,128)(2,1)S(1)}, u32[]{:S(2)}, u32[]{:S(2)}) %collective-permute-start.11) | collective-permute-done | bytes 262176 | tf_op jit(solution)/shard_map/cond/branch_1_fun/ppermute | solution.py:304
  215.3 6.7 %collective-permute-done.12 = bf16[1,128,1024]{2,1,0:T(8,128)(2,1)} collective-permute-done((bf16[1,128,1024]{2,1,0:T(8,128)(2,1)}, bf16[1,128,1024]{2,1,0:T(8,128)(2,1)}, u32[]{:S(2)}, u32[]{:S(2)}) %collective-permute-start.12) | collective-permute-done | bytes 262176 | tf_op jit(solution)/shard_map/cond/branch_1_fun/ppermute | solution.py:304
  223.2 4.4 %collective-permute-done.8 = bf16[2,128,1024]{2,1,0:T(8,128)(2,1)} collective-permute-done((bf16[2,128,1024]{2,1,0:T(8,128)(2,1)S(1)}, bf16[2,128,1024]{2,1,0:T(8,128)(2,1)}, u32[]{:S(2)}, u32[]{:S(2)}) %collective-permute-start.8) | collective-permute-done | bytes 524320 | tf_op jit(solution)/shard_map/cond/branch_1_fun/ppermute | solution.py:212
  230.0 2.4 collective-permute-done.36
  232.8 2.8 %slice_reduce_fusion = (bf16[128,8,128]{2,1,0:T(8,128)(2,1)S(1)}, bf16[128,8,128]{2,1,0:T(8,128)(2,1)S(1)}) fusion(bf16[128,8,2,128]{3,2,1,0:T(2,128)(2,1)S(1)} %reshape.883), kind=kLoop, calls=%fused_computation.79 | loop fusion | bytes 1048576 | tf_op jit(solution)/shard_map/slice | solution.py:333
  (110 shorter events, 37.0 us)
Async XLA Ops:
  3.1 8.5 %collective-permute-start.26 = (bf16[128,1024]{1,0:T(8,128)(2,1)S(1)}, bf16[128,1024]{1,0:T(8,128)(2,1)S(1)}, u32[]{:S(2)}, u32[]{:S(2)}) collective-permute-start(bf16[128,1024]{1,0:T(8,128)(2,1)S(1)} %bitcast.95), channel_id=1, source_target_pairs={{0,2},{2,0},{1,3},{3,1},{4,6},{6,4},{5,7},{7,5},{8,10},{10,8},{9,1... | collective-permute-start | bytes 786440 | tf_op jit(solution)/shard_map/ppermute | solution.py:205
  11.6 38.1 %collective-permute-start.30 = (bf16[2,128,1024]{2,1,0:T(8,128)(2,1)S(1)}, bf16[2,128,1024]{2,1,0:T(8,128)(2,1)S(1)}, u32[]{:S(2)}, u32[]{:S(2)}) collective-permute-start(bf16[2,128,1024]{2,1,0:T(8,128)(2,1)S(1)} %pad_maximum_fusion.4), channel_id=1, source_target_pairs={{0,4},{4,8},{8,12},{12,16},{16,20},{20,24},{24,28},{1,5},{5,9},{9,... | collective-permute-start | bytes 1572872 | tf_op jit(solution)/shard_map/ppermute | solution.py:212
  16.1 35.1 %collective-permute-start.32 = (bf16[2,128,1024]{2,1,0:T(8,128)(2,1)S(1)}, bf16[2,128,1024]{2,1,0:T(8,128)(2,1)}, u32[]{:S(2)}, u32[]{:S(2)}) collective-permute-start(bf16[2,128,1024]{2,1,0:T(8,128)(2,1)S(1)} %pad_maximum_fusion.4), channel_id=1, source_target_pairs={{0,8},{4,12},{8,16},{12,20},{16,24},{20,28},{1,9},{5,13},{9,17},{1... | collective-permute-start | bytes 1572872 | tf_op jit(solution)/shard_map/ppermute | solution.py:212
  34.4 2.6 %copy-start.12 = (s32[128]{0:T(128)S(1)}, s32[128]{0:T(128)}, u32[]{:S(2)}) copy-start(s32[128]{0:T(128)} %param.11) | copy-start | bytes 1540
  34.4 29.7 %collective-permute-start.27 = (bf16[128,4096]{1,0:T(8,128)(2,1)}, bf16[128,4096]{1,0:T(8,128)(2,1)}, u32[]{:S(2)}, u32[]{:S(2)}) collective-permute-start(bf16[128,4096]{1,0:T(8,128)(2,1)} %bitcast.75), channel_id=1, source_target_pairs={{0,2},{2,0},{1,3},{3,1},{4,6},{6,4},{5,7},{7,5},{8,10},{10,8},{9,1... | collective-permute-start | bytes 3145736 | tf_op jit(solution)/shard_map/ppermute | solution.py:205
  36.5 8.0 %copy-start = (bf16[128,1,4096]{2,1,0:T(2,128)(2,1)S(1)}, bf16[128,1,4096]{2,1,0:T(2,128)(2,1)}, u32[]{:S(2)}) copy-start(bf16[128,1,4096]{2,1,0:T(2,128)(2,1)} %get-tuple-element.444) | copy-start | bytes 3145732
  36.5 27.6 %collective-permute-start.28 = (bf16[128,4096]{1,0:T(8,128)(2,1)}, bf16[128,4096]{1,0:T(8,128)(2,1)}, u32[]{:S(2)}, u32[]{:S(2)}) collective-permute-start(bf16[128,4096]{1,0:T(8,128)(2,1)} %bitcast.73), channel_id=1, source_target_pairs={{0,2},{2,0},{1,3},{3,1},{4,6},{6,4},{5,7},{7,5},{8,10},{10,8},{9,1... | collective-permute-start | bytes 3145736 | tf_op jit(solution)/shard_map/ppermute | solution.py:205
  37.6 10.3 %all-to-all-start = ((s32[32,1,128]{2,1,0:T(1,128)}), s32[32,1,128]{2,1,0:T(1,128)S(1)}, u32[]{:S(2)}, u32[]{:S(2)}) async-start(s32[32,1,128]{2,1,0:T(1,128)} %broadcast_in_dim.110), calls=%async_computation | async-start | bytes 32768 | tf_op jit(solution)/shard_map/all_to_all | solution.py:223
  49.1 15.0 %collective-permute-start.29 = (bf16[2,128,1024]{2,1,0:T(8,128)(2,1)S(1)}, bf16[2,128,1024]{2,1,0:T(8,128)(2,1)}, u32[]{:S(2)}, u32[]{:S(2)}) collective-permute-start(bf16[2,128,1024]{2,1,0:T(8,128)(2,1)S(1)} %pad_maximum_fusion.4), channel_id=1, source_target_pairs={{0,1},{1,0},{2,3},{3,2},{4,5},{5,4},{6,7},{7,6},{8,9},{9,8},{10,11... | collective-permute-start | bytes 1572872 | tf_op jit(solution)/shard_map/ppermute | solution.py:208
  49.7 25.6 %collective-permute-start.31 = (bf16[2,128,1024]{2,1,0:T(8,128)(2,1)S(1)}, bf16[2,128,1024]{2,1,0:T(8,128)(2,1)}, u32[]{:S(2)}, u32[]{:S(2)}) collective-permute-start(bf16[2,128,1024]{2,1,0:T(8,128)(2,1)S(1)} %collective-permute-done.30), channel_id=1, source_target_pairs={{0,1},{1,0},{2,3},{3,2},{4,5},{5,4},{6,7},{7,6},{8,9},{9,8},{10,11... | collective-permute-start | bytes 1572872 | tf_op jit(solution)/shard_map/ppermute | solution.py:208
  51.2 34.2 %collective-permute-start.33 = (bf16[2,128,1024]{2,1,0:T(8,128)(2,1)}, bf16[2,128,1024]{2,1,0:T(8,128)(2,1)}, u32[]{:S(2)}, u32[]{:S(2)}) collective-permute-start(bf16[2,128,1024]{2,1,0:T(8,128)(2,1)} %collective-permute-done.32), channel_id=1, source_target_pairs={{0,1},{1,0},{2,3},{3,2},{4,5},{5,4},{6,7},{7,6},{8,9},{9,8},{10,11... | collective-permute-start | bytes 1572872 | tf_op jit(solution)/shard_map/ppermute | solution.py:208
  85.4 29.9 %copy-start.2 = (bf16[128,4096]{1,0:T(8,128)(2,1)S(1)}, bf16[128,4096]{1,0:T(8,128)(2,1)}, u32[]{:S(2)}) copy-start(bf16[128,4096]{1,0:T(8,128)(2,1)} %get-tuple-element.128.refs_5_) | copy-start | bytes 3145732 | tf_op jit(solution)/shard_map/conditional
  85.4 29.9 %copy-start.4 = (bf16[128,4096]{1,0:T(8,128)(2,1)S(1)}, bf16[128,4096]{1,0:T(8,128)(2,1)}, u32[]{:S(2)}) copy-start(bf16[128,4096]{1,0:T(8,128)(2,1)} %get-tuple-element.126.refs_3_) | copy-start | bytes 3145732 | tf_op jit(solution)/shard_map/conditional
  86.2 8.9 %collective-permute-start = (bf16[1,128,1024]{2,1,0:T(8,128)(2,1)S(1)}, bf16[1,128,1024]{2,1,0:T(8,128)(2,1)S(1)}, u32[]{:S(2)}, u32[]{:S(2)}) collective-permute-start(bf16[1,128,1024]{2,1,0:T(8,128)(2,1)S(1)} %constant_dynamic-slice_fusion), channel_id=1, source_target_pairs={{0,16},{1,17},{2,18},{3,19},{4,20},{5,21},{6,22},{7,23}} | collective-permute-start | bytes 786440 | tf_op jit(solution)/shard_map/cond/branch_1_fun/ppermute | solution.py:255
  95.1 5.7 %collective-permute-start.1 = (bf16[1,128,1024]{2,1,0:T(8,128)(2,1)S(1)}, bf16[1,128,1024]{2,1,0:T(8,128)(2,1)S(1)}, u32[]{:S(2)}, u32[]{:S(2)}) collective-permute-start(bf16[1,128,1024]{2,1,0:T(8,128)(2,1)S(1)} %broadcast_select_fusion.8), channel_id=1, source_target_pairs={{0,8},{16,24},{1,9},{17,25},{2,10},{18,26},{3,11},{19,27},{4,12},{... | collective-permute-start | bytes 786440 | tf_op jit(solution)/shard_map/cond/branch_1_fun/ppermute | solution.py:255
  100.8 7.3 %collective-permute-start.2 = (bf16[1,128,1024]{2,1,0:T(8,128)(2,1)S(1)}, bf16[1,128,1024]{2,1,0:T(8,128)(2,1)S(1)}, u32[]{:S(2)}, u32[]{:S(2)}) collective-permute-start(bf16[1,128,1024]{2,1,0:T(8,128)(2,1)S(1)} %broadcast_select_fusion.9), channel_id=1, source_target_pairs={{0,4},{1,5},{2,6},{3,7},{8,12},{9,13},{10,14},{11,15},{16,20},{17,... | collective-permute-start | bytes 786440 | tf_op jit(solution)/shard_map/cond/branch_1_fun/ppermute | solution.py:265
  108.1 6.5 %copy-start.11 = (bf16[1,128,1024]{2,1,0:T(8,128)(2,1)}, bf16[1,128,1024]{2,1,0:T(8,128)(2,1)S(1)}, u32[]{:S(2)}) copy-start(bf16[1,128,1024]{2,1,0:T(8,128)(2,1)S(1)} %broadcast_select_fusion.10.refs_13_) | copy-start | bytes 786436 | tf_op jit(solution)/shard_map/conditional
  108.1 6.4 %collective-permute-start.3 = (bf16[1,128,1024]{2,1,0:T(8,128)(2,1)S(1)}, bf16[1,128,1024]{2,1,0:T(8,128)(2,1)S(1)}, u32[]{:S(2)}, u32[]{:S(2)}) collective-permute-start(bf16[1,128,1024]{2,1,0:T(8,128)(2,1)S(1)} %broadcast_select_fusion.10.refs_13_), channel_id=1, source_target_pairs={{0,1},{1,0},{2,3},{3,2},{4,5},{5,4},{6,7},{7,6},{8,9},{9,8},{10,11... | collective-permute-start | bytes 786440 | tf_op jit(solution)/shard_map/cond/branch_1_fun/ppermute | solution.py:208
  144.9 9.5 %collective-permute-start.9 = (bf16[1,128,1024]{2,1,0:T(8,128)(2,1)}, bf16[1,128,1024]{2,1,0:T(8,128)(2,1)S(1)}, u32[]{:S(2)}, u32[]{:S(2)}) collective-permute-start(bf16[1,128,1024]{2,1,0:T(8,128)(2,1)} %get-tuple-element.149), channel_id=1, source_target_pairs={{0,1},{1,0},{2,3},{3,2},{4,5},{5,4},{6,7},{7,6},{8,9},{9,8},{10,11... | collective-permute-start | bytes 786440 | tf_op jit(solution)/shard_map/cond/branch_1_fun/ppermute | solution.py:208
  146.4 42.7 %collective-permute-start.5 = (bf16[2,128,1024]{2,1,0:T(8,128)(2,1)}, bf16[2,128,1024]{2,1,0:T(8,128)(2,1)S(1)}, u32[]{:S(2)}, u32[]{:S(2)}) collective-permute-start(bf16[2,128,1024]{2,1,0:T(8,128)(2,1)} %get-tuple-element.145), channel_id=1, source_target_pairs={{0,1},{1,0},{2,3},{3,2},{4,5},{5,4},{6,7},{7,6},{8,9},{9,8},{10,11... | collective-permute-start | bytes 1572872 | tf_op jit(solution)/shard_map/cond/branch_1_fun/ppermute | solution.py:208
  154.4 59.4 %copy-start.6 = (bf16[2,128,1024]{2,1,0:T(8,128)(2,1)S(1)}, bf16[2,128,1024]{2,1,0:T(8,128)(2,1)}, u32[]{:S(2)}) copy-start(bf16[2,128,1024]{2,1,0:T(8,128)(2,1)} %get-tuple-element.146) | copy-start | bytes 1572868 | tf_op jit(solution)/shard_map/conditional
  155.5 32.2 %collective-permute-start.10 = (bf16[1,128,1024]{2,1,0:T(8,128)(2,1)S(1)}, bf16[1,128,1024]{2,1,0:T(8,128)(2,1)S(1)}, u32[]{:S(2)}, u32[]{:S(2)}) collective-permute-start(bf16[1,128,1024]{2,1,0:T(8,128)(2,1)S(1)} %add_convert_fusion.5), channel_id=1, source_target_pairs={{4,0},{5,1},{6,2},{7,3},{12,8},{13,9},{14,10},{15,11},{20,16},{21,... | collective-permute-start | bytes 786440 | tf_op jit(solution)/shard_map/cond/branch_1_fun/ppermute | solution.py:301
  156.8 57.0 %collective-permute-start.7 = (bf16[2,128,1024]{2,1,0:T(8,128)(2,1)}, bf16[2,128,1024]{2,1,0:T(8,128)(2,1)S(1)}, u32[]{:S(2)}, u32[]{:S(2)}) collective-permute-start(bf16[2,128,1024]{2,1,0:T(8,128)(2,1)} %get-tuple-element.147), channel_id=1, source_target_pairs={{0,1},{1,0},{2,3},{3,2},{4,5},{5,4},{6,7},{7,6},{8,9},{9,8},{10,11... | collective-permute-start | bytes 1572872 | tf_op jit(solution)/shard_map/cond/branch_1_fun/ppermute | solution.py:208
  158.3 64.8 %collective-permute-start.4 = (bf16[2,128,1024]{2,1,0:T(8,128)(2,1)}, bf16[2,128,1024]{2,1,0:T(8,128)(2,1)S(1)}, u32[]{:S(2)}, u32[]{:S(2)}) collective-permute-start(bf16[2,128,1024]{2,1,0:T(8,128)(2,1)} %get-tuple-element.143), channel_id=1, source_target_pairs={{0,1},{1,0},{2,3},{3,2},{4,5},{5,4},{6,7},{7,6},{8,9},{9,8},{10,11... | collective-permute-start | bytes 1572872 | tf_op jit(solution)/shard_map/cond/branch_1_fun/ppermute | solution.py:208
  187.8 23.9 %collective-permute-start.11 = (bf16[1,128,1024]{2,1,0:T(8,128)(2,1)S(1)}, bf16[1,128,1024]{2,1,0:T(8,128)(2,1)S(1)}, u32[]{:S(2)}, u32[]{:S(2)}) collective-permute-start(bf16[1,128,1024]{2,1,0:T(8,128)(2,1)S(1)} %fusion.3), channel_id=1, source_target_pairs={{8,0},{24,16},{9,1},{25,17},{10,2},{26,18},{11,3},{27,19},{12,4},{... | collective-permute-start | bytes 786440 | tf_op jit(solution)/shard_map/cond/branch_1_fun/ppermute | solution.py:304
  190.3 37.2 %copy-start.10 = (bf16[2,128,1024]{2,1,0:T(8,128)(2,1)S(1)}, bf16[2,128,1024]{2,1,0:T(8,128)(2,1)}, u32[]{:S(2)}) copy-start(bf16[2,128,1024]{2,1,0:T(8,128)(2,1)} %get-tuple-element.142) | copy-start | bytes 1572868 | tf_op jit(solution)/shard_map/conditional
  190.3 32.8 %collective-permute-start.6 = (bf16[2,128,1024]{2,1,0:T(8,128)(2,1)S(1)}, bf16[2,128,1024]{2,1,0:T(8,128)(2,1)S(1)}, u32[]{:S(2)}, u32[]{:S(2)}) collective-permute-start(bf16[2,128,1024]{2,1,0:T(8,128)(2,1)S(1)} %add_convert_fusion.4), channel_id=1, source_target_pairs={{4,0},{8,4},{12,8},{16,12},{20,16},{24,20},{28,24},{5,1},{9,5},{13... | collective-permute-start | bytes 1572872 | tf_op jit(solution)/shard_map/cond/branch_1_fun/ppermute | solution.py:212
  212.4 9.6 %collective-permute-start.12 = (bf16[1,128,1024]{2,1,0:T(8,128)(2,1)}, bf16[1,128,1024]{2,1,0:T(8,128)(2,1)}, u32[]{:S(2)}, u32[]{:S(2)}) collective-permute-start(bf16[1,128,1024]{2,1,0:T(8,128)(2,1)} %fusion.4), channel_id=1, source_target_pairs={{16,0},{17,1},{18,2},{19,3},{20,4},{21,5},{22,6},{23,7}} | collective-permute-start | bytes 786440 | tf_op jit(solution)/shard_map/cond/branch_1_fun/ppermute | solution.py:304
  213.9 13.6 %collective-permute-start.8 = (bf16[2,128,1024]{2,1,0:T(8,128)(2,1)S(1)}, bf16[2,128,1024]{2,1,0:T(8,128)(2,1)}, u32[]{:S(2)}, u32[]{:S(2)}) collective-permute-start(bf16[2,128,1024]{2,1,0:T(8,128)(2,1)S(1)} %add_convert_fusion.3), channel_id=1, source_target_pairs={{8,0},{12,4},{16,8},{20,12},{24,16},{28,20},{9,1},{13,5},{17,9},{2... | collective-permute-start | bytes 1572872 | tf_op jit(solution)/shard_map/cond/branch_1_fun/ppermute | solution.py:212
  229.3 7.8 %collective-permute-start.35 = (bf16[128,4096]{1,0:T(8,128)(2,1)}, bf16[128,4096]{1,0:T(8,128)(2,1)S(1)}, u32[]{:S(2)}, u32[]{:S(2)}) collective-permute-start(bf16[128,4096]{1,0:T(8,128)(2,1)} %get-tuple-element.162), channel_id=1, source_target_pairs={{0,2},{2,0},{1,3},{3,1},{4,6},{6,4},{5,7},{7,5},{8,10},{10,8},{9,1... | collective-permute-start | bytes 3145736 | tf_op jit(solution)/shard_map/ppermute | solution.py:205
  229.4 3.0 %collective-permute-start.36 = (bf16[128,1024]{1,0:T(8,128)(2,1)S(1)}, bf16[128,1024]{1,0:T(8,128)(2,1)S(1)}, u32[]{:S(2)}, u32[]{:S(2)}) collective-permute-start(bf16[128,1024]{1,0:T(8,128)(2,1)S(1)} %slice_bitcast_fusion.2), channel_id=1, source_target_pairs={{0,2},{2,0},{1,3},{3,1},{4,6},{6,4},{5,7},{7,5},{8,10},{10,8},{9,1... | collective-permute-start | bytes 786440 | tf_op jit(solution)/shard_map/ppermute | solution.py:205
  229.9 10.0 %collective-permute-start.34 = (bf16[128,4096]{1,0:T(8,128)(2,1)}, bf16[128,4096]{1,0:T(8,128)(2,1)S(1)}, u32[]{:S(2)}, u32[]{:S(2)}) collective-permute-start(bf16[128,4096]{1,0:T(8,128)(2,1)} %get-tuple-element.160), channel_id=1, source_target_pairs={{0,2},{2,0},{1,3},{3,1},{4,6},{6,4},{5,7},{7,5},{8,10},{10,8},{9,1... | collective-permute-start | bytes 3145736 | tf_op jit(solution)/shard_map/ppermute | solution.py:205
  (2 other events, 1.5 us)
where the time goes:
time: 242 us; the launch traced here: 243 us
  waiting for transfers between devices  118 us (49%)
  local copies, waits for them, and re-layouts  42 us (17%)
  starting transfers between devices  37.1 us (15%)
  Pallas kernels  29.6 us (12%)
  other arithmetic  14.4 us (6%)
    ppermute x8, waiting for transfers between devices, rotate(): return lax.ppermute(a, 'x', [(i, (i + by) % n_sub) for i in range(n_sub)])  44.8 us
    pallas_call x1, Pallas kernels, attention(): pl.pallas_call(functools.partial(attention_kernel, n_sub, chunk, group, p...  29.6 us
    ppermute x1, waiting for transfers between devices, run(): back = back.astype(F32) + lax.ppermute(back, 'y', [(1, 0)]).astype(F32)  28.8 us
    ppermute x2, waiting for transfers between devices, run(): lax.ppermute(back.astype(BF16), 'z', [(i + step, i) for i in range(0, pla...  26.6 us
    unnamed x12, local copies, waits for them, and re-layouts  13.8 us
    dynamic_slice x4, local copies, waits for them, and re-layouts, per_device(): take = lambda a, i: lax.dynamic_index_in_dim(a, i, 1, keepdims=False)  12.2 us
    ppermute x4, starting transfers between devices, shift(): return lax.ppermute(a, ('z', 'y'), moves)  11.4 us
    ppermute x8, starting transfers between devices, rotate(): return lax.ppermute(a, 'x', [(i, (i + by) % n_sub) for i in range(n_sub)])  8.36 us
  transfers between devices with their start and end apart: 25, of which 14 were waited for; matrix products, arithmetic and copies ran while one was open for 20% of the time, Pallas kernels for 0%

commit v1 on v0

v1 whole, which is shorter than its diff:
```python
import functools
import math

import jax
import jax.numpy as jnp
import numpy as np
from jax import lax
from jax.experimental import pallas as pl
from jax.experimental.pallas import tpu as pltpu
from jax.sharding import Mesh
from jax.sharding import PartitionSpec as P

HEAD_DIM = 128
BLOCK = 256
WIDE = 4
NEG = -1e30
FAR = 1 << 30
ALL = ("z", "y", "c", "x")
CORES = 2
SPLIT = 2
F32 = jnp.float32
BF16 = jnp.bfloat16


def dot(a, b, dims):
    return lax.dot_general(a, b, (dims, ((), ())), preferred_element_type=F32)


def attention_kernel(n_sub, chunk, group, first_call, wide_column, parts, *refs):
    info, kinfo, rinfo = refs[:3]
    q_refs, g_refs = refs[3:5], refs[5:7]
    at = 7
    kv_refs = []
    for _ in parts:
        kv_refs.append(refs[at : at + n_sub])
        at += n_sub
    if not first_call:
        at += 4
    o_refs, dq_refs = refs[at : at + 2], refs[at + 2 : at + 4]
    at += 4
    dkv_refs = []
    for _ in parts:
        dkv_refs.append(refs[at : at + n_sub])
        at += n_sub
    order, kv, dkv, bias, s_buf, dp_buf, m_buf, l_buf, d_buf, acc, q_all, g_all, o_all, dq_all = refs[at:]
    n_blocks = parts[-1][0] + parts[-1][1]
    rows = group * chunk
    scale = 1.0 / math.sqrt(HEAD_DIM)
    log_scale = scale * math.log2(math.e)
    d = HEAD_DIM
    wide = info[1] > 0

    def load(s):
        base, n = parts[s]
        for b in range(n):
            for k in range(n_sub):
                kv[base + b, pl.ds(k * chunk, chunk), :] = kv_refs[s][k][b]

    for s in range(len(parts) - 1):
        load(s)
    plain = parts[-1][0]
    head = pl.program_id(0)
    pair = 2 * d

    def wide_part(array, k, column):
        here = kv.at[pl.ds(plain, n_blocks - plain), pl.ds(k * chunk, chunk), :]
        return here, array.at[:, :, pl.ds(pl.multiple_of(column * pair, pair), pair)]

    @pl.when(wide)
    def _():
        for k in range(n_sub):
            here, there = wide_part(kv_refs[-1][k], k, wide_column + head)
            pltpu.sync_copy(there, here)

    dkv[:plain] = jnp.zeros_like(dkv[:plain])

    @pl.when(wide)
    def _():
        dkv[plain:] = jnp.zeros_like(dkv[plain:])

    @pl.when(pl.program_id(0) == 0)
    def _():
        for r in range(CORES):
            count = 0
            for b in range(n_blocks):
                order[r, count] = b
                count = count + info[2 + r * n_blocks + b]
            order[r, n_blocks] = count
            rpos = rinfo[r, 0]
            rseg = rinfo[r, 1]
            for b in range(n_blocks):
                kpos = kinfo[b, 0]
                kseg = kinfo[b, 1]
                seen = (kpos <= rpos) & ((kseg == rseg) | (kseg == 0))
                bias[r, b] = jnp.where(seen, 0.0, NEG)

    for r in range(CORES):
        for h in range(group):
            q_all[r, pl.ds(h * chunk, chunk), :] = q_refs[r][:, h * d : (h + 1) * d]
            g_all[r, pl.ds(h * chunk, chunk), :] = g_refs[r][:, h * d : (h + 1) * d]

    def one_chunk(r, carry):
        m_buf[...] = jnp.full_like(m_buf, NEG)

        def each(fn):
            def turn(i, carry):
                fn(order[r, i])
                return carry

            lax.fori_loop(0, order[r, n_blocks], turn, 0)

        def fold(op, t):
            return op(t.reshape(BLOCK // 8, 8, -1), axis=0)

        sub = min(rows, 256)
        tiles = [slice(i, i + sub) for i in range(0, rows, sub)]

        def score_pass(b):
            for t in tiles:
                s = dot(kv[b, :, :d], q_all[r, t], ((1,), (1,))) * log_scale
                s = s + jnp.concatenate([bias[r, b]] * (sub // bias.shape[3]), axis=1)
                s_buf[b, :, t] = s
                m_buf[:, t] = jnp.maximum(m_buf[:, t], fold(jnp.max, s))

        each(score_pass)
        m_buf[...] = jnp.broadcast_to(jnp.max(m_buf[...], axis=0, keepdims=True), m_buf.shape)
        l_buf[...] = jnp.zeros_like(l_buf)
        d_buf[...] = jnp.zeros_like(d_buf)
        acc[...] = jnp.zeros_like(acc)

        def weight_pass(b):
            for t in tiles:
                p = jnp.exp2(s_buf[b, :, t] - m_buf[0:1, t])
                dp = dot(kv[b, :, d:], g_all[r, t], ((1,), (1,)))
                dp_buf[b, :, t] = dp
                l_buf[:, t] += fold(jnp.sum, p)
                d_buf[:, t] += fold(jnp.sum, p * dp)
                acc[:, t] += dot(kv[b, :, d:], p.astype(BF16), ((0,), (0,)))

        each(weight_pass)
        inv = 1.0 / jnp.sum(l_buf[...], axis=0, keepdims=True)
        delta = jnp.sum(d_buf[...], axis=0, keepdims=True) * inv
        m_buf[...] = m_buf[...] - jnp.broadcast_to(jnp.log2(inv), m_buf.shape)
        d_buf[...] = jnp.broadcast_to(delta, d_buf.shape)
        o_all[r] = (acc[...] * inv).astype(BF16).T
        acc[...] = jnp.zeros_like(acc)

        def slope_pass(b):
            ds_low = []
            for i in range(0, BLOCK, 128):
                u = slice(i, i + 128)
                w = jnp.exp2(s_buf[b, u] - m_buf[0:1])
                ds = (w * (dp_buf[b, u] - d_buf[0:1])).astype(BF16)
                ds_low.append(ds)
                dkv[b, u, :d] += dot(ds, q_all[r], ((1,), (0,)))
                dkv[b, u, d:] += dot(w.astype(BF16), g_all[r], ((1,), (0,)))
            acc[...] += dot(kv[b, :, :d], jnp.concatenate(ds_low, axis=0), ((0,), (0,)))

        each(slope_pass)
        dq_all[r] = (acc[...] * scale).astype(BF16).T
        return carry

    lax.fori_loop(0, CORES, one_chunk, 0)
    for r in range(CORES):
        for h in range(group):
            o_refs[r][:, h * d : (h + 1) * d] = o_all[r, pl.ds(h * chunk, chunk), :]
            dq_refs[r][:, h * d : (h + 1) * d] = dq_all[r, pl.ds(h * chunk, chunk), :]

    def store(s, base, n):
        for b in range(n):
            for k in range(n_sub):
                rows_k = pl.ds(k * chunk, chunk)
                dkv_refs[s][k][b, :, :d] = (dkv[base + b, rows_k, :d] * scale).astype(BF16)
                dkv_refs[s][k][b, :, d:] = dkv[base + b, rows_k, d:].astype(BF16)

    for s, (base, n) in enumerate(parts[:-1]):
        store(s, base, n)

    @pl.when(wide)
    def _():
        kv[plain:, :, :d] = (dkv[plain:, :, :d] * scale).astype(BF16)
        kv[plain:, :, d:] = dkv[plain:, :, d:].astype(BF16)
        for k in range(n_sub):
            here, there = wide_part(dkv_refs[-1][k], k, head)
            pltpu.sync_copy(here, there)


def attention(call, info, kinfo, rinfo, mine, other, kv_sets, outs, group, heads):
    chunk = mine[0].shape[0]
    n_sub = len(kv_sets[0][1])
    all_heads = other[0].shape[1] // (group * HEAD_DIM)
    rows = group * chunk
    width = group * HEAD_DIM
    parts, n_blocks = [], 0
    for _, arrays in kv_sets:
        parts.append((n_blocks, arrays[0].shape[0]))
        n_blocks += arrays[0].shape[0]
    parts = tuple(parts)
    first = call * heads
    whole = lambda shape: pl.BlockSpec(shape, lambda h, info: (0,) * len(shape))
    mine_spec = pl.BlockSpec((chunk, width), lambda h, info: (0, info[0] * all_heads + first + h))
    other_spec = pl.BlockSpec((chunk, width), lambda h, info: (0, first + h))

    def kv_spec(n, column):
        return pl.BlockSpec((n, chunk, 2 * HEAD_DIM), lambda h, info: (0, 0, column + h))

    anywhere = pl.BlockSpec(memory_space=pl.ANY)

    in_specs = [whole(kinfo.shape), whole(rinfo.shape)] + [mine_spec, other_spec] * 2
    operands = [kinfo, rinfo, mine[0], other[0], mine[1], other[1]]
    for (column, arrays), (_, n) in zip(kv_sets[:-1], parts):
        in_specs += [kv_spec(n, column)] * n_sub
        operands += arrays
    in_specs += [anywhere] * n_sub
    operands += kv_sets[-1][1]
    aliases = {}
    if call:
        aliases = {1 + len(operands) + i: i for i in range(4)}
        in_specs += [anywhere] * 4
        operands += list(outs)
    full = jax.ShapeDtypeStruct(mine[0].shape, BF16)
    part = jax.ShapeDtypeStruct(other[0].shape, BF16)
    out_shape = [full, part, full, part]
    out_specs = [mine_spec, other_spec, mine_spec, other_spec]
    for s, (_, n) in enumerate(parts):
        out_shape += [jax.ShapeDtypeStruct((n, chunk, heads * 2 * HEAD_DIM), BF16)] * n_sub
        out_specs += [kv_spec(n, 0) if s < len(parts) - 1 else anywhere] * n_sub
    pairs = rows * 5 * BLOCK * CORES * heads
    results = pl.pallas_call(
        functools.partial(
            attention_kernel, n_sub, chunk, group, not call, kv_sets[-1][0], parts
        ),
        grid_spec=pltpu.PrefetchScalarGridSpec(
            num_scalar_prefetch=1,
            grid=(heads,),
            in_specs=in_specs,
            out_specs=out_specs,
            scratch_shapes=[
                pltpu.SMEM((CORES, n_blocks + 1), jnp.int32),
                pltpu.VMEM((n_blocks, BLOCK, 2 * HEAD_DIM), BF16),
                pltpu.VMEM((n_blocks, BLOCK, 2 * HEAD_DIM), F32),
                pltpu.VMEM((CORES, n_blocks, BLOCK, rinfo.shape[3]), F32),
                pltpu.VMEM((n_blocks, BLOCK, rows), F32),
                pltpu.VMEM((n_blocks, BLOCK, rows), F32),
                pltpu.VMEM((8, rows), F32),
                pltpu.VMEM((8, rows), F32),
                pltpu.VMEM((8, rows), F32),
                pltpu.VMEM((HEAD_DIM, rows), F32),
            ]
            + [pltpu.VMEM((CORES, rows, HEAD_DIM), BF16)] * 4,
        ),
        out_shape=out_shape,
        input_output_aliases=aliases,
        compiler_params=pltpu.CompilerParams(vmem_limit_bytes=56 << 20),
        cost_estimate=pl.CostEstimate(
            flops=12 * pairs * HEAD_DIM, bytes_accessed=8 << 20, transcendentals=pairs
        ),
        name=f"attention_{call}",
    )(info, *operands)
    grads = [results[4 + n_sub * i : 4 + n_sub * (i + 1)] for i in range(len(parts))]
    return results[:4], grads


def blank(shape):
    return pl.pallas_call(
        lambda out: None,
        out_shape=jax.ShapeDtypeStruct(shape, BF16),
        out_specs=pl.BlockSpec(memory_space=pl.ANY),
        name="blank",
    )()


def per_device(query_rows, key_rows, value_rows, out_grad, segment_ids):
    chunk = query_rows.shape[0]
    planes, n_sub = lax.axis_size("z"), lax.axis_size("x")
    halves = 2 * planes
    z, y, c, x = (lax.axis_index(a) for a in ALL)
    half = 2 * z + y
    devices = planes * 2 * CORES * n_sub
    kv_heads = key_rows.shape[1] // HEAD_DIM
    group = query_rows.shape[1] // key_rows.shape[1]
    my_heads = kv_heads // CORES
    heads = my_heads // SPLIT
    call_width = heads * 2 * HEAD_DIM

    def swap_cores(a):
        return lax.ppermute(a, "c", [(0, 1), (1, 0)])

    def rotate(a, by):
        return lax.ppermute(a, "x", [(i, (i + by) % n_sub) for i in range(n_sub)])

    def spread(a):
        return [a] + [rotate(a, k) for k in range(1, n_sub)]

    def send(a, by, k):
        moves = [
            (h * n_sub + i, (h + by) * n_sub + (i + k) % n_sub)
            for h in range(halves)
            if 0 <= h + by < halves
            for i in range(n_sub)
        ]
        return lax.ppermute(a, ("z", "y", "x"), moves)

    def gather_back(arrays):
        total = arrays[0].astype(F32)
        for k in range(1, n_sub):
            total = total + rotate(arrays[k], -k).astype(F32)
        return total

    def half_of(a, core):
        width = a.shape[1] // CORES
        return lax.dynamic_slice_in_dim(a, core * width, width, axis=1)

    def columns(core):
        k, v = half_of(key_rows, core), half_of(value_rows, core)
        cut = lambda a, h: a[:, h * HEAD_DIM : (h + 1) * HEAD_DIM]
        return jnp.concatenate([cut(a, h) for h in range(my_heads) for a in (k, v)], axis=1)

    kv_mine = columns(c)
    kv_other = swap_cores(columns(1 - c))
    kv_both = [
        jnp.stack([a[:, i * call_width : (i + 1) * call_width] for a in (kv_mine, kv_other)])
        for i in range(SPLIT)
    ]
    q_send, g_send, _ = lax.optimization_barrier(
        (half_of(query_rows, 1 - c), half_of(out_grad, 1 - c), kv_other)
    )
    q_other = swap_cores(q_send)
    g_other = swap_cores(g_send)
    segment_ids, _ = lax.optimization_barrier((segment_ids, kv_other))
    ids = lax.all_to_all(
        jnp.broadcast_to(segment_ids[None], (devices, chunk)), ALL, split_axis=0, concat_axis=0, tiled=True
    )
    n0 = jnp.sum((ids == 0).astype(jnp.int32))
    wide = n0 > BLOCK

    prompt = jnp.where(c == 0, kv_mine, kv_other)[None]
    step = halves // 2
    while step:
        got = lax.ppermute(prompt, ("z", "y"), [(i, i + step) for i in range(0, halves, 2 * step)])
        if step == halves // 2:
            got, q_other, g_other = lax.optimization_barrier((got, q_other, g_other))
        prompt = jnp.where(half % (2 * step) == step, got, prompt)
        step //= 2
    prompt_set = spread(prompt)

    def fetch_wide(_):
        moved = jnp.concatenate(kv_both, axis=2)
        step = planes // 2
        while step:
            got = lax.ppermute(moved, "z", [(i, i + step) for i in range(0, planes, 2 * step)])
            moved = jnp.where(z % (2 * step) == step, got, moved)
            step //= 2
        across = lax.ppermute(moved, "y", [(0, 1), (1, 0)])
        moved = jnp.concatenate([jnp.where(y == 0, moved, across), jnp.where(y == 0, across, moved)])
        return tuple(spread(moved))

    def no_wide(_):
        return tuple(blank((WIDE, chunk, SPLIT * call_width)) for _ in range(n_sub))

    wide_set = lax.cond(wide, fetch_wide, no_wide, 0)

    bands = []
    for a in kv_both:
        if bands:
            a, _ = lax.optimization_barrier((a, bands[-1]))
        bands.append([[send(a, by, k) if by or k else a for k in range(n_sub)] for by in range(3)])

    row_chunk = jnp.stack([(2 * half + (c ^ r)) * n_sub + x for r in range(CORES)])
    row_pos = row_chunk[:, None] * chunk + jnp.arange(chunk, dtype=jnp.int32)
    row_seg = jnp.take(ids, row_chunk, axis=0)
    rinfo = jnp.tile(jnp.stack([row_pos, row_seg], axis=1)[:, :, None], (1, 1, 1, pl.cdiv(128, chunk)))
    starts = jnp.sum((ids[None] < row_seg[:, :1, None]).astype(jnp.int32), axis=(1, 2))
    sub = (x - jnp.arange(n_sub, dtype=jnp.int32)) % n_sub
    block = jnp.stack(
        [2 * (half - s) + (c ^ k) for s in range(3) for k in range(CORES)]
        + [jnp.zeros((), jnp.int32), c, 1 - c, 2 + c, 3 - c]
    )
    place = jnp.arange(block.shape[0])
    usable = jnp.where(
        place < 6, block >= jnp.where(wide, WIDE, 1), jnp.where(place == 6, ~wide, wide)
    )
    key_chunk = jnp.clip(block, 0)[:, None] * n_sub + sub[None]
    key_seg = jnp.take(ids, key_chunk.reshape(-1), axis=0).reshape(-1, BLOCK)
    key_pos = (key_chunk[..., None] * chunk + jnp.arange(chunk, dtype=jnp.int32)).reshape(-1, BLOCK)
    key_pos = jnp.where(usable[:, None], key_pos, FAR)
    kinfo = jnp.stack([key_pos, key_seg], axis=1)[..., None]
    first = block * BLOCK
    need = (
        usable[None]
        & (first[None] <= row_pos[:, -1:])
        & ((first[None] < n0) | (first[None] + BLOCK > starts[:, None]))
    )
    info = jnp.concatenate(
        [jnp.stack([c, wide.astype(jnp.int32)]), need.astype(jnp.int32).reshape(-1)]
    )

    outs = None
    owns, prompts, wide_parts = [], [], []
    for i in range(SPLIT):
        column = heads * i
        sets = [(0, b) for b in bands[i]] + [(column, prompt_set), (column, wide_set)]
        outs, grads = attention(
            i, info, kinfo, rinfo, (query_rows, out_grad), (q_other, g_other), sets, outs, group, heads
        )
        if owns:
            (outs, grads), owns[-1] = lax.optimization_barrier(((outs, grads), owns[-1]))
        owns.append(
            [send(grads[by][k], -by, -k) if by or k else grads[0][0] for by in range(3) for k in range(n_sub)]
        )
        prompts.append(grads[3])
        wide_parts.append(tuple(grads[4]))

    back = gather_back([jnp.concatenate([p[k] for p in prompts], axis=2) for k in range(n_sub)])[0]
    step = 1
    while step < halves:
        got = lax.ppermute(
            back.astype(BF16), ("z", "y"), [(j + step, j) for j in range(0, halves, 2 * step)]
        )
        back = back + got.astype(F32)
        step *= 2
    mine = (jnp.arange(CORES) == c)[:, None, None] & (half == 0)
    total = jnp.where(mine, back[None], 0.0) + jnp.concatenate(
        [sum(a.astype(F32) for a in arrays) for arrays in owns], axis=2
    )

    def return_wide(parts):
        total = gather_back([jnp.concatenate([p[k] for p in parts], axis=2) for k in range(n_sub)])
        total = total.astype(BF16)
        keep = jnp.where(y == 0, total[:2], total[2:])
        send = jnp.where(y == 0, total[2:], total[:2])
        back = keep.astype(F32) + lax.ppermute(send, "y", [(0, 1), (1, 0)]).astype(F32)
        step = 1
        while step < planes:
            got = lax.ppermute(back.astype(BF16), "z", [(j + step, j) for j in range(0, planes, 2 * step)])
            back = back + got.astype(F32)
            step *= 2
        return jnp.where(z == 0, back, 0.0)

    total = lax.cond(
        wide,
        lambda t, parts: t + return_wide(parts),
        lambda t, parts: t,
        total,
        tuple(wide_parts),
    ).astype(BF16)

    got = swap_cores(total[1])
    low = jnp.where(c == 0, total[0], got)
    high = jnp.where(c == 0, got, total[0])

    def columns_back(t):
        starts = [(2 * h + t) * HEAD_DIM for h in range(my_heads)]
        return jnp.concatenate([a[:, s : s + HEAD_DIM] for a in (low, high) for s in starts], axis=1)

    def join(full, part):
        start = (1 - c) * part.shape[1]
        return lax.dynamic_update_slice(full, swap_cores(part), (0, start))

    return join(outs[0], outs[1]), join(outs[2], outs[3]), columns_back(0), columns_back(1)


def solution(mesh):
    blk, uly = mesh.shape["blk"], mesh.shape["uly"]
    parts = Mesh(np.asarray(mesh.devices).reshape(blk // 4, 2, CORES, uly), ALL)
    rows = P(ALL, None)
    return jax.shard_map(
        per_device,
        mesh=parts,
        in_specs=(rows, rows, rows, rows, P(ALL)),
        out_specs=(rows, rows, rows, rows),
        check_vma=False,
    )
```

time: 242 us -> 225 us (0.930)
  starting transfers between devices: 37.1 us -> 67.9 us
  waiting for transfers between devices: 118 us -> 89.6 us
  local copies, waits for them, and re-layouts: 42 us -> 21.7 us
  Pallas kernels: 29.6 us -> 34.8 us
  other arithmetic: 14.4 us -> 10.9 us
    ppermute x8 -> x2, waiting for transfers between devices: 44.8 us -> 5.5 us  [rotate(): return lax.ppermute(a, 'x', [(i, (i + by) % n_sub) for i in range(n_sub)])]
    ppermute x10 -> x26, starting transfers between devices: 23.8 us -> 60.8 us  [the longest x20 42.1 us: send(): return lax.ppermute(a, ('z', 'y', 'x'), moves)]
    dynamic_slice x6 -> x1, local copies, waits for them, and re-layouts: 12.2 us -> 1.69 us  [half_of(): return lax.dynamic_slice_in_dim(a, core * width, width, axis=1)]
    ppermute x10 -> x26, waiting for transfers between devices: 69.4 us -> 78.3 us  [the longest x3 57.1 us: per_device(): lax.ppermute(back.astype(BF16), ('z', 'y'), [(j + step, j) for j in range...]
    reshape x3 -> x0, local copies, waits for them, and re-layouts: 8.14 us -> none  [the longest x1 4.47 us: per_device(): g_cols = out_grad.reshape(chunk, CORES, -1)]
    ppermute x8 -> x2, starting transfers between devices: 8.36 us -> 2.83 us  [rotate(): return lax.ppermute(a, 'x', [(i, (i + by) % n_sub) for i in range(n_sub)])]
    pallas_call x1 -> x4, Pallas kernels: 29.6 us -> 34.8 us  [the longest x2 34.8 us: attention(): pl.pallas_call(functools.partial(attention_kernel, n_sub, chunk, group, n...]
    all_to_all x1, waiting for transfers between devices: 1.23 us -> 5.79 us  [per_device(): lax.all_to_all(jnp.broadcast_to(segment_ids[None], (devices, chunk)), ALL...]
  transfers between devices with their start and end apart: 25 -> 35, of which waited for: 14 -> 11; matrix products, arithmetic and copies ran while one was open for 20% -> 8% of each run, Pallas kernels for 0% -> 15%
where the time goes in v1:
time: 225 us; the launch traced here: 227 us
  waiting for transfers between devices  89.6 us (40%)
  starting transfers between devices  67.9 us (30%)
  Pallas kernels  34.8 us (15%)
  local copies, waits for them, and re-layouts  21.7 us (10%)
  other arithmetic  10.9 us (5%)
    ppermute x3, waiting for transfers between devices, per_device(): lax.ppermute(back.astype(BF16), ('z', 'y'), [(j + step, j) for j in range...  57.1 us
    ppermute x20, starting transfers between devices, send(): return lax.ppermute(a, ('z', 'y', 'x'), moves)  42.1 us
    pallas_call x2, Pallas kernels, attention(): pl.pallas_call(functools.partial(attention_kernel, n_sub, chunk, group, n...  34.8 us
    ppermute x3, starting transfers between devices, per_device(): lax.ppermute(prompt, ('z', 'y'), [(i, i + step) for i in range(0, halves,...  14.8 us
    ppermute x3, waiting for transfers between devices, per_device(): lax.ppermute(prompt, ('z', 'y'), [(i, i + step) for i in range(0, halves,...  11.3 us
    ppermute x20, waiting for transfers between devices, send(): return lax.ppermute(a, ('z', 'y', 'x'), moves)  9.87 us
    unnamed x61, local copies, waits for them, and re-layouts  9.84 us
    all_to_all x1, waiting for transfers between devices, per_device(): lax.all_to_all(jnp.broadcast_to(segment_ids[None], (devices, chunk)), ALL...  5.79 us
  transfers between devices with their start and end apart: 35, of which 11 were waited for; matrix products, arithmetic and copies ran while one was open for 8% of the time, Pallas kernels for 15%

profile of v1, /device:TPU:0, one launch (start us, length us, event | category | flops | bytes accessed | tf_op | source)
XLA Modules:
  0.0 227.2 jit_solution(12606907305341700488)
XLA Ops:
  9.8 1.7 constant_dynamic-slice_fusion.5
  12.9 6.2 %collective-permute-start.16 = (bf16[2,128,512]{2,1,0:T(8,128)(2,1)}, bf16[2,128,512]{2,1,0:T(8,128)(2,1)}, u32[]{:S(2)}, u32[]{:S(2)}) collective-permute-start(bf16[2,128,512]{2,1,0:T(8,128)(2,1)} %pad_maximum_fusion.3.refs_7_), channel_id=1, source_target_pairs={{0,9},{1,8},{4,13},{5,12},{8,17},{9,16},{12,21},{13,20},{16,25},{1... | collective-permute-start | bytes 786440 | tf_op jit(solution)/shard_map/ppermute | solution.py:302
  19.1 3.5 %collective-permute-start.15 = (bf16[2,128,512]{2,1,0:T(8,128)(2,1)}, bf16[2,128,512]{2,1,0:T(8,128)(2,1)}, u32[]{:S(2)}, u32[]{:S(2)}) collective-permute-start(bf16[2,128,512]{2,1,0:T(8,128)(2,1)} %pad_maximum_fusion.3.refs_7_), channel_id=1, source_target_pairs={{0,8},{1,9},{4,12},{5,13},{8,16},{9,17},{12,20},{13,21},{16,24},{1... | collective-permute-start | bytes 786440 | tf_op jit(solution)/shard_map/ppermute | solution.py:302
  23.2 2.5 %all-to-all-start = ((s32[32,1,128]{2,1,0:T(1,128)}), s32[32,1,128]{2,1,0:T(1,128)S(1)}, u32[]{:S(2)}, u32[]{:S(2)}) async-start(s32[32,1,128]{2,1,0:T(1,128)} %broadcast_in_dim.101), calls=%async_computation | async-start | bytes 32768 | tf_op jit(solution)/shard_map/all_to_all | solution.py:331
  27.0 5.8 %all-to-all-done = s32[32,1,128]{2,1,0:T(1,128)S(1)} async-done(((s32[32,1,128]{2,1,0:T(1,128)}), s32[32,1,128]{2,1,0:T(1,128)S(1)}, u32[]{:S(2)}, u32[]{:S(2)}) %all-to-all-start) | async-done | bytes 16416 | tf_op jit(solution)/shard_map/all_to_all | solution.py:331
  34.2 4.2 %collective-permute-start.9 = (bf16[1,128,1024]{2,1,0:T(8,128)(2,1)}, bf16[1,128,1024]{2,1,0:T(8,128)(2,1)S(1)}, u32[]{:S(2)}, u32[]{:S(2)}) collective-permute-start(bf16[1,128,1024]{2,1,0:T(8,128)(2,1)} %select_bitcast_fusion), channel_id=1, source_target_pairs={{0,16},{1,17},{2,18},{3,19}} | collective-permute-start | bytes 786440 | tf_op jit(solution)/shard_map/ppermute | solution.py:340
  39.8 4.3 %collective-permute-done.9 = bf16[1,128,1024]{2,1,0:T(8,128)(2,1)S(1)} collective-permute-done((bf16[1,128,1024]{2,1,0:T(8,128)(2,1)}, bf16[1,128,1024]{2,1,0:T(8,128)(2,1)S(1)}, u32[]{:S(2)}, u32[]{:S(2)}) %collective-permute-start.9) | collective-permute-done | bytes 262176 | tf_op jit(solution)/shard_map/ppermute | solution.py:340
  45.5 1.3 collective-permute-start.13
  47.8 9.3 %collective-permute-start.22 = (bf16[1,128,1024]{2,1,0:T(8,128)(2,1)S(1)}, bf16[1,128,1024]{2,1,0:T(8,128)(2,1)S(1)}, u32[]{:S(2)}, u32[]{:S(2)}) collective-permute-start(bf16[1,128,1024]{2,1,0:T(8,128)(2,1)S(1)} %broadcast_select_fusion.6), channel_id=1, source_target_pairs={{0,8},{16,24},{1,9},{17,25},{2,10},{18,26},{3,11},{19,27}} | collective-permute-start | bytes 786440 | tf_op jit(solution)/shard_map/ppermute | solution.py:340
  57.9 3.3 %collective-permute-done.22 = bf16[1,128,1024]{2,1,0:T(8,128)(2,1)S(1)} collective-permute-done((bf16[1,128,1024]{2,1,0:T(8,128)(2,1)S(1)}, bf16[1,128,1024]{2,1,0:T(8,128)(2,1)S(1)}, u32[]{:S(2)}, u32[]{:S(2)}) %collective-permute-start.22) | collective-permute-done | bytes 262176 | tf_op jit(solution)/shard_map/ppermute | solution.py:340
  61.2 1.3 collective-permute-start.23
  62.7 3.7 %collective-permute-done.23 = bf16[1,128,1024]{2,1,0:T(8,128)(2,1)S(1)} collective-permute-done((bf16[1,128,1024]{2,1,0:T(8,128)(2,1)S(1)}, bf16[1,128,1024]{2,1,0:T(8,128)(2,1)S(1)}, u32[]{:S(2)}, u32[]{:S(2)}) %collective-permute-start.23) | collective-permute-done | bytes 262176 | tf_op jit(solution)/shard_map/ppermute | solution.py:340
  67.0 1.6 collective-permute-start.24
  68.6 2.4 %copy.30.refs_1_ = s32[11,2,256,1]{3,2,1,0:T(8,128)} copy(s32[11,2,256,1]{2,0,1,3:T(8,128)S(1)} %add_bitcast_fusion) | data formatting | bytes 45056 | tf_op jit(solution)/shard_map/broadcast_in_dim | solution.py:387
  72.2 2.1 collective-permute-done.12.refs_8_
  74.4 7.3 %collective-permute-start.21 = (bf16[2,128,512]{2,1,0:T(8,128)(2,1)S(1)}, bf16[2,128,512]{2,1,0:T(8,128)(2,1)S(1)}, u32[]{:S(2)}, u32[]{:S(2)}) collective-permute-start(bf16[2,128,512]{2,1,0:T(8,128)(2,1)S(1)} %pad_maximum_fusion.2.refs_7_), channel_id=1, source_target_pairs={{0,9},{1,8},{4,13},{5,12},{8,17},{9,16},{12,21},{13,20},{16,25},{1... | collective-permute-start | bytes 786440 | tf_op jit(solution)/shard_map/ppermute | solution.py:302
  81.7 1.9 collective-permute-start.20
  83.6 4.4 %collective-permute-start.19 = (bf16[2,128,512]{2,1,0:T(8,128)(2,1)S(1)}, bf16[2,128,512]{2,1,0:T(8,128)(2,1)S(1)}, u32[]{:S(2)}, u32[]{:S(2)}) collective-permute-start(bf16[2,128,512]{2,1,0:T(8,128)(2,1)S(1)} %pad_maximum_fusion.2.refs_7_), channel_id=1, source_target_pairs={{0,5},{1,4},{4,9},{5,8},{8,13},{9,12},{12,17},{13,16},{16,21},{17,... | collective-permute-start | bytes 786440 | tf_op jit(solution)/shard_map/ppermute | solution.py:302
  88.0 1.6 collective-permute-start.18
  90.6 17.5 %attention_0.1 = (bf16[128,8192]{1,0:T(8,128)(2,1)}, bf16[128,4096]{1,0:T(8,128)(2,1)}, bf16[128,8192]{1,0:T(8,128)(2,1)}, bf16[128,4096]{1,0:T(8,128)(2,1)}, bf...) custom-call(s32[24]{0:T(128)} %pad_add_fusion.2.refs_0_, ...), custom_call_target="tpu_custom_call" | custom-call | flops 8053063680 | bytes 8388608 | tf_op jit(solution)/shard_map/attention_0/pallas_call | solution.py:229
  113.4 1.5 collective-permute-start.29
  114.9 17.3 %attention_1.1 = (bf16[128,8192]{1,0:T(8,128)(2,1)}, bf16[128,4096]{1,0:T(8,128)(2,1)}, bf16[128,8192]{1,0:T(8,128)(2,1)}, bf16[128,4096]{1,0:T(8,128)(2,1)}, bf...) custom-call(s32[24]{0:T(128)} %pad_add_fusion.2.refs_0_, ...), custom_call_target="tpu_custom_call", output_to_operand_aliasing={{0}: (17, {}), {1}: (18, {}), {2}: (19, {}), {3}: (20, {})} | custom-call | flops 8053063680 | bytes 8388608 | tf_op jit(solution)/shard_map/attention_1/pallas_call | solution.py:229
  132.3 4.5 %collective-permute-done.28 = bf16[2,128,512]{2,1,0:T(8,128)(2,1)S(1)} collective-permute-done((bf16[2,128,512]{2,1,0:T(8,128)(2,1)}, bf16[2,128,512]{2,1,0:T(8,128)(2,1)S(1)}, u32[]{:S(2)}, u32[]{:S(2)}) %collective-permute-start.28) | collective-permute-done | bytes 262176 | tf_op jit(solution)/shard_map/ppermute | solution.py:302
  136.8 3.2 %collective-permute-done.29 = bf16[2,128,512]{2,1,0:T(8,128)(2,1)S(1)} collective-permute-done((bf16[2,128,512]{2,1,0:T(8,128)(2,1)}, bf16[2,128,512]{2,1,0:T(8,128)(2,1)S(1)}, u32[]{:S(2)}, u32[]{:S(2)}) %collective-permute-start.29) | collective-permute-done | bytes 262176 | tf_op jit(solution)/shard_map/ppermute | solution.py:302
  142.9 5.5 %collective-permute-done.32 = bf16[1,128,1024]{2,1,0:T(8,128)(2,1)S(1)} collective-permute-done((bf16[1,128,1024]{2,1,0:T(8,128)(2,1)S(1)}, bf16[1,128,1024]{2,1,0:T(8,128)(2,1)S(1)}, u32[]{:S(2)}, u32[]{:S(2)}) %collective-permute-start.32) | collective-permute-done | bytes 262176 | tf_op jit(solution)/shard_map/ppermute | solution.py:290
  152.0 1.4 collective-permute-start.37
  156.0 9.4 %collective-permute-done.33 = bf16[128,1024]{1,0:T(8,128)(2,1)S(1)} collective-permute-done((bf16[128,1024]{1,0:T(8,128)(2,1)S(1)}, bf16[128,1024]{1,0:T(8,128)(2,1)S(1)}, u32[]{:S(2)}, u32[]{:S(2)}) %collective-permute-start.33) | collective-permute-done | bytes 262176 | tf_op jit(solution)/shard_map/ppermute | solution.py:417
  170.2 20.2 %collective-permute-done.34 = bf16[128,1024]{1,0:T(8,128)(2,1)S(1)} collective-permute-done((bf16[128,1024]{1,0:T(8,128)(2,1)S(1)}, bf16[128,1024]{1,0:T(8,128)(2,1)S(1)}, u32[]{:S(2)}, u32[]{:S(2)}) %collective-permute-start.34) | collective-permute-done | bytes 262176 | tf_op jit(solution)/shard_map/ppermute | solution.py:417
  192.7 27.5 %collective-permute-done.35 = bf16[128,1024]{1,0:T(8,128)(2,1)S(1)} collective-permute-done((bf16[128,1024]{1,0:T(8,128)(2,1)S(1)}, bf16[128,1024]{1,0:T(8,128)(2,1)S(1)}, u32[]{:S(2)}, u32[]{:S(2)}) %collective-permute-start.35) | collective-permute-done | bytes 262176 | tf_op jit(solution)/shard_map/ppermute | solution.py:417
  220.8 1.4 copy-done.10
  222.2 1.3 constant_dynamic-update-slice_fusion.35
  223.6 2.1 constant_dynamic-update-slice_fusion.34
  (171 shorter events, 43.7 us)
Async XLA Ops:
  12.9 54.1 %collective-permute-start.16 = (bf16[2,128,512]{2,1,0:T(8,128)(2,1)}, bf16[2,128,512]{2,1,0:T(8,128)(2,1)}, u32[]{:S(2)}, u32[]{:S(2)}) collective-permute-start(bf16[2,128,512]{2,1,0:T(8,128)(2,1)} %pad_maximum_fusion.3.refs_7_), channel_id=1, source_target_pairs={{0,9},{1,8},{4,13},{5,12},{8,17},{9,16},{12,21},{13,20},{16,25},{1... | collective-permute-start | bytes 786440 | tf_op jit(solution)/shard_map/ppermute | solution.py:302
  19.1 53.1 %collective-permute-start.15 = (bf16[2,128,512]{2,1,0:T(8,128)(2,1)}, bf16[2,128,512]{2,1,0:T(8,128)(2,1)}, u32[]{:S(2)}, u32[]{:S(2)}) collective-permute-start(bf16[2,128,512]{2,1,0:T(8,128)(2,1)} %pad_maximum_fusion.3.refs_7_), channel_id=1, source_target_pairs={{0,8},{1,9},{4,12},{5,13},{8,16},{9,17},{12,20},{13,21},{16,24},{1... | collective-permute-start | bytes 786440 | tf_op jit(solution)/shard_map/ppermute | solution.py:302
  23.2 9.7 %all-to-all-start = ((s32[32,1,128]{2,1,0:T(1,128)}), s32[32,1,128]{2,1,0:T(1,128)S(1)}, u32[]{:S(2)}, u32[]{:S(2)}) async-start(s32[32,1,128]{2,1,0:T(1,128)} %broadcast_in_dim.101), calls=%async_computation | async-start | bytes 32768 | tf_op jit(solution)/shard_map/all_to_all | solution.py:331
  25.7 19.8 %collective-permute-start.10 = (bf16[128,4096]{1,0:T(8,128)(2,1)S(1)}, bf16[128,4096]{1,0:T(8,128)(2,1)}, u32[]{:S(2)}, u32[]{:S(2)}) collective-permute-start(bf16[128,4096]{1,0:T(8,128)(2,1)S(1)} %get-tuple-element.99), channel_id=1, source_target_pairs={{0,2},{2,0},{1,3},{3,1},{4,6},{6,4},{5,7},{7,5},{8,10},{10,8},{9,1... | collective-permute-start | bytes 3145736 | tf_op jit(solution)/shard_map/ppermute | solution.py:287
  25.9 20.9 %collective-permute-start.11 = (bf16[128,4096]{1,0:T(8,128)(2,1)S(1)}, bf16[128,4096]{1,0:T(8,128)(2,1)}, u32[]{:S(2)}, u32[]{:S(2)}) collective-permute-start(bf16[128,4096]{1,0:T(8,128)(2,1)S(1)} %get-tuple-element.100), channel_id=1, source_target_pairs={{0,2},{2,0},{1,3},{3,1},{4,6},{6,4},{5,7},{7,5},{8,10},{10,8},{9,1... | collective-permute-start | bytes 3145736 | tf_op jit(solution)/shard_map/ppermute | solution.py:287
  34.2 10.0 %collective-permute-start.9 = (bf16[1,128,1024]{2,1,0:T(8,128)(2,1)}, bf16[1,128,1024]{2,1,0:T(8,128)(2,1)S(1)}, u32[]{:S(2)}, u32[]{:S(2)}) collective-permute-start(bf16[1,128,1024]{2,1,0:T(8,128)(2,1)} %select_bitcast_fusion), channel_id=1, source_target_pairs={{0,16},{1,17},{2,18},{3,19}} | collective-permute-start | bytes 786440 | tf_op jit(solution)/shard_map/ppermute | solution.py:340
  44.2 28.1 %collective-permute-start.14 = (bf16[2,128,512]{2,1,0:T(8,128)(2,1)}, bf16[2,128,512]{2,1,0:T(8,128)(2,1)S(1)}, u32[]{:S(2)}, u32[]{:S(2)}) collective-permute-start(bf16[2,128,512]{2,1,0:T(8,128)(2,1)} %pad_maximum_fusion.3.refs_7_), channel_id=1, source_target_pairs={{0,5},{1,4},{4,9},{5,8},{8,13},{9,12},{12,17},{13,16},{16,21},{17,... | collective-permute-start | bytes 786440 | tf_op jit(solution)/shard_map/ppermute | solution.py:302
  45.5 26.8 %collective-permute-start.13 = (bf16[2,128,512]{2,1,0:T(8,128)(2,1)}, bf16[2,128,512]{2,1,0:T(8,128)(2,1)S(1)}, u32[]{:S(2)}, u32[]{:S(2)}) collective-permute-start(bf16[2,128,512]{2,1,0:T(8,128)(2,1)} %pad_maximum_fusion.3.refs_7_), channel_id=1, source_target_pairs={{0,4},{1,5},{4,8},{5,9},{8,12},{9,13},{12,16},{13,17},{16,20},{17,... | collective-permute-start | bytes 786440 | tf_op jit(solution)/shard_map/ppermute | solution.py:302
  47.8 13.4 %collective-permute-start.22 = (bf16[1,128,1024]{2,1,0:T(8,128)(2,1)S(1)}, bf16[1,128,1024]{2,1,0:T(8,128)(2,1)S(1)}, u32[]{:S(2)}, u32[]{:S(2)}) collective-permute-start(bf16[1,128,1024]{2,1,0:T(8,128)(2,1)S(1)} %broadcast_select_fusion.6), channel_id=1, source_target_pairs={{0,8},{16,24},{1,9},{17,25},{2,10},{18,26},{3,11},{19,27}} | collective-permute-start | bytes 786440 | tf_op jit(solution)/shard_map/ppermute | solution.py:340
  66.4 8.0 %collective-permute-start.12 = (bf16[2,128,512]{2,1,0:T(8,128)(2,1)}, bf16[2,128,512]{2,1,0:T(8,128)(2,1)S(1)}, u32[]{:S(2)}, u32[]{:S(2)}) collective-permute-start(bf16[2,128,512]{2,1,0:T(8,128)(2,1)} %pad_maximum_fusion.3.refs_7_), channel_id=1, source_target_pairs={{0,1},{1,0},{4,5},{5,4},{8,9},{9,8},{12,13},{13,12},{16,17},{17,16... | collective-permute-start | bytes 786440 | tf_op jit(solution)/shard_map/ppermute | solution.py:302
  67.0 22.7 %collective-permute-start.24 = (bf16[1,128,1024]{2,1,0:T(8,128)(2,1)S(1)}, bf16[1,128,1024]{2,1,0:T(8,128)(2,1)S(1)}, u32[]{:S(2)}, u32[]{:S(2)}) collective-permute-start(bf16[1,128,1024]{2,1,0:T(8,128)(2,1)S(1)} %broadcast_select_fusion.8.refs_13_), channel_id=1, source_target_pairs={{0,1},{1,0},{2,3},{3,2},{4,5},{5,4},{6,7},{7,6},{8,9},{9,8},{10,11... | collective-permute-start | bytes 786440 | tf_op jit(solution)/shard_map/ppermute | solution.py:290
  74.4 33.8 %collective-permute-start.21 = (bf16[2,128,512]{2,1,0:T(8,128)(2,1)S(1)}, bf16[2,128,512]{2,1,0:T(8,128)(2,1)S(1)}, u32[]{:S(2)}, u32[]{:S(2)}) collective-permute-start(bf16[2,128,512]{2,1,0:T(8,128)(2,1)S(1)} %pad_maximum_fusion.2.refs_7_), channel_id=1, source_target_pairs={{0,9},{1,8},{4,13},{5,12},{8,17},{9,16},{12,21},{13,20},{16,25},{1... | collective-permute-start | bytes 786440 | tf_op jit(solution)/shard_map/ppermute | solution.py:302
  81.7 27.7 %collective-permute-start.20 = (bf16[2,128,512]{2,1,0:T(8,128)(2,1)S(1)}, bf16[2,128,512]{2,1,0:T(8,128)(2,1)S(1)}, u32[]{:S(2)}, u32[]{:S(2)}) collective-permute-start(bf16[2,128,512]{2,1,0:T(8,128)(2,1)S(1)} %pad_maximum_fusion.2.refs_7_), channel_id=1, source_target_pairs={{0,8},{1,9},{4,12},{5,13},{8,16},{9,17},{12,20},{13,21},{16,24},{1... | collective-permute-start | bytes 786440 | tf_op jit(solution)/shard_map/ppermute | solution.py:302
  83.6 27.1 %collective-permute-start.19 = (bf16[2,128,512]{2,1,0:T(8,128)(2,1)S(1)}, bf16[2,128,512]{2,1,0:T(8,128)(2,1)S(1)}, u32[]{:S(2)}, u32[]{:S(2)}) collective-permute-start(bf16[2,128,512]{2,1,0:T(8,128)(2,1)S(1)} %pad_maximum_fusion.2.refs_7_), channel_id=1, source_target_pairs={{0,5},{1,4},{4,9},{5,8},{8,13},{9,12},{12,17},{13,16},{16,21},{17,... | collective-permute-start | bytes 786440 | tf_op jit(solution)/shard_map/ppermute | solution.py:302
  88.0 24.0 %collective-permute-start.18 = (bf16[2,128,512]{2,1,0:T(8,128)(2,1)S(1)}, bf16[2,128,512]{2,1,0:T(8,128)(2,1)S(1)}, u32[]{:S(2)}, u32[]{:S(2)}) collective-permute-start(bf16[2,128,512]{2,1,0:T(8,128)(2,1)S(1)} %pad_maximum_fusion.2.refs_7_), channel_id=1, source_target_pairs={{0,4},{1,5},{4,8},{5,9},{8,12},{9,13},{12,16},{13,17},{16,20},{17,... | collective-permute-start | bytes 786440 | tf_op jit(solution)/shard_map/ppermute | solution.py:302
  89.7 23.6 %collective-permute-start.17 = (bf16[2,128,512]{2,1,0:T(8,128)(2,1)S(1)}, bf16[2,128,512]{2,1,0:T(8,128)(2,1)S(1)}, u32[]{:S(2)}, u32[]{:S(2)}) collective-permute-start(bf16[2,128,512]{2,1,0:T(8,128)(2,1)S(1)} %pad_maximum_fusion.2.refs_7_), channel_id=1, source_target_pairs={{0,1},{1,0},{4,5},{5,4},{8,9},{9,8},{12,13},{13,12},{16,17},{17,16... | collective-permute-start | bytes 786440 | tf_op jit(solution)/shard_map/ppermute | solution.py:302
  108.2 24.1 %collective-permute-start.25 = (bf16[2,128,512]{2,1,0:T(8,128)(2,1)}, bf16[2,128,512]{2,1,0:T(8,128)(2,1)S(1)}, u32[]{:S(2)}, u32[]{:S(2)}) collective-permute-start(bf16[2,128,512]{2,1,0:T(8,128)(2,1)} %get-tuple-element.126), channel_id=1, source_target_pairs={{0,1},{1,0},{4,5},{5,4},{8,9},{9,8},{12,13},{13,12},{16,17},{17,16... | collective-permute-start | bytes 786440 | tf_op jit(solution)/shard_map/ppermute | solution.py:302
  109.4 22.9 %collective-permute-start.26 = (bf16[2,128,512]{2,1,0:T(8,128)(2,1)}, bf16[2,128,512]{2,1,0:T(8,128)(2,1)S(1)}, u32[]{:S(2)}, u32[]{:S(2)}) collective-permute-start(bf16[2,128,512]{2,1,0:T(8,128)(2,1)} %get-tuple-element.127), channel_id=1, source_target_pairs={{4,0},{5,1},{8,4},{9,5},{12,8},{13,9},{16,12},{17,13},{20,16},{21,... | collective-permute-start | bytes 786440 | tf_op jit(solution)/shard_map/ppermute | solution.py:302
  110.7 21.6 %collective-permute-start.27 = (bf16[2,128,512]{2,1,0:T(8,128)(2,1)}, bf16[2,128,512]{2,1,0:T(8,128)(2,1)S(1)}, u32[]{:S(2)}, u32[]{:S(2)}) collective-permute-start(bf16[2,128,512]{2,1,0:T(8,128)(2,1)} %get-tuple-element.128), channel_id=1, source_target_pairs={{4,1},{5,0},{8,5},{9,4},{12,9},{13,8},{16,13},{17,12},{20,17},{21,... | collective-permute-start | bytes 786440 | tf_op jit(solution)/shard_map/ppermute | solution.py:302
  112.0 24.8 %collective-permute-start.28 = (bf16[2,128,512]{2,1,0:T(8,128)(2,1)}, bf16[2,128,512]{2,1,0:T(8,128)(2,1)S(1)}, u32[]{:S(2)}, u32[]{:S(2)}) collective-permute-start(bf16[2,128,512]{2,1,0:T(8,128)(2,1)} %get-tuple-element.129), channel_id=1, source_target_pairs={{8,0},{9,1},{12,4},{13,5},{16,8},{17,9},{20,12},{21,13},{24,16},{2... | collective-permute-start | bytes 786440 | tf_op jit(solution)/shard_map/ppermute | solution.py:302
  113.4 26.6 %collective-permute-start.29 = (bf16[2,128,512]{2,1,0:T(8,128)(2,1)}, bf16[2,128,512]{2,1,0:T(8,128)(2,1)S(1)}, u32[]{:S(2)}, u32[]{:S(2)}) collective-permute-start(bf16[2,128,512]{2,1,0:T(8,128)(2,1)} %get-tuple-element.130), channel_id=1, source_target_pairs={{8,1},{9,0},{12,5},{13,4},{16,9},{17,8},{20,13},{21,12},{24,17},{2... | collective-permute-start | bytes 786440 | tf_op jit(solution)/shard_map/ppermute | solution.py:302
  141.6 6.8 %collective-permute-start.32 = (bf16[1,128,1024]{2,1,0:T(8,128)(2,1)S(1)}, bf16[1,128,1024]{2,1,0:T(8,128)(2,1)S(1)}, u32[]{:S(2)}, u32[]{:S(2)}) collective-permute-start(bf16[1,128,1024]{2,1,0:T(8,128)(2,1)S(1)} %pad_maximum_fusion.5), channel_id=1, source_target_pairs={{0,1},{1,0},{2,3},{3,2},{4,5},{5,4},{6,7},{7,6},{8,9},{9,8},{10,11... | collective-permute-start | bytes 786440 | tf_op jit(solution)/shard_map/ppermute | solution.py:290
  149.4 16.0 %collective-permute-start.33 = (bf16[128,1024]{1,0:T(8,128)(2,1)S(1)}, bf16[128,1024]{1,0:T(8,128)(2,1)S(1)}, u32[]{:S(2)}, u32[]{:S(2)}) collective-permute-start(bf16[128,1024]{1,0:T(8,128)(2,1)S(1)} %bitcast_convert_fusion), channel_id=1, source_target_pairs={{4,0},{12,8},{20,16},{28,24},{5,1},{13,9},{21,17},{29,25},{6,2},{1... | collective-permute-start | bytes 786440 | tf_op jit(solution)/shard_map/ppermute | solution.py:417
  150.7 17.0 %collective-permute-start.36 = (bf16[2,128,512]{2,1,0:T(8,128)(2,1)}, bf16[2,128,512]{2,1,0:T(8,128)(2,1)S(1)}, u32[]{:S(2)}, u32[]{:S(2)}) collective-permute-start(bf16[2,128,512]{2,1,0:T(8,128)(2,1)} %get-tuple-element.146), channel_id=1, source_target_pairs={{0,1},{1,0},{4,5},{5,4},{8,9},{9,8},{12,13},{13,12},{16,17},{17,16... | collective-permute-start | bytes 786440 | tf_op jit(solution)/shard_map/ppermute | solution.py:302
  152.0 38.6 %collective-permute-start.37 = (bf16[2,128,512]{2,1,0:T(8,128)(2,1)}, bf16[2,128,512]{2,1,0:T(8,128)(2,1)S(1)}, u32[]{:S(2)}, u32[]{:S(2)}) collective-permute-start(bf16[2,128,512]{2,1,0:T(8,128)(2,1)} %get-tuple-element.147), channel_id=1, source_target_pairs={{4,0},{5,1},{8,4},{9,5},{12,8},{13,9},{16,12},{17,13},{20,16},{21,... | collective-permute-start | bytes 786440 | tf_op jit(solution)/shard_map/ppermute | solution.py:302
  153.4 37.8 %collective-permute-start.38 = (bf16[2,128,512]{2,1,0:T(8,128)(2,1)}, bf16[2,128,512]{2,1,0:T(8,128)(2,1)S(1)}, u32[]{:S(2)}, u32[]{:S(2)}) collective-permute-start(bf16[2,128,512]{2,1,0:T(8,128)(2,1)} %get-tuple-element.148), channel_id=1, source_target_pairs={{4,1},{5,0},{8,5},{9,4},{12,9},{13,8},{16,13},{17,12},{20,17},{21,... | collective-permute-start | bytes 786440 | tf_op jit(solution)/shard_map/ppermute | solution.py:302
  154.7 37.8 %collective-permute-start.39 = (bf16[2,128,512]{2,1,0:T(8,128)(2,1)}, bf16[2,128,512]{2,1,0:T(8,128)(2,1)S(1)}, u32[]{:S(2)}, u32[]{:S(2)}) collective-permute-start(bf16[2,128,512]{2,1,0:T(8,128)(2,1)} %get-tuple-element.149), channel_id=1, source_target_pairs={{8,0},{9,1},{12,4},{13,5},{16,8},{17,9},{20,12},{21,13},{24,16},{2... | collective-permute-start | bytes 786440 | tf_op jit(solution)/shard_map/ppermute | solution.py:302
  165.4 27.1 %collective-permute-start.40 = (bf16[2,128,512]{2,1,0:T(8,128)(2,1)}, bf16[2,128,512]{2,1,0:T(8,128)(2,1)S(1)}, u32[]{:S(2)}, u32[]{:S(2)}) collective-permute-start(bf16[2,128,512]{2,1,0:T(8,128)(2,1)} %get-tuple-element.150), channel_id=1, source_target_pairs={{8,1},{9,0},{12,5},{13,4},{16,9},{17,8},{20,13},{21,12},{24,17},{2... | collective-permute-start | bytes 786440 | tf_op jit(solution)/shard_map/ppermute | solution.py:302
  167.7 22.7 %collective-permute-start.34 = (bf16[128,1024]{1,0:T(8,128)(2,1)S(1)}, bf16[128,1024]{1,0:T(8,128)(2,1)S(1)}, u32[]{:S(2)}, u32[]{:S(2)}) collective-permute-start(bf16[128,1024]{1,0:T(8,128)(2,1)S(1)} %fusion.7), channel_id=1, source_target_pairs={{8,0},{24,16},{9,1},{25,17},{10,2},{26,18},{11,3},{27,19}} | collective-permute-start | bytes 786440 | tf_op jit(solution)/shard_map/ppermute | solution.py:417
  190.4 30.4 %collective-permute-start.30 = (bf16[128,4096]{1,0:T(8,128)(2,1)}, bf16[128,4096]{1,0:T(8,128)(2,1)}, u32[]{:S(2)}, u32[]{:S(2)}) collective-permute-start(bf16[128,4096]{1,0:T(8,128)(2,1)} %get-tuple-element.132), channel_id=1, source_target_pairs={{0,2},{2,0},{1,3},{3,1},{4,6},{6,4},{5,7},{7,5},{8,10},{10,8},{9,1... | collective-permute-start | bytes 3145736 | tf_op jit(solution)/shard_map/ppermute | solution.py:287
  190.6 33.0 %collective-permute-start.31 = (bf16[128,4096]{1,0:T(8,128)(2,1)}, bf16[128,4096]{1,0:T(8,128)(2,1)}, u32[]{:S(2)}, u32[]{:S(2)}) collective-permute-start(bf16[128,4096]{1,0:T(8,128)(2,1)} %get-tuple-element.134), channel_id=1, source_target_pairs={{0,2},{2,0},{1,3},{3,1},{4,6},{6,4},{5,7},{7,5},{8,10},{10,8},{9,1... | collective-permute-start | bytes 3145736 | tf_op jit(solution)/shard_map/ppermute | solution.py:287
  191.2 29.0 %collective-permute-start.35 = (bf16[128,1024]{1,0:T(8,128)(2,1)S(1)}, bf16[128,1024]{1,0:T(8,128)(2,1)S(1)}, u32[]{:S(2)}, u32[]{:S(2)}) collective-permute-start(bf16[128,1024]{1,0:T(8,128)(2,1)S(1)} %fusion.2), channel_id=1, source_target_pairs={{16,0},{17,1},{18,2},{19,3}} | collective-permute-start | bytes 786440 | tf_op jit(solution)/shard_map/ppermute | solution.py:417
  (26 other events, 321.2 us)

commit v2 on v1

--- a/solution.py
+++ b/solution.py
@@ -28,16 +28,16 @@
 
 def attention_kernel(n_sub, chunk, group, first_call, wide_column, parts, *refs):
     info, kinfo, rinfo = refs[:3]
-    q_refs, g_refs = refs[3:5], refs[5:7]
-    at = 7
+    q_mine, g_mine, other = refs[3:6]
+    at = 6
     kv_refs = []
     for _ in parts:
         kv_refs.append(refs[at : at + n_sub])
         at += n_sub
     if not first_call:
-        at += 4
-    o_refs, dq_refs = refs[at : at + 2], refs[at + 2 : at + 4]
-    at += 4
+        at += 3
+    o_mine, dq_mine, other_out = refs[at : at + 3]
+    at += 3
     dkv_refs = []
     for _ in parts:
         dkv_refs.append(refs[at : at + n_sub])
@@ -48,7 +48,7 @@
     scale = 1.0 / math.sqrt(HEAD_DIM)
     log_scale = scale * math.log2(math.e)
     d = HEAD_DIM
-    wide = info[1] > 0
+    wide = info[1] > 1
 
     def load(s):
         base, n = parts[s]
@@ -62,14 +62,16 @@
     head = pl.program_id(0)
     pair = 2 * d
 
-    def wide_part(array, k, column):
-        here = kv.at[pl.ds(plain, n_blocks - plain), pl.ds(k * chunk, chunk), :]
-        return here, array.at[:, :, pl.ds(pl.multiple_of(column * pair, pair), pair)]
+    def wide_part(array, first, k, column):
+        more = n_blocks - plain
+        here = kv.at[pl.ds(plain, more), pl.ds(k * chunk, chunk), :]
+        there = array.at[pl.ds(first, more), :, pl.ds(pl.multiple_of(column * pair, pair), pair)]
+        return here, there
 
     @pl.when(wide)
     def _():
         for k in range(n_sub):
-            here, there = wide_part(kv_refs[-1][k], k, wide_column + head)
+            here, there = wide_part(kv_refs[-1][k], 1, k, wide_column + head)
             pltpu.sync_copy(there, here)
 
     dkv[:plain] = jnp.zeros_like(dkv[:plain])
@@ -96,8 +98,9 @@
 
     for r in range(CORES):
         for h in range(group):
-            q_all[r, pl.ds(h * chunk, chunk), :] = q_refs[r][:, h * d : (h + 1) * d]
-            g_all[r, pl.ds(h * chunk, chunk), :] = g_refs[r][:, h * d : (h + 1) * d]
+            here, columns = pl.ds(h * chunk, chunk), slice(h * d, (h + 1) * d)
+            q_all[r, here, :] = other[0, :, columns] if r else q_mine[:, columns]
+            g_all[r, here, :] = other[1, :, columns] if r else g_mine[:, columns]
 
     def one_chunk(r, carry):
         m_buf[...] = jnp.full_like(m_buf, NEG)
@@ -163,8 +166,13 @@
     lax.fori_loop(0, CORES, one_chunk, 0)
     for r in range(CORES):
         for h in range(group):
-            o_refs[r][:, h * d : (h + 1) * d] = o_all[r, pl.ds(h * chunk, chunk), :]
-            dq_refs[r][:, h * d : (h + 1) * d] = dq_all[r, pl.ds(h * chunk, chunk), :]
+            here, columns = pl.ds(h * chunk, chunk), slice(h * d, (h + 1) * d)
+            if r:
+                other_out[0, :, columns] = o_all[r, here, :]
+                other_out[1, :, columns] = dq_all[r, here, :]
+            else:
+                o_mine[:, columns] = o_all[r, here, :]
+                dq_mine[:, columns] = dq_all[r, here, :]
 
     def store(s, base, n):
         for b in range(n):
@@ -181,47 +189,46 @@
         kv[plain:, :, :d] = (dkv[plain:, :, :d] * scale).astype(BF16)
         kv[plain:, :, d:] = dkv[plain:, :, d:].astype(BF16)
         for k in range(n_sub):
-            here, there = wide_part(dkv_refs[-1][k], k, head)
+            here, there = wide_part(dkv_refs[-1][k], 0, k, head)
             pltpu.sync_copy(here, there)
 
 
 def attention(call, info, kinfo, rinfo, mine, other, kv_sets, outs, group, heads):
     chunk = mine[0].shape[0]
     n_sub = len(kv_sets[0][1])
-    all_heads = other[0].shape[1] // (group * HEAD_DIM)
+    all_heads = other.shape[2] // (group * HEAD_DIM)
     rows = group * chunk
     width = group * HEAD_DIM
     parts, n_blocks = [], 0
-    for _, arrays in kv_sets:
-        parts.append((n_blocks, arrays[0].shape[0]))
-        n_blocks += arrays[0].shape[0]
+    for n in [a[0].shape[0] for _, a in kv_sets[:-1]] + [1, WIDE - 1]:
+        parts.append((n_blocks, n))
+        n_blocks += n
     parts = tuple(parts)
     first = call * heads
     whole = lambda shape: pl.BlockSpec(shape, lambda h, info: (0,) * len(shape))
     mine_spec = pl.BlockSpec((chunk, width), lambda h, info: (0, info[0] * all_heads + first + h))
-    other_spec = pl.BlockSpec((chunk, width), lambda h, info: (0, first + h))
+    other_spec = pl.BlockSpec((2, chunk, width), lambda h, info: (0, 0, first + h))
 
     def kv_spec(n, column):
         return pl.BlockSpec((n, chunk, 2 * HEAD_DIM), lambda h, info: (0, 0, column + h))
 
     anywhere = pl.BlockSpec(memory_space=pl.ANY)
 
-    in_specs = [whole(kinfo.shape), whole(rinfo.shape)] + [mine_spec, other_spec] * 2
-    operands = [kinfo, rinfo, mine[0], other[0], mine[1], other[1]]
-    for (column, arrays), (_, n) in zip(kv_sets[:-1], parts):
+    in_specs = [whole(kinfo.shape), whole(rinfo.shape), mine_spec, mine_spec, other_spec]
+    operands = [kinfo, rinfo, *mine, other]
+    for (column, arrays), (_, n) in zip(kv_sets, parts):
         in_specs += [kv_spec(n, column)] * n_sub
         operands += arrays
     in_specs += [anywhere] * n_sub
     operands += kv_sets[-1][1]
     aliases = {}
     if call:
-        aliases = {1 + len(operands) + i: i for i in range(4)}
-        in_specs += [anywhere] * 4
+        aliases = {1 + len(operands) + i: i for i in range(3)}
+        in_specs += [anywhere] * 3
         operands += list(outs)
     full = jax.ShapeDtypeStruct(mine[0].shape, BF16)
-    part = jax.ShapeDtypeStruct(other[0].shape, BF16)
-    out_shape = [full, part, full, part]
-    out_specs = [mine_spec, other_spec, mine_spec, other_spec]
+    out_shape = [full, full, jax.ShapeDtypeStruct(other.shape, BF16)]
+    out_specs = [mine_spec, mine_spec, other_spec]
     for s, (_, n) in enumerate(parts):
         out_shape += [jax.ShapeDtypeStruct((n, chunk, heads * 2 * HEAD_DIM), BF16)] * n_sub
         out_specs += [kv_spec(n, 0) if s < len(parts) - 1 else anywhere] * n_sub
@@ -257,8 +264,8 @@
         ),
         name=f"attention_{call}",
     )(info, *operands)
-    grads = [results[4 + n_sub * i : 4 + n_sub * (i + 1)] for i in range(len(parts))]
-    return results[:4], grads
+    grads = [results[3 + n_sub * i : 3 + n_sub * (i + 1)] for i in range(len(parts))]
+    return results[:3], grads
 
 
 def blank(shape):
@@ -318,34 +325,55 @@
 
     kv_mine = columns(c)
     kv_other = swap_cores(columns(1 - c))
-    kv_both = [
-        jnp.stack([a[:, i * call_width : (i + 1) * call_width] for a in (kv_mine, kv_other)])
-        for i in range(SPLIT)
-    ]
-    q_send, g_send, _ = lax.optimization_barrier(
-        (half_of(query_rows, 1 - c), half_of(out_grad, 1 - c), kv_other)
-    )
-    q_other = swap_cores(q_send)
-    g_other = swap_cores(g_send)
-    segment_ids, _ = lax.optimization_barrier((segment_ids, kv_other))
+    kv_pair = jnp.stack([kv_mine, kv_other])
+    kv_both = [kv_pair[:, :, i * call_width : (i + 1) * call_width] for i in range(SPLIT)]
+    other = swap_cores(jnp.stack([half_of(query_rows, 1 - c), half_of(out_grad, 1 - c)]))
     ids = lax.all_to_all(
         jnp.broadcast_to(segment_ids[None], (devices, chunk)), ALL, split_axis=0, concat_axis=0, tiled=True
     )
     n0 = jnp.sum((ids == 0).astype(jnp.int32))
-    wide = n0 > BLOCK
-
-    prompt = jnp.where(c == 0, kv_mine, kv_other)[None]
-    step = halves // 2
-    while step:
-        got = lax.ppermute(prompt, ("z", "y"), [(i, i + step) for i in range(0, halves, 2 * step)])
-        if step == halves // 2:
-            got, q_other, g_other = lax.optimization_barrier((got, q_other, g_other))
-        prompt = jnp.where(half % (2 * step) == step, got, prompt)
-        step //= 2
-    prompt_set = spread(prompt)
-
-    def fetch_wide(_):
-        moved = jnp.concatenate(kv_both, axis=2)
+    level = (n0 > BLOCK).astype(jnp.int32) + (n0 > 2 * BLOCK).astype(jnp.int32)
+    count = jnp.left_shift(1, level)
+
+    routes = [(by, k) for by in range(3) for k in range(n_sub)]
+
+    def send_bands(a):
+        sent = [send(a, *to) if any(to) else a for to in routes]
+        return [sent[n_sub * by : n_sub * (by + 1)] for by in range(3)]
+
+    def after(moved, sent, stage, stages):
+        flat, tree_of = jax.tree.flatten(sent)
+        part = len(flat) * stage // stages
+        moved, flat[:part] = lax.optimization_barrier((moved, flat[:part]))
+        return moved, jax.tree.unflatten(tree_of, flat)
+
+    def return_bands(grads):
+        return [send(grads[by][k], -by, -k) if by or k else grads[by][k] for by, k in routes]
+
+    in_order = jnp.where(c == 0, kv_pair, kv_pair[::-1])
+
+    def padded(arrays):
+        room = blank((WIDE, chunk, SPLIT * call_width))
+        return tuple(lax.dynamic_update_slice(room, a, (0, 0, 0)) for a in arrays)
+
+    def fetch(blocks):
+        def run(pair, band):
+            moved = pair[:blocks]
+            bands = send_bands(band)
+            step, stages = halves // 2, halves.bit_length() - 1
+            stage = 0
+            while step:
+                got = lax.ppermute(moved, ("z", "y"), [(i, i + step) for i in range(0, halves, 2 * step)])
+                moved = jnp.where(half % (2 * step) == step, got, moved)
+                step //= 2
+                stage += 1
+                moved, bands = after(moved, bands, stage, stages)
+            return padded(spread(moved)), bands
+
+        return run
+
+    def fetch_all(moved, band):
+        bands = send_bands(band)
         step = planes // 2
         while step:
             got = lax.ppermute(moved, "z", [(i, i + step) for i in range(0, planes, 2 * step)])
@@ -353,18 +381,17 @@
             step //= 2
         across = lax.ppermute(moved, "y", [(0, 1), (1, 0)])
         moved = jnp.concatenate([jnp.where(y == 0, moved, across), jnp.where(y == 0, across, moved)])
-        return tuple(spread(moved))
-
-    def no_wide(_):
-        return tuple(blank((WIDE, chunk, SPLIT * call_width)) for _ in range(n_sub))
-
-    wide_set = lax.cond(wide, fetch_wide, no_wide, 0)
-
-    bands = []
-    for a in kv_both:
-        if bands:
-            a, _ = lax.optimization_barrier((a, bands[-1]))
-        bands.append([[send(a, by, k) if by or k else a for k in range(n_sub)] for by in range(3)])
+        return tuple(spread(moved)), bands
+
+    in_order, other = lax.optimization_barrier((in_order, other))
+    prompt_set, first_bands = lax.switch(
+        level, [fetch(1), fetch(2), fetch_all], in_order, kv_both[0]
+    )
+    bands = [first_bands]
+
+    for a in kv_both[1:]:
+        a, _, prompt_set = lax.optimization_barrier((a, bands[-1], prompt_set))
+        bands.append(send_bands(a))
 
     row_chunk = jnp.stack([(2 * half + (c ^ r)) * n_sub + x for r in range(CORES)])
     row_pos = row_chunk[:, None] * chunk + jnp.arange(chunk, dtype=jnp.int32)
@@ -374,12 +401,10 @@
     sub = (x - jnp.arange(n_sub, dtype=jnp.int32)) % n_sub
     block = jnp.stack(
         [2 * (half - s) + (c ^ k) for s in range(3) for k in range(CORES)]
-        + [jnp.zeros((), jnp.int32), c, 1 - c, 2 + c, 3 - c]
+        + [jnp.full((), j, jnp.int32) for j in range(WIDE)]
     )
     place = jnp.arange(block.shape[0])
-    usable = jnp.where(
-        place < 6, block >= jnp.where(wide, WIDE, 1), jnp.where(place == 6, ~wide, wide)
-    )
+    usable = jnp.where(place < 6, block >= count, place - 6 < count)
     key_chunk = jnp.clip(block, 0)[:, None] * n_sub + sub[None]
     key_seg = jnp.take(ids, key_chunk.reshape(-1), axis=0).reshape(-1, BLOCK)
     key_pos = (key_chunk[..., None] * chunk + jnp.arange(chunk, dtype=jnp.int32)).reshape(-1, BLOCK)
@@ -392,58 +417,74 @@
         & ((first[None] < n0) | (first[None] + BLOCK > starts[:, None]))
     )
     info = jnp.concatenate(
-        [jnp.stack([c, wide.astype(jnp.int32)]), need.astype(jnp.int32).reshape(-1)]
+        [jnp.stack([c, count]), need.astype(jnp.int32).reshape(-1)]
     )
 
     outs = None
     owns, prompts, wide_parts = [], [], []
     for i in range(SPLIT):
         column = heads * i
-        sets = [(0, b) for b in bands[i]] + [(column, prompt_set), (column, wide_set)]
+        sets = [(0, b) for b in bands[i]] + [(column, prompt_set)]
         outs, grads = attention(
-            i, info, kinfo, rinfo, (query_rows, out_grad), (q_other, g_other), sets, outs, group, heads
+            i, info, kinfo, rinfo, (query_rows, out_grad), other, sets, outs, group, heads
         )
         if owns:
             (outs, grads), owns[-1] = lax.optimization_barrier(((outs, grads), owns[-1]))
-        owns.append(
-            [send(grads[by][k], -by, -k) if by or k else grads[0][0] for by in range(3) for k in range(n_sub)]
-        )
-        prompts.append(grads[3])
+        if i < SPLIT - 1:
+            owns.append(return_bands(grads))
+        prompts.append(tuple(grads[3]))
         wide_parts.append(tuple(grads[4]))
 
-    back = gather_back([jnp.concatenate([p[k] for p in prompts], axis=2) for k in range(n_sub)])[0]
-    step = 1
-    while step < halves:
-        got = lax.ppermute(
-            back.astype(BF16), ("z", "y"), [(j + step, j) for j in range(0, halves, 2 * step)]
-        )
-        back = back + got.astype(F32)
-        step *= 2
-    mine = (jnp.arange(CORES) == c)[:, None, None] & (half == 0)
-    total = jnp.where(mine, back[None], 0.0) + jnp.concatenate(
-        [sum(a.astype(F32) for a in arrays) for arrays in owns], axis=2
-    )
-
-    def return_wide(parts):
-        total = gather_back([jnp.concatenate([p[k] for p in parts], axis=2) for k in range(n_sub)])
-        total = total.astype(BF16)
-        keep = jnp.where(y == 0, total[:2], total[2:])
-        send = jnp.where(y == 0, total[2:], total[:2])
-        back = keep.astype(F32) + lax.ppermute(send, "y", [(0, 1), (1, 0)]).astype(F32)
-        step = 1
-        while step < planes:
-            got = lax.ppermute(back.astype(BF16), "z", [(j + step, j) for j in range(0, planes, 2 * step)])
+    joined = lambda parts, k: jnp.concatenate([p[k] for p in parts], axis=2)
+
+    def tree(back, axes, length, beside):
+        step, stage, stages = 1, 1, length.bit_length()
+        while step < length:
+            back, beside = after(back, beside, stage, stages)
+            got = lax.ppermute(back.astype(BF16), axes, [(j + step, j) for j in range(0, length, 2 * step)])
             back = back + got.astype(F32)
             step *= 2
-        return jnp.where(z == 0, back, 0.0)
-
-    total = lax.cond(
-        wide,
-        lambda t, parts: t + return_wide(parts),
-        lambda t, parts: t,
-        total,
-        tuple(wide_parts),
-    ).astype(BF16)
+            stage += 1
+        return back, beside
+
+    def give_back(blocks):
+        def run(parts, band, rows):
+            own, arrived = return_bands(band), swap_cores(rows)
+            arrays = []
+            for k in range(n_sub):
+                a = joined(parts[0], k)
+                arrays.append(a if blocks == 1 else jnp.concatenate([a, joined(parts[1], k)[:1]]))
+            back, (own, arrived) = tree(gather_back(arrays), ("z", "y"), halves, (own, arrived))
+            if blocks == 1:
+                back = jnp.where((jnp.arange(CORES) == c)[:, None, None], back, 0.0)
+            else:
+                back = jnp.where(c == 0, back, back[::-1])
+            return jnp.where(half == 0, back, 0.0), own, arrived
+
+        return run
+
+    def give_all_back(parts, band, rows):
+        own, arrived = return_bands(band), swap_cores(rows)
+        back = gather_back(
+            [jnp.concatenate([joined(parts[0], k), joined(parts[1], k)]) for k in range(n_sub)]
+        ).astype(BF16)
+        keep = jnp.where(y == 0, back[:2], back[2:])
+        leave = jnp.where(y == 0, back[2:], back[:2])
+        back = keep.astype(F32) + lax.ppermute(leave, "y", [(0, 1), (1, 0)]).astype(F32)
+        back, (own, arrived) = tree(back, "z", planes, (own, arrived))
+        back = jnp.where(c == 0, back, back[::-1])
+        return jnp.where(z == 0, back, 0.0), own, arrived
+
+    back, last_own, arrived = lax.switch(
+        level,
+        [give_back(1), give_back(2), give_all_back],
+        (tuple(prompts), tuple(wide_parts)),
+        grads[:3],
+        outs[2],
+    )
+    owns.append(last_own)
+    total = back + jnp.concatenate([sum(a.astype(F32) for a in arrays) for arrays in owns], axis=2)
+    total = total.astype(BF16)
 
     got = swap_cores(total[1])
     low = jnp.where(c == 0, total[0], got)
@@ -454,10 +495,9 @@
         return jnp.concatenate([a[:, s : s + HEAD_DIM] for a in (low, high) for s in starts], axis=1)
 
     def join(full, part):
-        start = (1 - c) * part.shape[1]
-        return lax.dynamic_update_slice(full, swap_cores(part), (0, start))
-
-    return join(outs[0], outs[1]), join(outs[2], outs[3]), columns_back(0), columns_back(1)
+        return lax.dynamic_update_slice(full, part, (0, (1 - c) * part.shape[1]))
+
+    return join(outs[0], arrived[0]), join(outs[1], arrived[1]), columns_back(0), columns_back(1)
 
 
 def solution(mesh):

time: 225 us -> 231 us (1.027); the launches traced: 227 us -> 231 us
  local copies, waits for them, and re-layouts: 21.7 us -> 26.6 us
  other arithmetic: 10.9 us -> 8.57 us
    ppermute x20, waiting for transfers between devices: 9.87 us -> 35.5 us  [send(): return lax.ppermute(a, ('z', 'y', 'x'), moves)]
    ppermute x6, waiting for transfers between devices: 68.4 us -> 46.9 us  [the longest x3 42.6 us: tree(): lax.ppermute(back.astype(BF16), axes, [(j + step, j) for j in range(0, le...]
    all_to_all x1, waiting for transfers between devices: 5.79 us -> 0.01 us  [per_device(): lax.all_to_all(jnp.broadcast_to(segment_ids[None], (devices, chunk)), ALL...]
    all_to_all x1, starting transfers between devices: 2.54 us -> 7.3 us  [per_device(): lax.all_to_all(jnp.broadcast_to(segment_ids[None], (devices, chunk)), ALL...]
    ppermute x6, starting transfers between devices: 18.7 us -> 14.3 us  [the longest x3 10.4 us: run(): lax.ppermute(moved, ('z', 'y'), [(i, i + step) for i in range(0, halves,...]
    ppermute x2, waiting for transfers between devices: 5.5 us -> 9.41 us  [rotate(): return lax.ppermute(a, 'x', [(i, (i + by) % n_sub) for i in range(n_sub)])]
    unnamed x61 -> x69, local copies, waits for them, and re-layouts: 9.84 us -> 12.5 us
    add x2, other arithmetic: 1.35 us -> 3.84 us  [per_device(): sum((a.astype(F32) for a in arrays))]
  transfers between devices with their start and end apart: 35 -> 33, of which waited for: 11 -> 15; matrix products, arithmetic and copies ran while one was open for 8% -> 10% of each run, Pallas kernels for 15% -> 15%
where the time goes in v2:
time: 231 us
  waiting for transfers between devices  91.7 us (40%)
  starting transfers between devices  66.8 us (29%)
  Pallas kernels  34 us (15%)
  local copies, waits for them, and re-layouts  26.6 us (12%)
  other arithmetic  8.57 us (4%)
  between operations  2.55 us (1%)
    ppermute x20, starting transfers between devices, send(): return lax.ppermute(a, ('z', 'y', 'x'), moves)  43.5 us
    ppermute x3, waiting for transfers between devices, tree(): lax.ppermute(back.astype(BF16), axes, [(j + step, j) for j in range(0, le...  42.6 us
    ppermute x20, waiting for transfers between devices, send(): return lax.ppermute(a, ('z', 'y', 'x'), moves)  35.5 us
    pallas_call x2, Pallas kernels, attention(): pl.pallas_call(functools.partial(attention_kernel, n_sub, chunk, group, n...  34 us
    unnamed x69, local copies, waits for them, and re-layouts  12.5 us
    ppermute x3, starting transfers between devices, run(): lax.ppermute(moved, ('z', 'y'), [(i, i + step) for i in range(0, halves,...  10.4 us
    ppermute x2, waiting for transfers between devices, rotate(): return lax.ppermute(a, 'x', [(i, (i + by) % n_sub) for i in range(n_sub)])  9.41 us
    all_to_all x1, starting transfers between devices, per_device(): lax.all_to_all(jnp.broadcast_to(segment_ids[None], (devices, chunk)), ALL...  7.3 us
  transfers between devices with their start and end apart: 33, of which 15 were waited for; matrix products, arithmetic and copies ran while one was open for 10% of the time, Pallas kernels for 15%

profile of v2, /device:TPU:0, one launch (start us, length us, event | category | flops | bytes accessed | tf_op | source)
XLA Modules:
  0.0 230.6 jit_solution(16463831493805627616)
XLA Ops:
  1.9 7.3 %all-to-all-start = ((s32[32,1,128]{2,1,0:T(1,128)}), s32[32,1,128]{2,1,0:T(1,128)S(1)}, u32[]{:S(2)}, u32[]{:S(2)}) async-start(s32[32,1,128]{2,1,0:T(1,128)} %broadcast_in_dim.95), calls=%async_computation | async-start | bytes 32768 | tf_op jit(solution)/shard_map/all_to_all | solution.py:331
  17.5 1.7 dynamic-slice_bitcast_fusion
  25.4 2.3 copy.29.refs_1_
  29.1 52.0 %conditional.4 = (bf16[4,128,1024]{2,1,0:T(8,128)(2,1)}, bf16[4,128,1024]{2,1,0:T(8,128)(2,1)}, bf16[2,128,512]{2,1,0:T(8,128)(2,1)S(1)}, bf16[2,128,512]{2,1,0:...) conditional(s32[]{:T(128)} %clamp.4, (s32[]{:T(128)}, ...), branch_computations={%region_2.3_spmd, %region_3.4_spmd, %region_4.5_spmd} | conditional | flops 1572886 | bytes 23069314 | solution.py:387
  29.1 4.6 %collective-permute-start = (bf16[1,128,1024]{2,1,0:T(8,128)(2,1)S(1)}, bf16[1,128,1024]{2,1,0:T(8,128)(2,1)S(1)}, u32[]{:S(2)}, u32[]{:S(2)}) collective-permute-start(bf16[1,128,1024]{2,1,0:T(8,128)(2,1)S(1)} %slice.103), channel_id=1, source_target_pairs={{0,16},{1,17},{2,18},{3,19}} | collective-permute-start | bytes 786440 | tf_op jit(solution)/shard_map/cond/branch_0_fun/ppermute | solution.py:366
  35.2 4.3 %collective-permute-done = bf16[1,128,1024]{2,1,0:T(8,128)(2,1)S(1)} collective-permute-done((bf16[1,128,1024]{2,1,0:T(8,128)(2,1)S(1)}, bf16[1,128,1024]{2,1,0:T(8,128)(2,1)S(1)}, u32[]{:S(2)}, u32[]{:S(2)}) %collective-permute-start) | collective-permute-done | bytes 262176 | tf_op jit(solution)/shard_map/cond/branch_0_fun/ppermute | solution.py:366
  39.5 2.4 %collective-permute-done.1 = bf16[2,128,512]{2,1,0:T(8,128)(2,1)} collective-permute-done((bf16[2,128,512]{2,1,0:T(8,128)(2,1)S(1)}, bf16[2,128,512]{2,1,0:T(8,128)(2,1)}, u32[]{:S(2)}, u32[]{:S(2)}) %collective-permute-start.1) | collective-permute-done | bytes 262176 | tf_op jit(solution)/shard_map/cond/branch_0_fun/ppermute | solution.py:309
  43.2 2.0 collective-permute-start.4
  45.2 3.0 %collective-permute-start.3 = (bf16[2,128,512]{2,1,0:T(8,128)(2,1)S(1)}, bf16[2,128,512]{2,1,0:T(8,128)(2,1)}, u32[]{:S(2)}, u32[]{:S(2)}) collective-permute-start(bf16[2,128,512]{2,1,0:T(8,128)(2,1)S(1)} %get-tuple-element.473), channel_id=1, source_target_pairs={{0,4},{1,5},{4,8},{5,9},{8,12},{9,13},{12,16},{13,17},{16,20},{17,... | collective-permute-start | bytes 786440 | tf_op jit(solution)/shard_map/cond/branch_0_fun/ppermute | solution.py:309
  49.5 6.5 %collective-permute-done.3 = bf16[2,128,512]{2,1,0:T(8,128)(2,1)} collective-permute-done((bf16[2,128,512]{2,1,0:T(8,128)(2,1)S(1)}, bf16[2,128,512]{2,1,0:T(8,128)(2,1)}, u32[]{:S(2)}, u32[]{:S(2)}) %collective-permute-start.3) | collective-permute-done | bytes 262176 | tf_op jit(solution)/shard_map/cond/branch_0_fun/ppermute | solution.py:309
  56.0 4.5 %collective-permute-start.5 = (bf16[1,128,1024]{2,1,0:T(8,128)(2,1)S(1)}, bf16[1,128,1024]{2,1,0:T(8,128)(2,1)S(1)}, u32[]{:S(2)}, u32[]{:S(2)}) collective-permute-start(bf16[1,128,1024]{2,1,0:T(8,128)(2,1)S(1)} %broadcast_select_fusion.1), channel_id=1, source_target_pairs={{0,4},{8,12},{16,20},{24,28},{1,5},{9,13},{17,21},{25,29},{2,6},{1... | collective-permute-start | bytes 786440 | tf_op jit(solution)/shard_map/cond/branch_0_fun/ppermute | solution.py:366
  60.5 4.6 %collective-permute-start.7 = (bf16[2,128,512]{2,1,0:T(8,128)(2,1)S(1)}, bf16[2,128,512]{2,1,0:T(8,128)(2,1)}, u32[]{:S(2)}, u32[]{:S(2)}) collective-permute-start(bf16[2,128,512]{2,1,0:T(8,128)(2,1)S(1)} %get-tuple-element.473), channel_id=1, source_target_pairs={{0,9},{1,8},{4,13},{5,12},{8,17},{9,16},{12,21},{13,20},{16,25},{1... | collective-permute-start | bytes 786440 | tf_op jit(solution)/shard_map/cond/branch_0_fun/ppermute | solution.py:309
  65.1 3.4 %collective-permute-start.6 = (bf16[2,128,512]{2,1,0:T(8,128)(2,1)S(1)}, bf16[2,128,512]{2,1,0:T(8,128)(2,1)}, u32[]{:S(2)}, u32[]{:S(2)}) collective-permute-start(bf16[2,128,512]{2,1,0:T(8,128)(2,1)S(1)} %get-tuple-element.473), channel_id=1, source_target_pairs={{0,8},{1,9},{4,12},{5,13},{8,16},{9,17},{12,20},{13,21},{16,24},{1... | collective-permute-start | bytes 786440 | tf_op jit(solution)/shard_map/cond/branch_0_fun/ppermute | solution.py:309
  70.1 3.8 %collective-permute-done.6 = bf16[2,128,512]{2,1,0:T(8,128)(2,1)} collective-permute-done((bf16[2,128,512]{2,1,0:T(8,128)(2,1)S(1)}, bf16[2,128,512]{2,1,0:T(8,128)(2,1)}, u32[]{:S(2)}, u32[]{:S(2)}) %collective-permute-start.6) | collective-permute-done | bytes 262176 | tf_op jit(solution)/shard_map/cond/branch_0_fun/ppermute | solution.py:309
  74.5 2.3 copy.33
  77.5 2.9 %collective-permute-done.8 = bf16[1,128,1024]{2,1,0:T(8,128)(2,1)S(1)} collective-permute-done((bf16[1,128,1024]{2,1,0:T(8,128)(2,1)S(1)}, bf16[1,128,1024]{2,1,0:T(8,128)(2,1)S(1)}, u32[]{:S(2)}, u32[]{:S(2)}) %collective-permute-start.8) | collective-permute-done | bytes 262176 | tf_op jit(solution)/shard_map/cond/branch_0_fun/ppermute | solution.py:297
  81.1 5.5 %collective-permute-start.63 = (bf16[2,128,512]{2,1,0:T(8,128)(2,1)S(1)}, bf16[2,128,512]{2,1,0:T(8,128)(2,1)S(1)}, u32[]{:S(2)}, u32[]{:S(2)}) collective-permute-start(bf16[2,128,512]{2,1,0:T(8,128)(2,1)S(1)} %get-tuple-element.349.refs_6_), channel_id=1, source_target_pairs={{0,9},{1,8},{4,13},{5,12},{8,17},{9,16},{12,21},{13,20},{16,25},{1... | collective-permute-start | bytes 786440 | tf_op jit(solution)/shard_map/ppermute | solution.py:309
  86.6 4.5 %collective-permute-start.62 = (bf16[2,128,512]{2,1,0:T(8,128)(2,1)S(1)}, bf16[2,128,512]{2,1,0:T(8,128)(2,1)S(1)}, u32[]{:S(2)}, u32[]{:S(2)}) collective-permute-start(bf16[2,128,512]{2,1,0:T(8,128)(2,1)S(1)} %get-tuple-element.349.refs_6_), channel_id=1, source_target_pairs={{0,8},{1,9},{4,12},{5,13},{8,16},{9,17},{12,20},{13,21},{16,24},{1... | collective-permute-start | bytes 786440 | tf_op jit(solution)/shard_map/ppermute | solution.py:309
  91.1 1.9 collective-permute-start.61
  93.1 4.4 %collective-permute-start.60 = (bf16[2,128,512]{2,1,0:T(8,128)(2,1)S(1)}, bf16[2,128,512]{2,1,0:T(8,128)(2,1)S(1)}, u32[]{:S(2)}, u32[]{:S(2)}) collective-permute-start(bf16[2,128,512]{2,1,0:T(8,128)(2,1)S(1)} %get-tuple-element.349.refs_6_), channel_id=1, source_target_pairs={{0,4},{1,5},{4,8},{5,9},{8,12},{9,13},{12,16},{13,17},{16,20},{17,... | collective-permute-start | bytes 786440 | tf_op jit(solution)/shard_map/ppermute | solution.py:309
  98.1 16.8 %attention_0.1 = (bf16[128,8192]{1,0:T(8,128)(2,1)}, bf16[128,8192]{1,0:T(8,128)(2,1)}, bf16[2,128,4096]{2,1,0:T(8,128)(2,1)}, bf16[2,128,512]{2,1,0:T(8,128)(2,...) custom-call(s32[22]{0:T(128)} %pad_add_fusion.2.refs_0_, ...), custom_call_target="tpu_custom_call" | custom-call | flops 8053063680 | bytes 8388608 | tf_op jit(solution)/shard_map/attention_0/pallas_call | solution.py:236
  121.9 17.2 %attention_1.1 = (bf16[128,8192]{1,0:T(8,128)(2,1)}, bf16[128,8192]{1,0:T(8,128)(2,1)}, bf16[2,128,4096]{2,1,0:T(8,128)(2,1)}, bf16[2,128,512]{2,1,0:T(8,128)(2,...) custom-call(s32[22]{0:T(128)} %pad_add_fusion.2.refs_0_, ...), custom_call_target="tpu_custom_call", output_to_operand_aliasing={{0}: (16, {}), {1}: (17, {}), {2}: (18, {})} | custom-call | flops 8053063680 | bytes 8388608 | tf_op jit(solution)/shard_map/attention_1/pallas_call | solution.py:236
  139.2 7.4 %collective-permute-done.67 = bf16[2,128,512]{2,1,0:T(8,128)(2,1)S(1)} collective-permute-done((bf16[2,128,512]{2,1,0:T(8,128)(2,1)}, bf16[2,128,512]{2,1,0:T(8,128)(2,1)S(1)}, u32[]{:S(2)}, u32[]{:S(2)}) %collective-permute-start.67) | collective-permute-done | bytes 262176 | tf_op jit(solution)/shard_map/ppermute | solution.py:309
  146.6 4.1 %collective-permute-done.68 = bf16[2,128,512]{2,1,0:T(8,128)(2,1)S(1)} collective-permute-done((bf16[2,128,512]{2,1,0:T(8,128)(2,1)}, bf16[2,128,512]{2,1,0:T(8,128)(2,1)S(1)}, u32[]{:S(2)}, u32[]{:S(2)}) %collective-permute-start.68) | collective-permute-done | bytes 262176 | tf_op jit(solution)/shard_map/ppermute | solution.py:309
  151.4 71.1 %conditional.6 = (f32[2,128,1024]{2,1,0:T(8,128)S(1)}, bf16[2,128,512]{2,1,0:T(8,128)(2,1)}, bf16[2,128,512]{2,1,0:T(8,128)(2,1)}, bf16[2,128,512]{2,1,0:T(8,128...) conditional(s32[]{:T(128)} %clamp.4, (s32[]{:T(128)}, ...), branch_computations={%region_5.6_spmd, %region_6.7_spmd, %region_7.8_spmd} | conditional | flops 13369347 | bytes 73401072
  151.8 6.6 %collective-permute-done.27 = bf16[1,128,1024]{2,1,0:T(8,128)(2,1)S(1)} collective-permute-done((bf16[1,128,1024]{2,1,0:T(8,128)(2,1)S(1)}, bf16[1,128,1024]{2,1,0:T(8,128)(2,1)S(1)}, u32[]{:S(2)}, u32[]{:S(2)}) %collective-permute-start.27) | collective-permute-done | bytes 262176 | tf_op jit(solution)/shard_map/cond/branch_0_fun/ppermute | solution.py:297
  161.1 12.6 %collective-permute-done.28 = bf16[1,128,1024]{2,1,0:T(8,128)(2,1)S(1)} collective-permute-done((bf16[1,128,1024]{2,1,0:T(8,128)(2,1)S(1)}, bf16[1,128,1024]{2,1,0:T(8,128)(2,1)S(1)}, u32[]{:S(2)}, u32[]{:S(2)}) %collective-permute-start.28) | collective-permute-done | bytes 262176 | tf_op jit(solution)/shard_map/cond/branch_0_fun/ppermute | solution.py:444
  173.8 2.8 %collective-permute-done.30 = bf16[2,128,512]{2,1,0:T(8,128)(2,1)} collective-permute-done((bf16[2,128,512]{2,1,0:T(8,128)(2,1)}, bf16[2,128,512]{2,1,0:T(8,128)(2,1)}, u32[]{:S(2)}, u32[]{:S(2)}) %collective-permute-start.30) | collective-permute-done | bytes 262176 | tf_op jit(solution)/shard_map/cond/branch_0_fun/ppermute | solution.py:309
  180.5 11.8 %collective-permute-done.31 = bf16[1,128,1024]{2,1,0:T(8,128)(2,1)S(1)} collective-permute-done((bf16[1,128,1024]{2,1,0:T(8,128)(2,1)S(1)}, bf16[1,128,1024]{2,1,0:T(8,128)(2,1)S(1)}, u32[]{:S(2)}, u32[]{:S(2)}) %collective-permute-start.31) | collective-permute-done | bytes 262176 | tf_op jit(solution)/shard_map/cond/branch_0_fun/ppermute | solution.py:444
  192.5 5.6 %collective-permute-done.33 = bf16[2,128,512]{2,1,0:T(8,128)(2,1)} collective-permute-done((bf16[2,128,512]{2,1,0:T(8,128)(2,1)}, bf16[2,128,512]{2,1,0:T(8,128)(2,1)}, u32[]{:S(2)}, u32[]{:S(2)}) %collective-permute-start.33) | collective-permute-done | bytes 262176 | tf_op jit(solution)/shard_map/cond/branch_0_fun/ppermute | solution.py:309
  200.8 18.2 %collective-permute-done.34 = bf16[1,128,1024]{2,1,0:T(8,128)(2,1)S(1)} collective-permute-done((bf16[1,128,1024]{2,1,0:T(8,128)(2,1)S(1)}, bf16[1,128,1024]{2,1,0:T(8,128)(2,1)S(1)}, u32[]{:S(2)}, u32[]{:S(2)}) %collective-permute-start.34) | collective-permute-done | bytes 262176 | tf_op jit(solution)/shard_map/cond/branch_0_fun/ppermute | solution.py:444
  222.5 2.3 %convert_add_fusion.11 = f32[2,128,512]{2,1,0:T(8,128)S(1)} fusion(bf16[2,128,512]{2,1,0:T(8,128)(2,1)} %copy-done.20, bf16[2,128,512]{2,1,0:T(8,128)(2,1)} %copy-done.19, bf16[2,128,512]{2,1,0:T(8,128)(2,1)} %copy-done.18, bf16[2,128,512]{2,1,0:T(8,128)(2,1)} %copy-done.17, bf16[2,128,512]{2,1,0:T(8,128)(2,1)} %copy-done.16, ...), kind=kLoop, calls=%fused_computation.54 | loop fusion | flops 1441792 | bytes 2097152 | tf_op jit(solution)/shard_map/add | solution.py:486
  (180 shorter events, 50.7 us)
Async XLA Ops:
  1.9 19.0 %all-to-all-start = ((s32[32,1,128]{2,1,0:T(1,128)}), s32[32,1,128]{2,1,0:T(1,128)S(1)}, u32[]{:S(2)}, u32[]{:S(2)}) async-start(s32[32,1,128]{2,1,0:T(1,128)} %broadcast_in_dim.95), calls=%async_computation | async-start | bytes 32768 | tf_op jit(solution)/shard_map/all_to_all | solution.py:331
  17.2 11.6 %collective-permute-start.57 = (bf16[128,1024]{1,0:T(8,128)(2,1)S(1)}, bf16[128,1024]{1,0:T(8,128)(2,1)S(1)}, u32[]{:S(2)}, u32[]{:S(2)}) collective-permute-start(bf16[128,1024]{1,0:T(8,128)(2,1)S(1)} %constant_dynamic-update-slice_fusion.12), channel_id=1, source_target_pairs={{0,2},{2,0},{1,3},{3,1},{4,6},{6,4},{5,7},{7,5},{8,10},{10,8},{9,1... | collective-permute-start | bytes 786440 | tf_op jit(solution)/shard_map/ppermute | solution.py:294
  19.4 9.7 %collective-permute-start.58 = (bf16[2,128,4096]{2,1,0:T(8,128)(2,1)S(1)}, bf16[2,128,4096]{2,1,0:T(8,128)(2,1)}, u32[]{:S(2)}, u32[]{:S(2)}) collective-permute-start(bf16[2,128,4096]{2,1,0:T(8,128)(2,1)S(1)} %pad_maximum_fusion.4), channel_id=1, source_target_pairs={{0,2},{2,0},{1,3},{3,1},{4,6},{6,4},{5,7},{7,5},{8,10},{10,8},{9,1... | collective-permute-start | bytes 6291464 | tf_op jit(solution)/shard_map/ppermute | solution.py:294
  29.1 10.4 %collective-permute-start = (bf16[1,128,1024]{2,1,0:T(8,128)(2,1)S(1)}, bf16[1,128,1024]{2,1,0:T(8,128)(2,1)S(1)}, u32[]{:S(2)}, u32[]{:S(2)}) collective-permute-start(bf16[1,128,1024]{2,1,0:T(8,128)(2,1)S(1)} %slice.103), channel_id=1, source_target_pairs={{0,16},{1,17},{2,18},{3,19}} | collective-permute-start | bytes 786440 | tf_op jit(solution)/shard_map/cond/branch_0_fun/ppermute | solution.py:366
  33.7 8.2 %collective-permute-start.1 = (bf16[2,128,512]{2,1,0:T(8,128)(2,1)S(1)}, bf16[2,128,512]{2,1,0:T(8,128)(2,1)}, u32[]{:S(2)}, u32[]{:S(2)}) collective-permute-start(bf16[2,128,512]{2,1,0:T(8,128)(2,1)S(1)} %get-tuple-element.473), channel_id=1, source_target_pairs={{0,1},{1,0},{4,5},{5,4},{8,9},{9,8},{12,13},{13,12},{16,17},{17,16... | collective-permute-start | bytes 786440 | tf_op jit(solution)/shard_map/cond/branch_0_fun/ppermute | solution.py:309
  41.9 6.3 %collective-permute-start.2 = (bf16[1,128,1024]{2,1,0:T(8,128)(2,1)S(1)}, bf16[1,128,1024]{2,1,0:T(8,128)(2,1)S(1)}, u32[]{:S(2)}, u32[]{:S(2)}) collective-permute-start(bf16[1,128,1024]{2,1,0:T(8,128)(2,1)S(1)} %broadcast_select_fusion), channel_id=1, source_target_pairs={{0,8},{16,24},{1,9},{17,25},{2,10},{18,26},{3,11},{19,27}} | collective-permute-start | bytes 786440 | tf_op jit(solution)/shard_map/cond/branch_0_fun/ppermute | solution.py:366
  43.2 6.3 %collective-permute-start.4 = (bf16[2,128,512]{2,1,0:T(8,128)(2,1)S(1)}, bf16[2,128,512]{2,1,0:T(8,128)(2,1)}, u32[]{:S(2)}, u32[]{:S(2)}) collective-permute-start(bf16[2,128,512]{2,1,0:T(8,128)(2,1)S(1)} %get-tuple-element.473), channel_id=1, source_target_pairs={{0,5},{1,4},{4,9},{5,8},{8,13},{9,12},{12,17},{13,16},{16,21},{17,... | collective-permute-start | bytes 786440 | tf_op jit(solution)/shard_map/cond/branch_0_fun/ppermute | solution.py:309
  45.2 10.8 %collective-permute-start.3 = (bf16[2,128,512]{2,1,0:T(8,128)(2,1)S(1)}, bf16[2,128,512]{2,1,0:T(8,128)(2,1)}, u32[]{:S(2)}, u32[]{:S(2)}) collective-permute-start(bf16[2,128,512]{2,1,0:T(8,128)(2,1)S(1)} %get-tuple-element.473), channel_id=1, source_target_pairs={{0,4},{1,5},{4,8},{5,9},{8,12},{9,13},{12,16},{13,17},{16,20},{17,... | collective-permute-start | bytes 786440 | tf_op jit(solution)/shard_map/cond/branch_0_fun/ppermute | solution.py:309
  56.0 12.5 %collective-permute-start.5 = (bf16[1,128,1024]{2,1,0:T(8,128)(2,1)S(1)}, bf16[1,128,1024]{2,1,0:T(8,128)(2,1)S(1)}, u32[]{:S(2)}, u32[]{:S(2)}) collective-permute-start(bf16[1,128,1024]{2,1,0:T(8,128)(2,1)S(1)} %broadcast_select_fusion.1), channel_id=1, source_target_pairs={{0,4},{8,12},{16,20},{24,28},{1,5},{9,13},{17,21},{25,29},{2,6},{1... | collective-permute-start | bytes 786440 | tf_op jit(solution)/shard_map/cond/branch_0_fun/ppermute | solution.py:366
  60.5 9.6 %collective-permute-start.7 = (bf16[2,128,512]{2,1,0:T(8,128)(2,1)S(1)}, bf16[2,128,512]{2,1,0:T(8,128)(2,1)}, u32[]{:S(2)}, u32[]{:S(2)}) collective-permute-start(bf16[2,128,512]{2,1,0:T(8,128)(2,1)S(1)} %get-tuple-element.473), channel_id=1, source_target_pairs={{0,9},{1,8},{4,13},{5,12},{8,17},{9,16},{12,21},{13,20},{16,25},{1... | collective-permute-start | bytes 786440 | tf_op jit(solution)/shard_map/cond/branch_0_fun/ppermute | solution.py:309
  65.1 8.8 %collective-permute-start.6 = (bf16[2,128,512]{2,1,0:T(8,128)(2,1)S(1)}, bf16[2,128,512]{2,1,0:T(8,128)(2,1)}, u32[]{:S(2)}, u32[]{:S(2)}) collective-permute-start(bf16[2,128,512]{2,1,0:T(8,128)(2,1)S(1)} %get-tuple-element.473), channel_id=1, source_target_pairs={{0,8},{1,9},{4,12},{5,13},{8,16},{9,17},{12,20},{13,21},{16,24},{1... | collective-permute-start | bytes 786440 | tf_op jit(solution)/shard_map/cond/branch_0_fun/ppermute | solution.py:309
  73.9 6.5 %collective-permute-start.8 = (bf16[1,128,1024]{2,1,0:T(8,128)(2,1)S(1)}, bf16[1,128,1024]{2,1,0:T(8,128)(2,1)S(1)}, u32[]{:S(2)}, u32[]{:S(2)}) collective-permute-start(bf16[1,128,1024]{2,1,0:T(8,128)(2,1)S(1)} %broadcast_select_fusion.2), channel_id=1, source_target_pairs={{0,1},{1,0},{2,3},{3,2},{4,5},{5,4},{6,7},{7,6},{8,9},{9,8},{10,11... | collective-permute-start | bytes 786440 | tf_op jit(solution)/shard_map/cond/branch_0_fun/ppermute | solution.py:297
  81.1 33.8 %collective-permute-start.63 = (bf16[2,128,512]{2,1,0:T(8,128)(2,1)S(1)}, bf16[2,128,512]{2,1,0:T(8,128)(2,1)S(1)}, u32[]{:S(2)}, u32[]{:S(2)}) collective-permute-start(bf16[2,128,512]{2,1,0:T(8,128)(2,1)S(1)} %get-tuple-element.349.refs_6_), channel_id=1, source_target_pairs={{0,9},{1,8},{4,13},{5,12},{8,17},{9,16},{12,21},{13,20},{16,25},{1... | collective-permute-start | bytes 786440 | tf_op jit(solution)/shard_map/ppermute | solution.py:309
  86.6 29.8 %collective-permute-start.62 = (bf16[2,128,512]{2,1,0:T(8,128)(2,1)S(1)}, bf16[2,128,512]{2,1,0:T(8,128)(2,1)S(1)}, u32[]{:S(2)}, u32[]{:S(2)}) collective-permute-start(bf16[2,128,512]{2,1,0:T(8,128)(2,1)S(1)} %get-tuple-element.349.refs_6_), channel_id=1, source_target_pairs={{0,8},{1,9},{4,12},{5,13},{8,16},{9,17},{12,20},{13,21},{16,24},{1... | collective-permute-start | bytes 786440 | tf_op jit(solution)/shard_map/ppermute | solution.py:309
  91.1 26.6 %collective-permute-start.61 = (bf16[2,128,512]{2,1,0:T(8,128)(2,1)S(1)}, bf16[2,128,512]{2,1,0:T(8,128)(2,1)S(1)}, u32[]{:S(2)}, u32[]{:S(2)}) collective-permute-start(bf16[2,128,512]{2,1,0:T(8,128)(2,1)S(1)} %get-tuple-element.349.refs_6_), channel_id=1, source_target_pairs={{0,5},{1,4},{4,9},{5,8},{8,13},{9,12},{12,17},{13,16},{16,21},{17,... | collective-permute-start | bytes 786440 | tf_op jit(solution)/shard_map/ppermute | solution.py:309
  93.1 26.0 %collective-permute-start.60 = (bf16[2,128,512]{2,1,0:T(8,128)(2,1)S(1)}, bf16[2,128,512]{2,1,0:T(8,128)(2,1)S(1)}, u32[]{:S(2)}, u32[]{:S(2)}) collective-permute-start(bf16[2,128,512]{2,1,0:T(8,128)(2,1)S(1)} %get-tuple-element.349.refs_6_), channel_id=1, source_target_pairs={{0,4},{1,5},{4,8},{5,9},{8,12},{9,13},{12,16},{13,17},{16,20},{17,... | collective-permute-start | bytes 786440 | tf_op jit(solution)/shard_map/ppermute | solution.py:309
  97.5 22.9 %collective-permute-start.59 = (bf16[2,128,512]{2,1,0:T(8,128)(2,1)S(1)}, bf16[2,128,512]{2,1,0:T(8,128)(2,1)S(1)}, u32[]{:S(2)}, u32[]{:S(2)}) collective-permute-start(bf16[2,128,512]{2,1,0:T(8,128)(2,1)S(1)} %get-tuple-element.349.refs_6_), channel_id=1, source_target_pairs={{0,1},{1,0},{4,5},{5,4},{8,9},{9,8},{12,13},{13,12},{16,17},{17,16... | collective-permute-start | bytes 786440 | tf_op jit(solution)/shard_map/ppermute | solution.py:309
  114.9 24.2 %collective-permute-start.64 = (bf16[2,128,512]{2,1,0:T(8,128)(2,1)}, bf16[2,128,512]{2,1,0:T(8,128)(2,1)S(1)}, u32[]{:S(2)}, u32[]{:S(2)}) collective-permute-start(bf16[2,128,512]{2,1,0:T(8,128)(2,1)} %get-tuple-element.369), channel_id=1, source_target_pairs={{0,1},{1,0},{4,5},{5,4},{8,9},{9,8},{12,13},{13,12},{16,17},{17,16... | collective-permute-start | bytes 786440 | tf_op jit(solution)/shard_map/ppermute | solution.py:309
  116.4 22.7 %collective-permute-start.65 = (bf16[2,128,512]{2,1,0:T(8,128)(2,1)}, bf16[2,128,512]{2,1,0:T(8,128)(2,1)S(1)}, u32[]{:S(2)}, u32[]{:S(2)}) collective-permute-start(bf16[2,128,512]{2,1,0:T(8,128)(2,1)} %get-tuple-element.370), channel_id=1, source_target_pairs={{4,0},{5,1},{8,4},{9,5},{12,8},{13,9},{16,12},{17,13},{20,16},{21,... | collective-permute-start | bytes 786440 | tf_op jit(solution)/shard_map/ppermute | solution.py:309
  117.8 21.4 %collective-permute-start.66 = (bf16[2,128,512]{2,1,0:T(8,128)(2,1)}, bf16[2,128,512]{2,1,0:T(8,128)(2,1)S(1)}, u32[]{:S(2)}, u32[]{:S(2)}) collective-permute-start(bf16[2,128,512]{2,1,0:T(8,128)(2,1)} %get-tuple-element.371), channel_id=1, source_target_pairs={{4,1},{5,0},{8,5},{9,4},{12,9},{13,8},{16,13},{17,12},{20,17},{21,... | collective-permute-start | bytes 786440 | tf_op jit(solution)/shard_map/ppermute | solution.py:309
  119.1 27.5 %collective-permute-start.67 = (bf16[2,128,512]{2,1,0:T(8,128)(2,1)}, bf16[2,128,512]{2,1,0:T(8,128)(2,1)S(1)}, u32[]{:S(2)}, u32[]{:S(2)}) collective-permute-start(bf16[2,128,512]{2,1,0:T(8,128)(2,1)} %get-tuple-element.372), channel_id=1, source_target_pairs={{8,0},{9,1},{12,4},{13,5},{16,8},{17,9},{20,12},{21,13},{24,16},{2... | collective-permute-start | bytes 786440 | tf_op jit(solution)/shard_map/ppermute | solution.py:309
  120.4 30.3 %collective-permute-start.68 = (bf16[2,128,512]{2,1,0:T(8,128)(2,1)}, bf16[2,128,512]{2,1,0:T(8,128)(2,1)S(1)}, u32[]{:S(2)}, u32[]{:S(2)}) collective-permute-start(bf16[2,128,512]{2,1,0:T(8,128)(2,1)} %get-tuple-element.373), channel_id=1, source_target_pairs={{8,1},{9,0},{12,5},{13,4},{16,9},{17,8},{20,13},{21,12},{24,17},{2... | collective-permute-start | bytes 786440 | tf_op jit(solution)/shard_map/ppermute | solution.py:309
  151.4 6.9 %collective-permute-start.27 = (bf16[1,128,1024]{2,1,0:T(8,128)(2,1)S(1)}, bf16[1,128,1024]{2,1,0:T(8,128)(2,1)S(1)}, u32[]{:S(2)}, u32[]{:S(2)}) collective-permute-start(bf16[1,128,1024]{2,1,0:T(8,128)(2,1)S(1)} %pad_maximum_fusion.1), channel_id=1, source_target_pairs={{0,1},{1,0},{2,3},{3,2},{4,5},{5,4},{6,7},{7,6},{8,9},{9,8},{10,11... | collective-permute-start | bytes 786440 | tf_op jit(solution)/shard_map/cond/branch_0_fun/ppermute | solution.py:297
  151.8 67.4 %collective-permute-start.35 = (bf16[2,128,4096]{2,1,0:T(8,128)(2,1)}, bf16[2,128,4096]{2,1,0:T(8,128)(2,1)S(1)}, u32[]{:S(2)}, u32[]{:S(2)}) collective-permute-start(bf16[2,128,4096]{2,1,0:T(8,128)(2,1)} %get-tuple-element.211), channel_id=1, source_target_pairs={{0,2},{2,0},{1,3},{3,1},{4,6},{6,4},{5,7},{7,5},{8,10},{10,8},{9,1... | collective-permute-start | bytes 6291464 | tf_op jit(solution)/shard_map/cond/branch_0_fun/ppermute | solution.py:294
  158.5 15.2 %collective-permute-start.28 = (bf16[1,128,1024]{2,1,0:T(8,128)(2,1)S(1)}, bf16[1,128,1024]{2,1,0:T(8,128)(2,1)S(1)}, u32[]{:S(2)}, u32[]{:S(2)}) collective-permute-start(bf16[1,128,1024]{2,1,0:T(8,128)(2,1)S(1)} %convert_element_type.107), channel_id=1, source_target_pairs={{4,0},{12,8},{20,16},{28,24},{5,1},{13,9},{21,17},{29,25},{6,2},{1... | collective-permute-start | bytes 786440 | tf_op jit(solution)/shard_map/cond/branch_0_fun/ppermute | solution.py:444
  159.8 14.0 %collective-permute-start.29 = (bf16[2,128,512]{2,1,0:T(8,128)(2,1)S(1)}, bf16[2,128,512]{2,1,0:T(8,128)(2,1)}, u32[]{:S(2)}, u32[]{:S(2)}) collective-permute-start(bf16[2,128,512]{2,1,0:T(8,128)(2,1)S(1)} %get-tuple-element.197), channel_id=1, source_target_pairs={{0,1},{1,0},{4,5},{5,4},{8,9},{9,8},{12,13},{13,12},{16,17},{17,16... | collective-permute-start | bytes 786440 | tf_op jit(solution)/shard_map/cond/branch_0_fun/ppermute | solution.py:309
  159.8 16.8 %collective-permute-start.30 = (bf16[2,128,512]{2,1,0:T(8,128)(2,1)}, bf16[2,128,512]{2,1,0:T(8,128)(2,1)}, u32[]{:S(2)}, u32[]{:S(2)}) collective-permute-start(bf16[2,128,512]{2,1,0:T(8,128)(2,1)} %get-tuple-element.198), channel_id=1, source_target_pairs={{4,0},{5,1},{8,4},{9,5},{12,8},{13,9},{16,12},{17,13},{20,16},{21,... | collective-permute-start | bytes 786440 | tf_op jit(solution)/shard_map/cond/branch_0_fun/ppermute | solution.py:309
  176.6 15.7 %collective-permute-start.31 = (bf16[1,128,1024]{2,1,0:T(8,128)(2,1)S(1)}, bf16[1,128,1024]{2,1,0:T(8,128)(2,1)S(1)}, u32[]{:S(2)}, u32[]{:S(2)}) collective-permute-start(bf16[1,128,1024]{2,1,0:T(8,128)(2,1)S(1)} %convert_element_type.109), channel_id=1, source_target_pairs={{8,0},{24,16},{9,1},{25,17},{10,2},{26,18},{11,3},{27,19}} | collective-permute-start | bytes 786440 | tf_op jit(solution)/shard_map/cond/branch_0_fun/ppermute | solution.py:444
  177.9 14.5 %collective-permute-start.32 = (bf16[2,128,512]{2,1,0:T(8,128)(2,1)}, bf16[2,128,512]{2,1,0:T(8,128)(2,1)S(1)}, u32[]{:S(2)}, u32[]{:S(2)}) collective-permute-start(bf16[2,128,512]{2,1,0:T(8,128)(2,1)} %get-tuple-element.203), channel_id=1, source_target_pairs={{4,1},{5,0},{8,5},{9,4},{12,9},{13,8},{16,13},{17,12},{20,17},{21,... | collective-permute-start | bytes 786440 | tf_op jit(solution)/shard_map/cond/branch_0_fun/ppermute | solution.py:309
  179.2 18.9 %collective-permute-start.33 = (bf16[2,128,512]{2,1,0:T(8,128)(2,1)}, bf16[2,128,512]{2,1,0:T(8,128)(2,1)}, u32[]{:S(2)}, u32[]{:S(2)}) collective-permute-start(bf16[2,128,512]{2,1,0:T(8,128)(2,1)} %get-tuple-element.204), channel_id=1, source_target_pairs={{8,0},{9,1},{12,4},{13,5},{16,8},{17,9},{20,12},{21,13},{24,16},{2... | collective-permute-start | bytes 786440 | tf_op jit(solution)/shard_map/cond/branch_0_fun/ppermute | solution.py:309
  198.1 20.8 %collective-permute-start.34 = (bf16[1,128,1024]{2,1,0:T(8,128)(2,1)S(1)}, bf16[1,128,1024]{2,1,0:T(8,128)(2,1)S(1)}, u32[]{:S(2)}, u32[]{:S(2)}) collective-permute-start(bf16[1,128,1024]{2,1,0:T(8,128)(2,1)S(1)} %convert_element_type.111), channel_id=1, source_target_pairs={{16,0},{17,1},{18,2},{19,3}} | collective-permute-start | bytes 786440 | tf_op jit(solution)/shard_map/cond/branch_0_fun/ppermute | solution.py:444
  199.4 21.4 %collective-permute-start.36 = (bf16[2,128,512]{2,1,0:T(8,128)(2,1)}, bf16[2,128,512]{2,1,0:T(8,128)(2,1)}, u32[]{:S(2)}, u32[]{:S(2)}) collective-permute-start(bf16[2,128,512]{2,1,0:T(8,128)(2,1)} %get-tuple-element.212), channel_id=1, source_target_pairs={{8,1},{9,0},{12,5},{13,4},{16,9},{17,8},{20,13},{21,12},{24,17},{2... | collective-permute-start | bytes 786440 | tf_op jit(solution)/shard_map/cond/branch_0_fun/ppermute | solution.py:309
  (27 other events, 188.6 us)

commit v3 on v2

--- a/solution.py
+++ b/solution.py
@@ -54,25 +54,26 @@
         base, n = parts[s]
         for b in range(n):
             for k in range(n_sub):
-                kv[base + b, pl.ds(k * chunk, chunk), :] = kv_refs[s][k][b]
+                for t in range(2):
+                    kv[base + b, pl.ds(k * chunk, chunk), t * d : (t + 1) * d] = kv_refs[s][k][b, t]
 
     for s in range(len(parts) - 1):
         load(s)
     plain = parts[-1][0]
     head = pl.program_id(0)
-    pair = 2 * d
-
-    def wide_part(array, first, k, column):
+
+    def wide_part(array, first, k, t, column):
         more = n_blocks - plain
-        here = kv.at[pl.ds(plain, more), pl.ds(k * chunk, chunk), :]
-        there = array.at[pl.ds(first, more), :, pl.ds(pl.multiple_of(column * pair, pair), pair)]
+        here = kv.at[pl.ds(plain, more), pl.ds(k * chunk, chunk), pl.ds(t * d, d)]
+        there = array.at[pl.ds(first, more), t, :, pl.ds(pl.multiple_of(column * d, d), d)]
         return here, there
 
     @pl.when(wide)
     def _():
         for k in range(n_sub):
-            here, there = wide_part(kv_refs[-1][k], 1, k, wide_column + head)
-            pltpu.sync_copy(there, here)
+            for t in range(2):
+                here, there = wide_part(kv_refs[-1][k], 1, k, t, wide_column + head)
+                pltpu.sync_copy(there, here)
 
     dkv[:plain] = jnp.zeros_like(dkv[:plain])
 
@@ -178,8 +179,8 @@
         for b in range(n):
             for k in range(n_sub):
                 rows_k = pl.ds(k * chunk, chunk)
-                dkv_refs[s][k][b, :, :d] = (dkv[base + b, rows_k, :d] * scale).astype(BF16)
-                dkv_refs[s][k][b, :, d:] = dkv[base + b, rows_k, d:].astype(BF16)
+                dkv_refs[s][k][b, 0] = (dkv[base + b, rows_k, :d] * scale).astype(BF16)
+                dkv_refs[s][k][b, 1] = dkv[base + b, rows_k, d:].astype(BF16)
 
     for s, (base, n) in enumerate(parts[:-1]):
         store(s, base, n)
@@ -189,8 +190,9 @@
         kv[plain:, :, :d] = (dkv[plain:, :, :d] * scale).astype(BF16)
         kv[plain:, :, d:] = dkv[plain:, :, d:].astype(BF16)
         for k in range(n_sub):
-            here, there = wide_part(dkv_refs[-1][k], 0, k, head)
-            pltpu.sync_copy(here, there)
+            for t in range(2):
+                here, there = wide_part(dkv_refs[-1][k], 0, k, t, head)
+                pltpu.sync_copy(here, there)
 
 
 def attention(call, info, kinfo, rinfo, mine, other, kv_sets, outs, group, heads):
@@ -210,7 +212,7 @@
     other_spec = pl.BlockSpec((2, chunk, width), lambda h, info: (0, 0, first + h))
 
     def kv_spec(n, column):
-        return pl.BlockSpec((n, chunk, 2 * HEAD_DIM), lambda h, info: (0, 0, column + h))
+        return pl.BlockSpec((n, 2, chunk, HEAD_DIM), lambda h, info: (0, 0, 0, column + h))
 
     anywhere = pl.BlockSpec(memory_space=pl.ANY)
 
@@ -230,7 +232,7 @@
     out_shape = [full, full, jax.ShapeDtypeStruct(other.shape, BF16)]
     out_specs = [mine_spec, mine_spec, other_spec]
     for s, (_, n) in enumerate(parts):
-        out_shape += [jax.ShapeDtypeStruct((n, chunk, heads * 2 * HEAD_DIM), BF16)] * n_sub
+        out_shape += [jax.ShapeDtypeStruct((n, 2, chunk, heads * HEAD_DIM), BF16)] * n_sub
         out_specs += [kv_spec(n, 0) if s < len(parts) - 1 else anywhere] * n_sub
     pairs = rows * 5 * BLOCK * CORES * heads
     results = pl.pallas_call(
@@ -288,7 +290,7 @@
     group = query_rows.shape[1] // key_rows.shape[1]
     my_heads = kv_heads // CORES
     heads = my_heads // SPLIT
-    call_width = heads * 2 * HEAD_DIM
+    call_width = heads * HEAD_DIM
 
     def swap_cores(a):
         return lax.ppermute(a, "c", [(0, 1), (1, 0)])
@@ -319,21 +321,17 @@
         return lax.dynamic_slice_in_dim(a, core * width, width, axis=1)
 
     def columns(core):
-        k, v = half_of(key_rows, core), half_of(value_rows, core)
-        cut = lambda a, h: a[:, h * HEAD_DIM : (h + 1) * HEAD_DIM]
-        return jnp.concatenate([cut(a, h) for h in range(my_heads) for a in (k, v)], axis=1)
-
-    kv_mine = columns(c)
-    kv_other = swap_cores(columns(1 - c))
-    kv_pair = jnp.stack([kv_mine, kv_other])
-    kv_both = [kv_pair[:, :, i * call_width : (i + 1) * call_width] for i in range(SPLIT)]
-    other = swap_cores(jnp.stack([half_of(query_rows, 1 - c), half_of(out_grad, 1 - c)]))
+        return jnp.stack([half_of(key_rows, core), half_of(value_rows, core)])
+
+    kv_send, segment_ids = lax.optimization_barrier((columns(1 - c), segment_ids))
+    kv_pair = jnp.stack([columns(c), swap_cores(kv_send)])
+    kv_both = [kv_pair[..., i * call_width : (i + 1) * call_width] for i in range(SPLIT)]
+    rows_send = jnp.stack([half_of(query_rows, 1 - c), half_of(out_grad, 1 - c)])
     ids = lax.all_to_all(
         jnp.broadcast_to(segment_ids[None], (devices, chunk)), ALL, split_axis=0, concat_axis=0, tiled=True
     )
     n0 = jnp.sum((ids == 0).astype(jnp.int32))
     level = (n0 > BLOCK).astype(jnp.int32) + (n0 > 2 * BLOCK).astype(jnp.int32)
-    count = jnp.left_shift(1, level)
 
     routes = [(by, k) for by in range(3) for k in range(n_sub)]
 
@@ -352,14 +350,43 @@
 
     in_order = jnp.where(c == 0, kv_pair, kv_pair[::-1])
 
+    def describe(ids, n0, count):
+        row_chunk = jnp.stack([(2 * half + (c ^ r)) * n_sub + x for r in range(CORES)])
+        row_pos = row_chunk[:, None] * chunk + jnp.arange(chunk, dtype=jnp.int32)
+        row_seg = jnp.take(ids, row_chunk, axis=0)
+        rinfo = jnp.tile(jnp.stack([row_pos, row_seg], axis=1)[:, :, None], (1, 1, 1, pl.cdiv(128, chunk)))
+        starts = jnp.sum((ids[None] < row_seg[:, :1, None]).astype(jnp.int32), axis=(1, 2))
+        sub = (x - jnp.arange(n_sub, dtype=jnp.int32)) % n_sub
+        block = jnp.stack(
+            [2 * (half - s) + (c ^ k) for s in range(3) for k in range(CORES)]
+            + [jnp.full((), j, jnp.int32) for j in range(WIDE)]
+        )
+        place = jnp.arange(block.shape[0])
+        usable = jnp.where(place < 6, block >= count, place - 6 < count)
+        key_chunk = jnp.clip(block, 0)[:, None] * n_sub + sub[None]
+        key_seg = jnp.take(ids, key_chunk.reshape(-1), axis=0).reshape(-1, BLOCK)
+        key_pos = (key_chunk[..., None] * chunk + jnp.arange(chunk, dtype=jnp.int32)).reshape(-1, BLOCK)
+        key_pos = jnp.where(usable[:, None], key_pos, FAR)
+        kinfo = jnp.stack([key_pos, key_seg], axis=1)[..., None]
+        first = block * BLOCK
+        need = (
+            usable[None]
+            & (first[None] <= row_pos[:, -1:])
+            & ((first[None] < n0) | (first[None] + BLOCK > starts[:, None]))
+        )
+        info = jnp.concatenate(
+            [jnp.stack([c, jnp.full((), count, c.dtype)]), need.astype(jnp.int32).reshape(-1)]
+        )
+        return info, kinfo, rinfo
+
     def padded(arrays):
-        room = blank((WIDE, chunk, SPLIT * call_width))
-        return tuple(lax.dynamic_update_slice(room, a, (0, 0, 0)) for a in arrays)
+        room = blank((WIDE, 2, chunk, SPLIT * call_width))
+        return tuple(lax.dynamic_update_slice(room, a, (0, 0, 0, 0)) for a in arrays)
 
     def fetch(blocks):
-        def run(pair, band):
+        def run(pair, band, rows, ids, n0):
             moved = pair[:blocks]
-            bands = send_bands(band)
+            bands = (send_bands(band), swap_cores(rows))
             step, stages = halves // 2, halves.bit_length() - 1
             stage = 0
             while step:
@@ -368,12 +395,12 @@
                 step //= 2
                 stage += 1
                 moved, bands = after(moved, bands, stage, stages)
-            return padded(spread(moved)), bands
+            return padded(spread(moved)), bands, describe(ids, n0, blocks)
 
         return run
 
-    def fetch_all(moved, band):
-        bands = send_bands(band)
+    def fetch_all(moved, band, rows, ids, n0):
+        bands = (send_bands(band), swap_cores(rows))
         step = planes // 2
         while step:
             got = lax.ppermute(moved, "z", [(i, i + step) for i in range(0, planes, 2 * step)])
@@ -381,44 +408,16 @@
             step //= 2
         across = lax.ppermute(moved, "y", [(0, 1), (1, 0)])
         moved = jnp.concatenate([jnp.where(y == 0, moved, across), jnp.where(y == 0, across, moved)])
-        return tuple(spread(moved)), bands
-
-    in_order, other = lax.optimization_barrier((in_order, other))
-    prompt_set, first_bands = lax.switch(
-        level, [fetch(1), fetch(2), fetch_all], in_order, kv_both[0]
+        return tuple(spread(moved)), bands, describe(ids, n0, WIDE)
+
+    prompt_set, (first_bands, other), (info, kinfo, rinfo) = lax.switch(
+        level, [fetch(1), fetch(2), fetch_all], in_order, kv_both[0], rows_send, ids, n0
     )
     bands = [first_bands]
 
     for a in kv_both[1:]:
         a, _, prompt_set = lax.optimization_barrier((a, bands[-1], prompt_set))
         bands.append(send_bands(a))
-
-    row_chunk = jnp.stack([(2 * half + (c ^ r)) * n_sub + x for r in range(CORES)])
-    row_pos = row_chunk[:, None] * chunk + jnp.arange(chunk, dtype=jnp.int32)
-    row_seg = jnp.take(ids, row_chunk, axis=0)
-    rinfo = jnp.tile(jnp.stack([row_pos, row_seg], axis=1)[:, :, None], (1, 1, 1, pl.cdiv(128, chunk)))
-    starts = jnp.sum((ids[None] < row_seg[:, :1, None]).astype(jnp.int32), axis=(1, 2))
-    sub = (x - jnp.arange(n_sub, dtype=jnp.int32)) % n_sub
-    block = jnp.stack(
-        [2 * (half - s) + (c ^ k) for s in range(3) for k in range(CORES)]
-        + [jnp.full((), j, jnp.int32) for j in range(WIDE)]
-    )
-    place = jnp.arange(block.shape[0])
-    usable = jnp.where(place < 6, block >= count, place - 6 < count)
-    key_chunk = jnp.clip(block, 0)[:, None] * n_sub + sub[None]
-    key_seg = jnp.take(ids, key_chunk.reshape(-1), axis=0).reshape(-1, BLOCK)
-    key_pos = (key_chunk[..., None] * chunk + jnp.arange(chunk, dtype=jnp.int32)).reshape(-1, BLOCK)
-    key_pos = jnp.where(usable[:, None], key_pos, FAR)
-    kinfo = jnp.stack([key_pos, key_seg], axis=1)[..., None]
-    first = block * BLOCK
-    need = (
-        usable[None]
-        & (first[None] <= row_pos[:, -1:])
-        & ((first[None] < n0) | (first[None] + BLOCK > starts[:, None]))
-    )
-    info = jnp.concatenate(
-        [jnp.stack([c, count]), need.astype(jnp.int32).reshape(-1)]
-    )
 
     outs = None
     owns, prompts, wide_parts = [], [], []
@@ -435,7 +434,7 @@
         prompts.append(tuple(grads[3]))
         wide_parts.append(tuple(grads[4]))
 
-    joined = lambda parts, k: jnp.concatenate([p[k] for p in parts], axis=2)
+    joined = lambda parts, k: jnp.concatenate([p[k] for p in parts], axis=3)
 
     def tree(back, axes, length, beside):
         step, stage, stages = 1, 1, length.bit_length()
@@ -456,7 +455,7 @@
                 arrays.append(a if blocks == 1 else jnp.concatenate([a, joined(parts[1], k)[:1]]))
             back, (own, arrived) = tree(gather_back(arrays), ("z", "y"), halves, (own, arrived))
             if blocks == 1:
-                back = jnp.where((jnp.arange(CORES) == c)[:, None, None], back, 0.0)
+                back = jnp.where((jnp.arange(CORES) == c)[:, None, None, None], back, 0.0)
             else:
                 back = jnp.where(c == 0, back, back[::-1])
             return jnp.where(half == 0, back, 0.0), own, arrived
@@ -483,7 +482,7 @@
         outs[2],
     )
     owns.append(last_own)
-    total = back + jnp.concatenate([sum(a.astype(F32) for a in arrays) for arrays in owns], axis=2)
+    total = back + jnp.concatenate([sum(a.astype(F32) for a in arrays) for arrays in owns], axis=3)
     total = total.astype(BF16)
 
     got = swap_cores(total[1])
@@ -491,8 +490,7 @@
     high = jnp.where(c == 0, got, total[0])
 
     def columns_back(t):
-        starts = [(2 * h + t) * HEAD_DIM for h in range(my_heads)]
-        return jnp.concatenate([a[:, s : s + HEAD_DIM] for a in (low, high) for s in starts], axis=1)
+        return jnp.concatenate([low[t], high[t]], axis=1)
 
     def join(full, part):
         return lax.dynamic_update_slice(full, part, (0, (1 - c) * part.shape[1]))

time: 231 us -> 213 us (0.922)
  local copies, waits for them, and re-layouts: 26.6 us -> 17.1 us
  waiting for transfers between devices: 91.7 us -> 84.8 us
  starting transfers between devices: 66.8 us -> 63.1 us
  other arithmetic: 8.57 us -> 11.1 us
    ppermute x20, waiting for transfers between devices: 35.5 us -> 21.4 us  [send(): return lax.ppermute(a, ('z', 'y', 'x'), moves)]
    ppermute x3, waiting for transfers between devices: 4.29 us -> 12.6 us  [run(): lax.ppermute(moved, ('z', 'y'), [(i, i + step) for i in range(0, halves,...]
    unnamed x69 -> x50, local copies, waits for them, and re-layouts: 12.5 us -> 5.31 us
    ppermute x20, starting transfers between devices: 43.5 us -> 39 us  [send(): return lax.ppermute(a, ('z', 'y', 'x'), moves)]
    all_to_all x1, waiting for transfers between devices: 0.01 us -> 3.58 us  [per_device(): lax.all_to_all(jnp.broadcast_to(segment_ids[None], (devices, chunk)), ALL...]
    ppermute x3, waiting for transfers between devices: 42.6 us -> 39.1 us  [tree(): lax.ppermute(back.astype(BF16), axes, [(j + step, j) for j in range(0, le...]
    broadcast_in_dim x3 -> x0, local copies, waits for them, and re-layouts: 2.38 us -> none  [the longest x1 2.28 us: per_device(): kinfo = jnp.stack([key_pos, key_seg], axis=1)[..., None]]
  transfers between devices with their start and end apart: 33 -> 33, of which waited for: 15 -> 15; matrix products, arithmetic and copies ran while one was open for 10% -> 6% of each run, Pallas kernels for 15% -> 15%
where the time goes in v3:
time: 213 us; the launch traced here: 211 us
  waiting for transfers between devices  84.8 us (40%)
  starting transfers between devices  63.1 us (30%)
  Pallas kernels  31.9 us (15%)
  local copies, waits for them, and re-layouts  17.1 us (8%)
  other arithmetic  11.1 us (5%)
  between operations  2.37 us (1%)
    ppermute x3, waiting for transfers between devices, tree(): lax.ppermute(back.astype(BF16), axes, [(j + step, j) for j in range(0, le...  39.1 us
    ppermute x20, starting transfers between devices, send(): return lax.ppermute(a, ('z', 'y', 'x'), moves)  39 us
    pallas_call x2, Pallas kernels, attention(): pl.pallas_call(functools.partial(attention_kernel, n_sub, chunk, group, n...  31.9 us
    ppermute x20, waiting for transfers between devices, send(): return lax.ppermute(a, ('z', 'y', 'x'), moves)  21.4 us
    ppermute x3, waiting for transfers between devices, run(): lax.ppermute(moved, ('z', 'y'), [(i, i + step) for i in range(0, halves,...  12.6 us
    ppermute x3, starting transfers between devices, run(): lax.ppermute(moved, ('z', 'y'), [(i, i + step) for i in range(0, halves,...  11.2 us
    ppermute x2, waiting for transfers between devices, rotate(): return lax.ppermute(a, 'x', [(i, (i + by) % n_sub) for i in range(n_sub)])  8.18 us
    all_to_all x1, starting transfers between devices, per_device(): lax.all_to_all(jnp.broadcast_to(segment_ids[None], (devices, chunk)), ALL...  7.3 us
  transfers between devices with their start and end apart: 33, of which 15 were waited for; matrix products, arithmetic and copies ran while one was open for 6% of the time, Pallas kernels for 15%

profile of v3, /device:TPU:0, one launch (start us, length us, event | category | flops | bytes accessed | tf_op | source)
XLA Modules:
  0.0 210.8 jit_solution(4505929904707010725)
XLA Ops:
  3.1 7.3 %all-to-all-start = ((s32[32,1,128]{2,1,0:T(1,128)}), s32[32,1,128]{2,1,0:T(1,128)S(1)}, u32[]{:S(2)}, u32[]{:S(2)}) async-start(s32[32,1,128]{2,1,0:T(1,128)} %broadcast_in_dim.143), calls=%async_computation | async-start | bytes 32768 | tf_op jit(solution)/shard_map/all_to_all | solution.py:330
  10.7 1.7 dynamic-slice_bitcast_fusion
  13.9 3.6 %all-to-all-done = s32[32,1,128]{2,1,0:T(1,128)S(1)} async-done(((s32[32,1,128]{2,1,0:T(1,128)}), s32[32,1,128]{2,1,0:T(1,128)S(1)}, u32[]{:S(2)}, u32[]{:S(2)}) %all-to-all-start) | async-done | bytes 16416 | tf_op jit(solution)/shard_map/all_to_all | solution.py:330
  20.3 48.6 %conditional.4 = (bf16[4,2,128,512]{3,2,1,0:T(8,128)(2,1)}, bf16[4,2,128,512]{3,2,1,0:T(8,128)(2,1)}, bf16[2,2,128,256]{3,2,1,0:T(8,128)(2,1)}, bf16[2,2,128,256...) conditional(s32[]{:T(128)} %clamp.4, (s32[]{:T(128)}, ...), branch_computations={%region_1.5_spmd, %region_3.7_spmd, %region_5.9_spmd} | conditional | flops 1614144 | bytes 33793784 | solution.py:413
  20.4 2.5 %collective-permute-start.37 = (bf16[2,2,128,256]{3,2,1,0:T(8,128)(2,1)}, bf16[2,2,128,256]{3,2,1,0:T(8,128)(2,1)S(1)}, u32[]{:S(2)}, u32[]{:S(2)}) collective-permute-start(bf16[2,2,128,256]{3,2,1,0:T(8,128)(2,1)} %get-tuple-element.535), channel_id=1, source_target_pairs={{0,9},{1,8},{4,13},{5,12},{8,17},{9,16},{12,21},{13,20},{16,25},{1... | collective-permute-start | bytes 786440 | tf_op jit(solution)/shard_map/cond/branch_0_fun/ppermute | solution.py:311
  22.8 4.1 %collective-permute-start.34 = (bf16[2,2,128,256]{3,2,1,0:T(8,128)(2,1)}, bf16[2,2,128,256]{3,2,1,0:T(8,128)(2,1)}, u32[]{:S(2)}, u32[]{:S(2)}) collective-permute-start(bf16[2,2,128,256]{3,2,1,0:T(8,128)(2,1)} %get-tuple-element.535), channel_id=1, source_target_pairs={{0,5},{1,4},{4,9},{5,8},{8,13},{9,12},{12,17},{13,16},{16,21},{17,... | collective-permute-start | bytes 786440 | tf_op jit(solution)/shard_map/cond/branch_0_fun/ppermute | solution.py:311
  27.5 3.1 %collective-permute-start.30 = (bf16[1,2,128,512]{3,2,1,0:T(8,128)(2,1)S(1)}, bf16[1,2,128,512]{3,2,1,0:T(8,128)(2,1)S(1)}, u32[]{:S(2)}, u32[]{:S(2)}) collective-permute-start(bf16[1,2,128,512]{3,2,1,0:T(8,128)(2,1)S(1)} %slice.55), channel_id=1, source_target_pairs={{0,16},{1,17},{2,18},{3,19}} | collective-permute-start | bytes 786440 | tf_op jit(solution)/shard_map/cond/branch_0_fun/ppermute | solution.py:393
  33.6 2.2 %collective-permute-done.30 = bf16[1,2,128,512]{3,2,1,0:T(8,128)(2,1)S(1)} collective-permute-done((bf16[1,2,128,512]{3,2,1,0:T(8,128)(2,1)S(1)}, bf16[1,2,128,512]{3,2,1,0:T(8,128)(2,1)S(1)}, u32[]{:S(2)}, u32[]{:S(2)}) %collective-permute-start.30) | collective-permute-done | bytes 262176 | tf_op jit(solution)/shard_map/cond/branch_0_fun/ppermute | solution.py:393
  35.8 2.0 collective-permute-start.33
  38.4 6.8 %collective-permute-start.32 = (bf16[1,2,128,512]{3,2,1,0:T(8,128)(2,1)S(1)}, bf16[1,2,128,512]{3,2,1,0:T(8,128)(2,1)S(1)}, u32[]{:S(2)}, u32[]{:S(2)}) collective-permute-start(bf16[1,2,128,512]{3,2,1,0:T(8,128)(2,1)S(1)} %broadcast_select_fusion.1), channel_id=1, source_target_pairs={{0,8},{16,24},{1,9},{17,25},{2,10},{18,26},{3,11},{19,27}} | collective-permute-start | bytes 786440 | tf_op jit(solution)/shard_map/cond/branch_0_fun/ppermute | solution.py:393
  45.3 5.6 %collective-permute-done.32 = bf16[1,2,128,512]{3,2,1,0:T(8,128)(2,1)S(1)} collective-permute-done((bf16[1,2,128,512]{3,2,1,0:T(8,128)(2,1)S(1)}, bf16[1,2,128,512]{3,2,1,0:T(8,128)(2,1)S(1)}, u32[]{:S(2)}, u32[]{:S(2)}) %collective-permute-start.32) | collective-permute-done | bytes 262176 | tf_op jit(solution)/shard_map/cond/branch_0_fun/ppermute | solution.py:393
  50.9 4.4 %collective-permute-start.36 = (bf16[2,2,128,256]{3,2,1,0:T(8,128)(2,1)}, bf16[2,2,128,256]{3,2,1,0:T(8,128)(2,1)S(1)}, u32[]{:S(2)}, u32[]{:S(2)}) collective-permute-start(bf16[2,2,128,256]{3,2,1,0:T(8,128)(2,1)} %get-tuple-element.535), channel_id=1, source_target_pairs={{0,8},{1,9},{4,12},{5,13},{8,16},{9,17},{12,20},{13,21},{16,24},{1... | collective-permute-start | bytes 786440 | tf_op jit(solution)/shard_map/cond/branch_0_fun/ppermute | solution.py:311
  56.8 4.8 %collective-permute-done.35 = bf16[1,2,128,512]{3,2,1,0:T(8,128)(2,1)S(1)} collective-permute-done((bf16[1,2,128,512]{3,2,1,0:T(8,128)(2,1)S(1)}, bf16[1,2,128,512]{3,2,1,0:T(8,128)(2,1)S(1)}, u32[]{:S(2)}, u32[]{:S(2)}) %collective-permute-start.35) | collective-permute-done | bytes 262176 | tf_op jit(solution)/shard_map/cond/branch_0_fun/ppermute | solution.py:393
  62.4 2.3 %copy.35 = bf16[4,2,128,512]{3,2,1,0:T(8,128)(2,1)} copy(bf16[4,2,128,512]{3,2,1,0:T(8,128)(2,1)} %blank.2) | data formatting | bytes 2097152 | tf_op jit(solution)/shard_map/cond
  66.3 1.9 collective-permute-done.39
  68.9 3.0 %collective-permute-start.65 = (bf16[2,2,128,256]{3,2,1,0:T(8,128)(2,1)S(1)}, bf16[2,2,128,256]{3,2,1,0:T(8,128)(2,1)S(1)}, u32[]{:S(2)}, u32[]{:S(2)}) collective-permute-start(bf16[2,2,128,256]{3,2,1,0:T(8,128)(2,1)S(1)} %get-tuple-element.409.refs_6_), channel_id=1, source_target_pairs={{0,9},{1,8},{4,13},{5,12},{8,17},{9,16},{12,21},{13,20},{16,25},{1... | collective-permute-start | bytes 786440 | tf_op jit(solution)/shard_map/ppermute | solution.py:311
  71.9 2.9 %collective-permute-start.64 = (bf16[2,2,128,256]{3,2,1,0:T(8,128)(2,1)S(1)}, bf16[2,2,128,256]{3,2,1,0:T(8,128)(2,1)S(1)}, u32[]{:S(2)}, u32[]{:S(2)}) collective-permute-start(bf16[2,2,128,256]{3,2,1,0:T(8,128)(2,1)S(1)} %get-tuple-element.409.refs_6_), channel_id=1, source_target_pairs={{0,8},{1,9},{4,12},{5,13},{8,16},{9,17},{12,20},{13,21},{16,24},{1... | collective-permute-start | bytes 786440 | tf_op jit(solution)/shard_map/ppermute | solution.py:311
  74.9 4.4 %collective-permute-start.63 = (bf16[2,2,128,256]{3,2,1,0:T(8,128)(2,1)S(1)}, bf16[2,2,128,256]{3,2,1,0:T(8,128)(2,1)S(1)}, u32[]{:S(2)}, u32[]{:S(2)}) collective-permute-start(bf16[2,2,128,256]{3,2,1,0:T(8,128)(2,1)S(1)} %get-tuple-element.409.refs_6_), channel_id=1, source_target_pairs={{0,5},{1,4},{4,9},{5,8},{8,13},{9,12},{12,17},{13,16},{16,21},{17,... | collective-permute-start | bytes 786440 | tf_op jit(solution)/shard_map/ppermute | solution.py:311
  79.2 2.2 %collective-permute-start.62 = (bf16[2,2,128,256]{3,2,1,0:T(8,128)(2,1)S(1)}, bf16[2,2,128,256]{3,2,1,0:T(8,128)(2,1)S(1)}, u32[]{:S(2)}, u32[]{:S(2)}) collective-permute-start(bf16[2,2,128,256]{3,2,1,0:T(8,128)(2,1)S(1)} %get-tuple-element.409.refs_6_), channel_id=1, source_target_pairs={{0,4},{1,5},{4,8},{5,9},{8,12},{9,13},{12,16},{13,17},{16,20},{17,... | collective-permute-start | bytes 786440 | tf_op jit(solution)/shard_map/ppermute | solution.py:311
  83.1 15.9 %attention_0.1 = (bf16[128,8192]{1,0:T(8,128)(2,1)}, bf16[128,8192]{1,0:T(8,128)(2,1)}, bf16[2,128,4096]{2,1,0:T(8,128)(2,1)}, bf16[2,2,128,256]{3,2,1,0:T(8,128...) custom-call(s32[22]{0:T(128)S(1)} %get-tuple-element.397.refs_0_, ...), custom_call_target="tpu_custom_call" | custom-call | flops 8053063680 | bytes 8388608 | tf_op jit(solution)/shard_map/attention_0/pallas_call | solution.py:238
  105.0 16.0 %attention_1.1 = (bf16[128,8192]{1,0:T(8,128)(2,1)}, bf16[128,8192]{1,0:T(8,128)(2,1)}, bf16[2,128,4096]{2,1,0:T(8,128)(2,1)}, bf16[2,2,128,256]{3,2,1,0:T(8,128...) custom-call(s32[22]{0:T(128)S(1)} %get-tuple-element.397.refs_0_, ...), custom_call_target="tpu_custom_call", output_to_operand_aliasing={{0}: (16, {}), {1}: (17, {}), {2}: (18, {})} | custom-call | flops 8053063680 | bytes 8388608 | tf_op jit(solution)/shard_map/attention_1/pallas_call | solution.py:238
  121.4 6.7 %collective-permute-done.69 = bf16[2,2,128,256]{3,2,1,0:T(8,128)(2,1)S(1)} collective-permute-done((bf16[2,2,128,256]{3,2,1,0:T(8,128)(2,1)}, bf16[2,2,128,256]{3,2,1,0:T(8,128)(2,1)S(1)}, u32[]{:S(2)}, u32[]{:S(2)}) %collective-permute-start.69) | collective-permute-done | bytes 262176 | tf_op jit(solution)/shard_map/ppermute | solution.py:311
  128.1 3.8 %collective-permute-done.70 = bf16[2,2,128,256]{3,2,1,0:T(8,128)(2,1)S(1)} collective-permute-done((bf16[2,2,128,256]{3,2,1,0:T(8,128)(2,1)}, bf16[2,2,128,256]{3,2,1,0:T(8,128)(2,1)S(1)}, u32[]{:S(2)}, u32[]{:S(2)}) %collective-permute-start.70) | collective-permute-done | bytes 262176 | tf_op jit(solution)/shard_map/ppermute | solution.py:311
  132.6 69.5 %conditional.6 = (f32[2,2,128,512]{3,2,1,0:T(8,128)S(1)}, bf16[2,2,128,256]{3,2,1,0:T(8,128)(2,1)}, bf16[2,2,128,256]{3,2,1,0:T(8,128)(2,1)}, bf16[2,2,128,256]{...) conditional(s32[]{:T(128)} %clamp.4, (s32[]{:T(128)}, ...), branch_computations={%region_7.10_spmd, %region_8.11_spmd, %region_9.12_spmd} | conditional | flops 13369347 | bytes 72876760
  133.3 6.3 %collective-permute-done = bf16[1,2,128,512]{3,2,1,0:T(8,128)(2,1)S(1)} collective-permute-done((bf16[1,2,128,512]{3,2,1,0:T(8,128)(2,1)S(1)}, bf16[1,2,128,512]{3,2,1,0:T(8,128)(2,1)S(1)}, u32[]{:S(2)}, u32[]{:S(2)}) %collective-permute-start) | collective-permute-done | bytes 262176 | tf_op jit(solution)/shard_map/cond/branch_0_fun/ppermute | solution.py:299
  142.7 9.0 %collective-permute-done.1 = bf16[1,2,128,512]{3,2,1,0:T(8,128)(2,1)S(1)} collective-permute-done((bf16[1,2,128,512]{3,2,1,0:T(8,128)(2,1)S(1)}, bf16[1,2,128,512]{3,2,1,0:T(8,128)(2,1)S(1)}, u32[]{:S(2)}, u32[]{:S(2)}) %collective-permute-start.1) | collective-permute-done | bytes 262176 | tf_op jit(solution)/shard_map/cond/branch_0_fun/ppermute | solution.py:443
  151.8 2.8 %collective-permute-done.3 = bf16[2,2,128,256]{3,2,1,0:T(8,128)(2,1)} collective-permute-done((bf16[2,2,128,256]{3,2,1,0:T(8,128)(2,1)}, bf16[2,2,128,256]{3,2,1,0:T(8,128)(2,1)}, u32[]{:S(2)}, u32[]{:S(2)}) %collective-permute-start.3) | collective-permute-done | bytes 262176 | tf_op jit(solution)/shard_map/cond/branch_0_fun/ppermute | solution.py:311
  158.5 11.9 %collective-permute-done.4 = bf16[1,2,128,512]{3,2,1,0:T(8,128)(2,1)S(1)} collective-permute-done((bf16[1,2,128,512]{3,2,1,0:T(8,128)(2,1)S(1)}, bf16[1,2,128,512]{3,2,1,0:T(8,128)(2,1)S(1)}, u32[]{:S(2)}, u32[]{:S(2)}) %collective-permute-start.4) | collective-permute-done | bytes 262176 | tf_op jit(solution)/shard_map/cond/branch_0_fun/ppermute | solution.py:443
  170.5 7.1 %collective-permute-done.6 = bf16[2,2,128,256]{3,2,1,0:T(8,128)(2,1)} collective-permute-done((bf16[2,2,128,256]{3,2,1,0:T(8,128)(2,1)}, bf16[2,2,128,256]{3,2,1,0:T(8,128)(2,1)}, u32[]{:S(2)}, u32[]{:S(2)}) %collective-permute-start.6) | collective-permute-done | bytes 262176 | tf_op jit(solution)/shard_map/cond/branch_0_fun/ppermute | solution.py:311
  180.3 18.2 %collective-permute-done.7 = bf16[1,2,128,512]{3,2,1,0:T(8,128)(2,1)S(1)} collective-permute-done((bf16[1,2,128,512]{3,2,1,0:T(8,128)(2,1)S(1)}, bf16[1,2,128,512]{3,2,1,0:T(8,128)(2,1)S(1)}, u32[]{:S(2)}, u32[]{:S(2)}) %collective-permute-start.7) | collective-permute-done | bytes 262176 | tf_op jit(solution)/shard_map/cond/branch_0_fun/ppermute | solution.py:443
  202.1 2.3 %convert_add_fusion.11 = f32[2,2,128,256]{3,2,1,0:T(8,128)S(1)} fusion(bf16[2,2,128,256]{3,2,1,0:T(8,128)(2,1)} %copy-done.17, bf16[2,2,128,256]{3,2,1,0:T(8,128)(2,1)} %copy-done.16, bf16[2,2,128,256]{3,2,1,0:T(8,128)(2,1)} %copy-done.15, bf16[2,2,128,256]{3,2,1,0:T(8,128)(2,1)} %copy-done.14, bf16[2,2,128,256]{3,2,1,0:T(8,128)(2,1)} %copy-done.13, ...), kind=kLoop, calls=%fused_computation.154 | loop fusion | flops 1441792 | bytes 2097152 | tf_op jit(solution)/shard_map/add | solution.py:485
  204.4 1.5 convert_add_fusion.10
  (165 shorter events, 41.8 us)
Async XLA Ops:
  3.1 14.4 %all-to-all-start = ((s32[32,1,128]{2,1,0:T(1,128)}), s32[32,1,128]{2,1,0:T(1,128)S(1)}, u32[]{:S(2)}, u32[]{:S(2)}) async-start(s32[32,1,128]{2,1,0:T(1,128)} %broadcast_in_dim.143), calls=%async_computation | async-start | bytes 32768 | tf_op jit(solution)/shard_map/all_to_all | solution.py:330
  10.4 9.0 %collective-permute-start.60 = (bf16[2,128,512]{2,1,0:T(8,128)(2,1)S(1)}, bf16[2,128,512]{2,1,0:T(8,128)(2,1)S(1)}, u32[]{:S(2)}, u32[]{:S(2)}) collective-permute-start(bf16[2,128,512]{2,1,0:T(8,128)(2,1)S(1)} %pad_maximum_fusion.6), channel_id=1, source_target_pairs={{0,2},{2,0},{1,3},{3,1},{4,6},{6,4},{5,7},{7,5},{8,10},{10,8},{9,1... | collective-permute-start | bytes 786440 | tf_op jit(solution)/shard_map/ppermute | solution.py:296
  20.4 41.2 %collective-permute-start.37 = (bf16[2,2,128,256]{3,2,1,0:T(8,128)(2,1)}, bf16[2,2,128,256]{3,2,1,0:T(8,128)(2,1)S(1)}, u32[]{:S(2)}, u32[]{:S(2)}) collective-permute-start(bf16[2,2,128,256]{3,2,1,0:T(8,128)(2,1)} %get-tuple-element.535), channel_id=1, source_target_pairs={{0,9},{1,8},{4,13},{5,12},{8,17},{9,16},{12,21},{13,20},{16,25},{1... | collective-permute-start | bytes 786440 | tf_op jit(solution)/shard_map/cond/branch_0_fun/ppermute | solution.py:311
  22.8 32.5 %collective-permute-start.34 = (bf16[2,2,128,256]{3,2,1,0:T(8,128)(2,1)}, bf16[2,2,128,256]{3,2,1,0:T(8,128)(2,1)}, u32[]{:S(2)}, u32[]{:S(2)}) collective-permute-start(bf16[2,2,128,256]{3,2,1,0:T(8,128)(2,1)} %get-tuple-element.535), channel_id=1, source_target_pairs={{0,5},{1,4},{4,9},{5,8},{8,13},{9,12},{12,17},{13,16},{16,21},{17,... | collective-permute-start | bytes 786440 | tf_op jit(solution)/shard_map/cond/branch_0_fun/ppermute | solution.py:311
  26.9 11.5 %collective-permute-start.31 = (bf16[2,2,128,256]{3,2,1,0:T(8,128)(2,1)}, bf16[2,2,128,256]{3,2,1,0:T(8,128)(2,1)}, u32[]{:S(2)}, u32[]{:S(2)}) collective-permute-start(bf16[2,2,128,256]{3,2,1,0:T(8,128)(2,1)} %get-tuple-element.535), channel_id=1, source_target_pairs={{0,1},{1,0},{4,5},{5,4},{8,9},{9,8},{12,13},{13,12},{16,17},{17,16... | collective-permute-start | bytes 786440 | tf_op jit(solution)/shard_map/cond/branch_0_fun/ppermute | solution.py:311
  27.5 8.3 %collective-permute-start.30 = (bf16[1,2,128,512]{3,2,1,0:T(8,128)(2,1)S(1)}, bf16[1,2,128,512]{3,2,1,0:T(8,128)(2,1)S(1)}, u32[]{:S(2)}, u32[]{:S(2)}) collective-permute-start(bf16[1,2,128,512]{3,2,1,0:T(8,128)(2,1)S(1)} %slice.55), channel_id=1, source_target_pairs={{0,16},{1,17},{2,18},{3,19}} | collective-permute-start | bytes 786440 | tf_op jit(solution)/shard_map/cond/branch_0_fun/ppermute | solution.py:393
  30.6 31.0 %collective-permute-start.38 = (bf16[2,128,4096]{2,1,0:T(8,128)(2,1)}, bf16[2,128,4096]{2,1,0:T(8,128)(2,1)}, u32[]{:S(2)}, u32[]{:S(2)}) collective-permute-start(bf16[2,128,4096]{2,1,0:T(8,128)(2,1)} %get-tuple-element.193), channel_id=1, source_target_pairs={{0,2},{2,0},{1,3},{3,1},{4,6},{6,4},{5,7},{7,5},{8,10},{10,8},{9,1... | collective-permute-start | bytes 6291464 | tf_op jit(solution)/shard_map/cond/branch_0_fun/ppermute | solution.py:296
  35.8 19.6 %collective-permute-start.33 = (bf16[2,2,128,256]{3,2,1,0:T(8,128)(2,1)}, bf16[2,2,128,256]{3,2,1,0:T(8,128)(2,1)}, u32[]{:S(2)}, u32[]{:S(2)}) collective-permute-start(bf16[2,2,128,256]{3,2,1,0:T(8,128)(2,1)} %get-tuple-element.535), channel_id=1, source_target_pairs={{0,4},{1,5},{4,8},{5,9},{8,12},{9,13},{12,16},{13,17},{16,20},{17,... | collective-permute-start | bytes 786440 | tf_op jit(solution)/shard_map/cond/branch_0_fun/ppermute | solution.py:311
  38.4 12.5 %collective-permute-start.32 = (bf16[1,2,128,512]{3,2,1,0:T(8,128)(2,1)S(1)}, bf16[1,2,128,512]{3,2,1,0:T(8,128)(2,1)S(1)}, u32[]{:S(2)}, u32[]{:S(2)}) collective-permute-start(bf16[1,2,128,512]{3,2,1,0:T(8,128)(2,1)S(1)} %broadcast_select_fusion.1), channel_id=1, source_target_pairs={{0,8},{16,24},{1,9},{17,25},{2,10},{18,26},{3,11},{19,27}} | collective-permute-start | bytes 786440 | tf_op jit(solution)/shard_map/cond/branch_0_fun/ppermute | solution.py:393
  50.9 10.7 %collective-permute-start.36 = (bf16[2,2,128,256]{3,2,1,0:T(8,128)(2,1)}, bf16[2,2,128,256]{3,2,1,0:T(8,128)(2,1)S(1)}, u32[]{:S(2)}, u32[]{:S(2)}) collective-permute-start(bf16[2,2,128,256]{3,2,1,0:T(8,128)(2,1)} %get-tuple-element.535), channel_id=1, source_target_pairs={{0,8},{1,9},{4,12},{5,13},{8,16},{9,17},{12,20},{13,21},{16,24},{1... | collective-permute-start | bytes 786440 | tf_op jit(solution)/shard_map/cond/branch_0_fun/ppermute | solution.py:311
  55.4 6.2 %collective-permute-start.35 = (bf16[1,2,128,512]{3,2,1,0:T(8,128)(2,1)S(1)}, bf16[1,2,128,512]{3,2,1,0:T(8,128)(2,1)S(1)}, u32[]{:S(2)}, u32[]{:S(2)}) collective-permute-start(bf16[1,2,128,512]{3,2,1,0:T(8,128)(2,1)S(1)} %broadcast_select_fusion.2), channel_id=1, source_target_pairs={{0,4},{8,12},{16,20},{24,28},{1,5},{9,13},{17,21},{25,29},{2,6},{1... | collective-permute-start | bytes 786440 | tf_op jit(solution)/shard_map/cond/branch_0_fun/ppermute | solution.py:393
  61.6 6.5 %collective-permute-start.39 = (bf16[1,2,128,512]{3,2,1,0:T(8,128)(2,1)S(1)}, bf16[1,2,128,512]{3,2,1,0:T(8,128)(2,1)S(1)}, u32[]{:S(2)}, u32[]{:S(2)}) collective-permute-start(bf16[1,2,128,512]{3,2,1,0:T(8,128)(2,1)S(1)} %broadcast_select_fusion.3), channel_id=1, source_target_pairs={{0,1},{1,0},{2,3},{3,2},{4,5},{5,4},{6,7},{7,6},{8,9},{9,8},{10,11... | collective-permute-start | bytes 786440 | tf_op jit(solution)/shard_map/cond/branch_0_fun/ppermute | solution.py:299
  68.9 30.1 %collective-permute-start.65 = (bf16[2,2,128,256]{3,2,1,0:T(8,128)(2,1)S(1)}, bf16[2,2,128,256]{3,2,1,0:T(8,128)(2,1)S(1)}, u32[]{:S(2)}, u32[]{:S(2)}) collective-permute-start(bf16[2,2,128,256]{3,2,1,0:T(8,128)(2,1)S(1)} %get-tuple-element.409.refs_6_), channel_id=1, source_target_pairs={{0,9},{1,8},{4,13},{5,12},{8,17},{9,16},{12,21},{13,20},{16,25},{1... | collective-permute-start | bytes 786440 | tf_op jit(solution)/shard_map/ppermute | solution.py:311
  71.9 27.7 %collective-permute-start.64 = (bf16[2,2,128,256]{3,2,1,0:T(8,128)(2,1)S(1)}, bf16[2,2,128,256]{3,2,1,0:T(8,128)(2,1)S(1)}, u32[]{:S(2)}, u32[]{:S(2)}) collective-permute-start(bf16[2,2,128,256]{3,2,1,0:T(8,128)(2,1)S(1)} %get-tuple-element.409.refs_6_), channel_id=1, source_target_pairs={{0,8},{1,9},{4,12},{5,13},{8,16},{9,17},{12,20},{13,21},{16,24},{1... | collective-permute-start | bytes 786440 | tf_op jit(solution)/shard_map/ppermute | solution.py:311
  74.9 26.1 %collective-permute-start.63 = (bf16[2,2,128,256]{3,2,1,0:T(8,128)(2,1)S(1)}, bf16[2,2,128,256]{3,2,1,0:T(8,128)(2,1)S(1)}, u32[]{:S(2)}, u32[]{:S(2)}) collective-permute-start(bf16[2,2,128,256]{3,2,1,0:T(8,128)(2,1)S(1)} %get-tuple-element.409.refs_6_), channel_id=1, source_target_pairs={{0,5},{1,4},{4,9},{5,8},{8,13},{9,12},{12,17},{13,16},{16,21},{17,... | collective-permute-start | bytes 786440 | tf_op jit(solution)/shard_map/ppermute | solution.py:311
  79.2 23.0 %collective-permute-start.62 = (bf16[2,2,128,256]{3,2,1,0:T(8,128)(2,1)S(1)}, bf16[2,2,128,256]{3,2,1,0:T(8,128)(2,1)S(1)}, u32[]{:S(2)}, u32[]{:S(2)}) collective-permute-start(bf16[2,2,128,256]{3,2,1,0:T(8,128)(2,1)S(1)} %get-tuple-element.409.refs_6_), channel_id=1, source_target_pairs={{0,4},{1,5},{4,8},{5,9},{8,12},{9,13},{12,16},{13,17},{16,20},{17,... | collective-permute-start | bytes 786440 | tf_op jit(solution)/shard_map/ppermute | solution.py:311
  81.5 22.1 %collective-permute-start.61 = (bf16[2,2,128,256]{3,2,1,0:T(8,128)(2,1)S(1)}, bf16[2,2,128,256]{3,2,1,0:T(8,128)(2,1)S(1)}, u32[]{:S(2)}, u32[]{:S(2)}) collective-permute-start(bf16[2,2,128,256]{3,2,1,0:T(8,128)(2,1)S(1)} %get-tuple-element.409.refs_6_), channel_id=1, source_target_pairs={{0,1},{1,0},{4,5},{5,4},{8,9},{9,8},{12,13},{13,12},{16,17},{17,16... | collective-permute-start | bytes 786440 | tf_op jit(solution)/shard_map/ppermute | solution.py:311
  99.0 21.9 %collective-permute-start.66 = (bf16[2,2,128,256]{3,2,1,0:T(8,128)(2,1)}, bf16[2,2,128,256]{3,2,1,0:T(8,128)(2,1)S(1)}, u32[]{:S(2)}, u32[]{:S(2)}) collective-permute-start(bf16[2,2,128,256]{3,2,1,0:T(8,128)(2,1)} %get-tuple-element.429), channel_id=1, source_target_pairs={{0,1},{1,0},{4,5},{5,4},{8,9},{9,8},{12,13},{13,12},{16,17},{17,16... | collective-permute-start | bytes 786440 | tf_op jit(solution)/shard_map/ppermute | solution.py:311
  99.6 21.3 %collective-permute-start.67 = (bf16[2,2,128,256]{3,2,1,0:T(8,128)(2,1)}, bf16[2,2,128,256]{3,2,1,0:T(8,128)(2,1)S(1)}, u32[]{:S(2)}, u32[]{:S(2)}) collective-permute-start(bf16[2,2,128,256]{3,2,1,0:T(8,128)(2,1)} %get-tuple-element.430), channel_id=1, source_target_pairs={{4,0},{5,1},{8,4},{9,5},{12,8},{13,9},{16,12},{17,13},{20,16},{21,... | collective-permute-start | bytes 786440 | tf_op jit(solution)/shard_map/ppermute | solution.py:311
  101.0 20.4 %collective-permute-start.68 = (bf16[2,2,128,256]{3,2,1,0:T(8,128)(2,1)}, bf16[2,2,128,256]{3,2,1,0:T(8,128)(2,1)S(1)}, u32[]{:S(2)}, u32[]{:S(2)}) collective-permute-start(bf16[2,2,128,256]{3,2,1,0:T(8,128)(2,1)} %get-tuple-element.431), channel_id=1, source_target_pairs={{4,1},{5,0},{8,5},{9,4},{12,9},{13,8},{16,13},{17,12},{20,17},{21,... | collective-permute-start | bytes 786440 | tf_op jit(solution)/shard_map/ppermute | solution.py:311
  102.3 25.8 %collective-permute-start.69 = (bf16[2,2,128,256]{3,2,1,0:T(8,128)(2,1)}, bf16[2,2,128,256]{3,2,1,0:T(8,128)(2,1)S(1)}, u32[]{:S(2)}, u32[]{:S(2)}) collective-permute-start(bf16[2,2,128,256]{3,2,1,0:T(8,128)(2,1)} %get-tuple-element.432), channel_id=1, source_target_pairs={{8,0},{9,1},{12,4},{13,5},{16,8},{17,9},{20,12},{21,13},{24,16},{2... | collective-permute-start | bytes 786440 | tf_op jit(solution)/shard_map/ppermute | solution.py:311
  103.6 28.3 %collective-permute-start.70 = (bf16[2,2,128,256]{3,2,1,0:T(8,128)(2,1)}, bf16[2,2,128,256]{3,2,1,0:T(8,128)(2,1)S(1)}, u32[]{:S(2)}, u32[]{:S(2)}) collective-permute-start(bf16[2,2,128,256]{3,2,1,0:T(8,128)(2,1)} %get-tuple-element.433), channel_id=1, source_target_pairs={{8,1},{9,0},{12,5},{13,4},{16,9},{17,8},{20,13},{21,12},{24,17},{2... | collective-permute-start | bytes 786440 | tf_op jit(solution)/shard_map/ppermute | solution.py:311
  132.6 6.9 %collective-permute-start = (bf16[1,2,128,512]{3,2,1,0:T(8,128)(2,1)S(1)}, bf16[1,2,128,512]{3,2,1,0:T(8,128)(2,1)S(1)}, u32[]{:S(2)}, u32[]{:S(2)}) collective-permute-start(bf16[1,2,128,512]{3,2,1,0:T(8,128)(2,1)S(1)} %pad_maximum_fusion), channel_id=1, source_target_pairs={{0,1},{1,0},{2,3},{3,2},{4,5},{5,4},{6,7},{7,6},{8,9},{9,8},{10,11... | collective-permute-start | bytes 786440 | tf_op jit(solution)/shard_map/cond/branch_0_fun/ppermute | solution.py:299
  133.3 65.5 %collective-permute-start.8 = (bf16[2,128,4096]{2,1,0:T(8,128)(2,1)}, bf16[2,128,4096]{2,1,0:T(8,128)(2,1)S(1)}, u32[]{:S(2)}, u32[]{:S(2)}) collective-permute-start(bf16[2,128,4096]{2,1,0:T(8,128)(2,1)} %get-tuple-element.263), channel_id=1, source_target_pairs={{0,2},{2,0},{1,3},{3,1},{4,6},{6,4},{5,7},{7,5},{8,10},{10,8},{9,1... | collective-permute-start | bytes 6291464 | tf_op jit(solution)/shard_map/cond/branch_0_fun/ppermute | solution.py:296
  139.6 12.0 %collective-permute-start.1 = (bf16[1,2,128,512]{3,2,1,0:T(8,128)(2,1)S(1)}, bf16[1,2,128,512]{3,2,1,0:T(8,128)(2,1)S(1)}, u32[]{:S(2)}, u32[]{:S(2)}) collective-permute-start(bf16[1,2,128,512]{3,2,1,0:T(8,128)(2,1)S(1)} %convert_element_type.130), channel_id=1, source_target_pairs={{4,0},{12,8},{20,16},{28,24},{5,1},{13,9},{21,17},{29,25},{6,2},{1... | collective-permute-start | bytes 786440 | tf_op jit(solution)/shard_map/cond/branch_0_fun/ppermute | solution.py:443
  140.9 10.8 %collective-permute-start.2 = (bf16[2,2,128,256]{3,2,1,0:T(8,128)(2,1)S(1)}, bf16[2,2,128,256]{3,2,1,0:T(8,128)(2,1)S(1)}, u32[]{:S(2)}, u32[]{:S(2)}) collective-permute-start(bf16[2,2,128,256]{3,2,1,0:T(8,128)(2,1)S(1)} %get-tuple-element.249), channel_id=1, source_target_pairs={{0,1},{1,0},{4,5},{5,4},{8,9},{9,8},{12,13},{13,12},{16,17},{17,16... | collective-permute-start | bytes 786440 | tf_op jit(solution)/shard_map/cond/branch_0_fun/ppermute | solution.py:311
  141.4 13.2 %collective-permute-start.3 = (bf16[2,2,128,256]{3,2,1,0:T(8,128)(2,1)}, bf16[2,2,128,256]{3,2,1,0:T(8,128)(2,1)}, u32[]{:S(2)}, u32[]{:S(2)}) collective-permute-start(bf16[2,2,128,256]{3,2,1,0:T(8,128)(2,1)} %get-tuple-element.250), channel_id=1, source_target_pairs={{4,0},{5,1},{8,4},{9,5},{12,8},{13,9},{16,12},{17,13},{20,16},{21,... | collective-permute-start | bytes 786440 | tf_op jit(solution)/shard_map/cond/branch_0_fun/ppermute | solution.py:311
  154.6 15.8 %collective-permute-start.4 = (bf16[1,2,128,512]{3,2,1,0:T(8,128)(2,1)S(1)}, bf16[1,2,128,512]{3,2,1,0:T(8,128)(2,1)S(1)}, u32[]{:S(2)}, u32[]{:S(2)}) collective-permute-start(bf16[1,2,128,512]{3,2,1,0:T(8,128)(2,1)S(1)} %convert_element_type.132), channel_id=1, source_target_pairs={{8,0},{24,16},{9,1},{25,17},{10,2},{26,18},{11,3},{27,19}} | collective-permute-start | bytes 786440 | tf_op jit(solution)/shard_map/cond/branch_0_fun/ppermute | solution.py:443
  155.9 14.6 %collective-permute-start.5 = (bf16[2,2,128,256]{3,2,1,0:T(8,128)(2,1)}, bf16[2,2,128,256]{3,2,1,0:T(8,128)(2,1)}, u32[]{:S(2)}, u32[]{:S(2)}) collective-permute-start(bf16[2,2,128,256]{3,2,1,0:T(8,128)(2,1)} %get-tuple-element.255), channel_id=1, source_target_pairs={{4,1},{5,0},{8,5},{9,4},{12,9},{13,8},{16,13},{17,12},{20,17},{21,... | collective-permute-start | bytes 786440 | tf_op jit(solution)/shard_map/cond/branch_0_fun/ppermute | solution.py:311
  157.2 20.4 %collective-permute-start.6 = (bf16[2,2,128,256]{3,2,1,0:T(8,128)(2,1)}, bf16[2,2,128,256]{3,2,1,0:T(8,128)(2,1)}, u32[]{:S(2)}, u32[]{:S(2)}) collective-permute-start(bf16[2,2,128,256]{3,2,1,0:T(8,128)(2,1)} %get-tuple-element.256), channel_id=1, source_target_pairs={{8,0},{9,1},{12,4},{13,5},{16,8},{17,9},{20,12},{21,13},{24,16},{2... | collective-permute-start | bytes 786440 | tf_op jit(solution)/shard_map/cond/branch_0_fun/ppermute | solution.py:311
  177.7 20.8 %collective-permute-start.7 = (bf16[1,2,128,512]{3,2,1,0:T(8,128)(2,1)S(1)}, bf16[1,2,128,512]{3,2,1,0:T(8,128)(2,1)S(1)}, u32[]{:S(2)}, u32[]{:S(2)}) collective-permute-start(bf16[1,2,128,512]{3,2,1,0:T(8,128)(2,1)S(1)} %convert_element_type.134), channel_id=1, source_target_pairs={{16,0},{17,1},{18,2},{19,3}} | collective-permute-start | bytes 786440 | tf_op jit(solution)/shard_map/cond/branch_0_fun/ppermute | solution.py:443
  179.0 21.5 %collective-permute-start.9 = (bf16[2,2,128,256]{3,2,1,0:T(8,128)(2,1)}, bf16[2,2,128,256]{3,2,1,0:T(8,128)(2,1)}, u32[]{:S(2)}, u32[]{:S(2)}) collective-permute-start(bf16[2,2,128,256]{3,2,1,0:T(8,128)(2,1)} %get-tuple-element.264), channel_id=1, source_target_pairs={{8,1},{9,0},{12,5},{13,4},{16,9},{17,8},{20,13},{21,12},{24,17},{2... | collective-permute-start | bytes 786440 | tf_op jit(solution)/shard_map/cond/branch_0_fun/ppermute | solution.py:311
  (27 other events, 196.4 us)
